TPU v7x, 512 devices: a whole 4x4x16 slice. The times are simulated.
512 devices in a mesh: oi: 16 (over z), oj: 32 (over y, x, core).
Axes of the slice: x: 4, y: 4, z: 16, core: 2. Of those that a mesh axis runs over, the one named last changes fastest.
Arguments:
- amplitudes: bfloat16 [12288, 128, 128], P(('oi', 'oj')), may hold values from -6 to 6
- exchange_ints: bfloat16 [12288, 128, 128], P(('oi', 'oj')), may hold values from -6 to 6
- row_intersection: bfloat16 [12288, 128, 128], P(('oi', 'oj')), may hold values from -0.5 to 0.5
- col_intersection: bfloat16 [12288, 128, 128], P(('oi', 'oj')), may hold values from -0.5 to 0.5
- pno_energy: float32 [12288, 128], P(('oi', 'oj')), may hold values from 0.2 to 1
- row_fock: float32 [12288], P(('oi', 'oj')), may hold values from -1 to 1
- col_fock: float32 [12288], P(('oi', 'oj')), may hold values from -1 to 1
- pair_occ: int32 [12288, 2], P(('oi', 'oj')), may hold values from 0 to 19999
- fock_occ: float32 [20000], replicated, may hold values from -0.6 to -0.2
- row_peer: int32 [12288, 1], P(('oi', 'oj')), may hold values from 0 to 31; in each aligned block of 24 rows (0 to 23, 24 to 47, ...) at most 2 rows name the same one
- row_slot: int32 [12288], P(('oi', 'oj')), may hold values from 0 to 23
- col_peer: int32 [12288, 1], P(('oi', 'oj')), may hold values from 0 to 15; in each aligned block of 24 rows (0 to 23, 24 to 47, ...) at most 3 rows name the same one
- col_slot: int32 [12288], P(('oi', 'oj')), may hold values from 0 to 23
Outputs:
- new_amplitudes: bfloat16 [12288, 128, 128], P(('oi', 'oj'))
- residual: bfloat16 [12288, 128, 128], P(('oi', 'oj'))
Inputs may be any that keep to these rules, and one draw needn't show every extreme that they name: `row_peer`: among the pairs of one device no index is named by more than 2 pairs, a bound that some block reaches. `col_peer`: among the pairs of one device no index is named by more than 3 pairs, a bound that some block reaches.
All inputs are finite; a program needn't handle non-finite values.
Results may differ from a plain program's by a relative error of at most 0.012.
The roundings to bfloat16 on the way count: a program that leaves them out, or rounds other values in their place, can miss the bound.
Values may be sent and summed in bfloat16 or wider, within the bound.
No kernel may reach another device: no remote copies, remote signals or barrier semaphores. Data moves between devices by JAX's collectives and lax.ppermute only.
A program may use at most 64 MiB of HBM per device.

v0:
```python
import jax
import jax.numpy as jnp
from jax import lax
from jax.sharding import PartitionSpec as P

ITERS = 3


def couple(blocks, intersection):
    first = jnp.einsum(
        "pab,pbc->pac", intersection, blocks, preferred_element_type=jnp.float32
    ).astype(jnp.bfloat16)
    return jnp.einsum("pac,pdc->pad", first, intersection, preferred_element_type=jnp.float32)


def layout(peer, slot, peer_count, capacity):
    marker = (peer[:, None] == jnp.arange(peer_count, dtype=jnp.int32)[None, :]).astype(jnp.int32)
    before = jnp.sum((jnp.cumsum(marker, axis=0) - marker) * marker, axis=1)
    target = peer * capacity + before
    slot_table = jnp.zeros((peer_count * capacity,), jnp.int32).at[target].set(slot)
    return (target, slot_table.reshape(peer_count, capacity))


def body(
    amplitudes,
    exchange_ints,
    row_intersection,
    col_intersection,
    pno_energy,
    row_fock,
    col_fock,
    pair_occ,
    fock_occ,
    row_peer,
    row_slot,
    col_peer,
    col_slot,
):
    pairs_here = amplitudes.shape[0]
    width = amplitudes.shape[1]
    row_count = lax.axis_size("oj")
    col_count = lax.axis_size("oi")
    row_capacity = max(2, (pairs_here + row_count - 1) // row_count + 1)
    col_capacity = max(2, (pairs_here + col_count - 1) // col_count + 1)
    row_target, row_table = layout(row_peer[:, 0], row_slot, row_count, row_capacity)
    col_target, col_table = layout(col_peer[:, 0], col_slot, col_count, col_capacity)
    matches = (
        pair_occ.reshape(-1)[:, None] == jnp.arange(fock_occ.shape[0], dtype=jnp.int32)[None, :]
    )
    picked = jnp.sum(jnp.where(matches, fock_occ[None, :], 0.0), axis=1).reshape(-1, 2)
    occupied = picked[:, 0] + picked[:, 1]
    denominator = pno_energy[:, :, None] + pno_energy[:, None, :] - occupied[:, None, None]
    ints_wide = exchange_ints.astype(jnp.float32)
    row_wanted = lax.all_to_all(row_table, "oj", split_axis=0, concat_axis=0, tiled=True)
    col_wanted = lax.all_to_all(col_table, "oi", split_axis=0, concat_axis=0, tiled=True)
    current = amplitudes
    residual = jnp.zeros(amplitudes.shape, jnp.float32)
    for sweep in range(ITERS):
        row_fetched = lax.all_to_all(
            current[row_wanted], "oj", split_axis=0, concat_axis=0, tiled=True
        )
        col_fetched = lax.all_to_all(
            current[col_wanted], "oi", split_axis=0, concat_axis=0, tiled=True
        )
        row_term = couple(row_fetched.reshape(-1, width, width)[row_target], row_intersection)
        col_term = couple(col_fetched.reshape(-1, width, width)[col_target], col_intersection)
        own_wide = current.astype(jnp.float32)
        residual = (
            ints_wide
            + denominator * own_wide
            - row_fock[:, None, None] * row_term
            - col_fock[:, None, None] * col_term
        )
        current = (own_wide - residual / denominator).astype(jnp.bfloat16)
    return (current, residual.astype(jnp.bfloat16))


def solution(mesh):
    return jax.shard_map(
        body,
        mesh=mesh,
        in_specs=(
            P(("oi", "oj"), None, None),
            P(("oi", "oj"), None, None),
            P(("oi", "oj"), None, None),
            P(("oi", "oj"), None, None),
            P(("oi", "oj"), None),
            P(("oi", "oj")),
            P(("oi", "oj")),
            P(("oi", "oj"), None),
            P(),
            P(("oi", "oj"), None),
            P(("oi", "oj")),
            P(("oi", "oj"), None),
            P(("oi", "oj")),
        ),
        out_specs=(P(("oi", "oj"), None, None), P(("oi", "oj"), None, None)),
        check_vma=False,
    )
```

profile of v0, /device:TPU:1, one launch (start us, length us, event | category | flops | bytes accessed | tf_op | source)
XLA Modules:
  0.0 406.3 jit_solution(11335015989227703800)
XLA Ops:
  4.5 10.4 %all-to-all-start = ((s32[32,1,2]{2,1,0:T(1,128)}), s32[32,1,2]{2,1,0:T(1,128)S(1)}, u32[]{:S(2)}, u32[]{:S(2)}) async-start(s32[32,1,2]{2,1,0:T(1,128)} %bitcast.3), calls=%async_computation | async-start | bytes 32768 | tf_op jit(solution)/shard_map/all_to_all | solution.py:54
  18.6 3.2 all-to-all-done
  21.8 13.0 %all-to-all-start.2 = ((s32[16,1,3]{2,1,0:T(1,128)}), s32[16,1,3]{2,1,0:T(1,128)S(1)}, u32[]{:S(2)}, u32[]{:S(2)}) async-start(s32[16,1,3]{2,1,0:T(1,128)} %bitcast.10), calls=%async_computation.2 | async-start | bytes 16384 | tf_op jit(solution)/shard_map/all_to_all | solution.py:55
  35.2 3.3 gather_fusion
  38.4 7.7 %all-to-all-done.2 = s32[16,1,3]{2,1,0:T(1,128)S(1)} async-done(((s32[16,1,3]{2,1,0:T(1,128)}), s32[16,1,3]{2,1,0:T(1,128)S(1)}, u32[]{:S(2)}, u32[]{:S(2)}) %all-to-all-start.2) | async-done | bytes 224 | tf_op jit(solution)/shard_map/all_to_all | solution.py:55
  46.1 6.5 %all-to-all-start.1 = ((bf16[32,2,128,128]{3,2,1,0:T(8,128)(2,1)}), bf16[32,2,128,128]{3,2,1,0:T(8,128)(2,1)}, u32[]{:S(2)}, u32[]{:S(2)}) async-start(bf16[32,2,128,128]{3,2,1,0:T(8,128)(2,1)} %bitcast.54), calls=%async_computation.1 | async-start | bytes 4194304 | tf_op jit(solution)/shard_map/all_to_all | solution.py:59
  54.9 25.7 %all-to-all-done.1 = bf16[32,2,128,128]{3,2,1,0:T(8,128)(2,1)} async-done(((bf16[32,2,128,128]{3,2,1,0:T(8,128)(2,1)}), bf16[32,2,128,128]{3,2,1,0:T(8,128)(2,1)}, u32[]{:S(2)}, u32[]{:S(2)}) %all-to-all-start.1) | async-done | bytes 2097184 | tf_op jit(solution)/shard_map/all_to_all | solution.py:59
  80.6 4.5 %all-to-all-start.3 = ((bf16[16,3,128,128]{3,2,1,0:T(8,128)(2,1)}), bf16[16,3,128,128]{3,2,1,0:T(8,128)(2,1)}, u32[]{:S(2)}, u32[]{:S(2)}) async-start(bf16[16,3,128,128]{3,2,1,0:T(8,128)(2,1)} %bitcast.57), calls=%async_computation.3 | async-start | bytes 3145728 | tf_op jit(solution)/shard_map/all_to_all | solution.py:62
  88.8 2.4 fusion.11
  91.2 63.0 %all-to-all-done.3 = bf16[16,3,128,128]{3,2,1,0:T(8,128)(2,1)} async-done(((bf16[16,3,128,128]{3,2,1,0:T(8,128)(2,1)}), bf16[16,3,128,128]{3,2,1,0:T(8,128)(2,1)}, u32[]{:S(2)}, u32[]{:S(2)}) %all-to-all-start.3) | async-done | bytes 1572896 | tf_op jit(solution)/shard_map/all_to_all | solution.py:62
  154.2 3.0 gather_fusion.3
  157.2 3.5 fusion
  162.8 9.9 %all-to-all-start.4 = ((bf16[32,2,128,128]{3,2,1,0:T(8,128)(2,1)}), bf16[32,2,128,128]{3,2,1,0:T(8,128)(2,1)}, u32[]{:S(2)}, u32[]{:S(2)}) async-start(bf16[32,2,128,128]{3,2,1,0:T(8,128)(2,1)} %bitcast.56), calls=%async_computation.4 | async-start | bytes 4194304 | tf_op jit(solution)/shard_map/all_to_all | solution.py:59
  174.7 26.0 %all-to-all-done.4 = bf16[32,2,128,128]{3,2,1,0:T(8,128)(2,1)} async-done(((bf16[32,2,128,128]{3,2,1,0:T(8,128)(2,1)}), bf16[32,2,128,128]{3,2,1,0:T(8,128)(2,1)}, u32[]{:S(2)}, u32[]{:S(2)}) %all-to-all-start.4) | async-done | bytes 2097184 | tf_op jit(solution)/shard_map/all_to_all | solution.py:59
  200.7 7.2 %all-to-all-start.5 = ((bf16[16,3,128,128]{3,2,1,0:T(8,128)(2,1)}), bf16[16,3,128,128]{3,2,1,0:T(8,128)(2,1)}, u32[]{:S(2)}, u32[]{:S(2)}) async-start(bf16[16,3,128,128]{3,2,1,0:T(8,128)(2,1)} %bitcast.59), calls=%async_computation.5 | async-start | bytes 3145728 | tf_op jit(solution)/shard_map/all_to_all | solution.py:62
  212.6 64.5 %all-to-all-done.5 = bf16[16,3,128,128]{3,2,1,0:T(8,128)(2,1)} async-done(((bf16[16,3,128,128]{3,2,1,0:T(8,128)(2,1)}), bf16[16,3,128,128]{3,2,1,0:T(8,128)(2,1)}, u32[]{:S(2)}, u32[]{:S(2)}) %all-to-all-start.5) | async-done | bytes 1572896 | tf_op jit(solution)/shard_map/all_to_all | solution.py:62
  277.1 3.0 gather_fusion.7
  280.1 3.5 fusion.1
  285.7 10.4 %all-to-all-start.6 = ((bf16[32,2,128,128]{3,2,1,0:T(8,128)(2,1)}), bf16[32,2,128,128]{3,2,1,0:T(8,128)(2,1)}, u32[]{:S(2)}, u32[]{:S(2)}) async-start(bf16[32,2,128,128]{3,2,1,0:T(8,128)(2,1)} %bitcast.55), calls=%async_computation.6 | async-start | bytes 4194304 | tf_op jit(solution)/shard_map/all_to_all | solution.py:59
  298.1 25.9 %all-to-all-done.6 = bf16[32,2,128,128]{3,2,1,0:T(8,128)(2,1)} async-done(((bf16[32,2,128,128]{3,2,1,0:T(8,128)(2,1)}), bf16[32,2,128,128]{3,2,1,0:T(8,128)(2,1)}, u32[]{:S(2)}, u32[]{:S(2)}) %all-to-all-start.6) | async-done | bytes 2097184 | tf_op jit(solution)/shard_map/all_to_all | solution.py:59
  324.0 6.7 %all-to-all-start.7 = ((bf16[16,3,128,128]{3,2,1,0:T(8,128)(2,1)}), bf16[16,3,128,128]{3,2,1,0:T(8,128)(2,1)}, u32[]{:S(2)}, u32[]{:S(2)}) async-start(bf16[16,3,128,128]{3,2,1,0:T(8,128)(2,1)} %bitcast.58), calls=%async_computation.7 | async-start | bytes 3145728 | tf_op jit(solution)/shard_map/all_to_all | solution.py:62
  333.0 2.4 fusion.13
  335.4 64.5 %all-to-all-done.7 = bf16[16,3,128,128]{3,2,1,0:T(8,128)(2,1)} async-done(((bf16[16,3,128,128]{3,2,1,0:T(8,128)(2,1)}), bf16[16,3,128,128]{3,2,1,0:T(8,128)(2,1)}, u32[]{:S(2)}, u32[]{:S(2)}) %all-to-all-start.7) | async-done | bytes 1572896 | tf_op jit(solution)/shard_map/all_to_all | solution.py:62
  402.1 4.2 %fusion.23 = (bf16[24,128,128]{2,1,0:T(8,128)(2,1)}, bf16[24,128,128]{2,1,0:T(8,128)(2,1)}) fusion(f32[24]{0:T(128)S(1)} %fusion.14, f32[24,128]{1,0:T(8,128)S(1)} %copy-done.6, bf16[24,128,128]{2,1,0:T(8,128)(2,1)S(1)} %fusion.1, bf16[24,128,128]{2,1,0:T(8,128)(2,1)S(1)} %copy-done, bf16[24,128,128]{2,1,0:T(8,128)(2,1)S(1)} %gather_fusion.11, ...), kind=kOutput, calls=%fused_computation.70 | convolution fusion | flops 207224832 | bytes 6304032 | tf_op jit(solution)/shard_map/pac,pdc->pad/dot_general | solution.py:13
  (57 shorter events, 31.0 us)
Async XLA Ops:
  0.6 156.5 %copy-start = (bf16[24,128,128]{2,1,0:T(8,128)(2,1)S(1)}, bf16[24,128,128]{2,1,0:T(8,128)(2,1)}, u32[]{:S(2)}) copy-start(bf16[24,128,128]{2,1,0:T(8,128)(2,1)} %param.16) | copy-start | bytes 2359300
  4.5 17.3 %all-to-all-start = ((s32[32,1,2]{2,1,0:T(1,128)}), s32[32,1,2]{2,1,0:T(1,128)S(1)}, u32[]{:S(2)}, u32[]{:S(2)}) async-start(s32[32,1,2]{2,1,0:T(1,128)} %bitcast.3), calls=%async_computation | async-start | bytes 32768 | tf_op jit(solution)/shard_map/all_to_all | solution.py:54
  21.8 24.3 %all-to-all-start.2 = ((s32[16,1,3]{2,1,0:T(1,128)}), s32[16,1,3]{2,1,0:T(1,128)S(1)}, u32[]{:S(2)}, u32[]{:S(2)}) async-start(s32[16,1,3]{2,1,0:T(1,128)} %bitcast.10), calls=%async_computation.2 | async-start | bytes 16384 | tf_op jit(solution)/shard_map/all_to_all | solution.py:55
  46.1 6.8 %copy-start.2 = (bf16[24,128,128]{2,1,0:T(8,128)(2,1)S(1)}, bf16[24,128,128]{2,1,0:T(8,128)(2,1)}, u32[]{:S(2)}) copy-start(bf16[24,128,128]{2,1,0:T(8,128)(2,1)} %param.13) | copy-start | bytes 2359300
  46.1 34.5 %all-to-all-start.1 = ((bf16[32,2,128,128]{3,2,1,0:T(8,128)(2,1)}), bf16[32,2,128,128]{3,2,1,0:T(8,128)(2,1)}, u32[]{:S(2)}, u32[]{:S(2)}) async-start(bf16[32,2,128,128]{3,2,1,0:T(8,128)(2,1)} %bitcast.54), calls=%async_computation.1 | async-start | bytes 4194304 | tf_op jit(solution)/shard_map/all_to_all | solution.py:59
  80.6 4.5 %copy-start.4 = (s32[24,2]{0,1:T(2,128)S(1)}, s32[24,2]{0,1:T(2,128)}, u32[]{:S(2)}) copy-start(s32[24,2]{0,1:T(2,128)} %param.20) | copy-start | bytes 580
  80.6 4.8 %copy-start.3 = (f32[20000]{0:T(1024)S(1)}, f32[20000]{0:T(1024)}, u32[]{:S(2)}) copy-start(f32[20000]{0:T(1024)} %param.21) | copy-start | bytes 240004
  80.6 73.6 %all-to-all-start.3 = ((bf16[16,3,128,128]{3,2,1,0:T(8,128)(2,1)}), bf16[16,3,128,128]{3,2,1,0:T(8,128)(2,1)}, u32[]{:S(2)}, u32[]{:S(2)}) async-start(bf16[16,3,128,128]{3,2,1,0:T(8,128)(2,1)} %bitcast.57), calls=%async_computation.3 | async-start | bytes 3145728 | tf_op jit(solution)/shard_map/all_to_all | solution.py:62
  85.2 3.6 copy-start.1
  91.2 66.0 %copy-start.6 = (f32[24,128]{1,0:T(8,128)S(1)}, f32[24,128]{1,0:T(8,128)}, u32[]{:S(2)}) copy-start(f32[24,128]{1,0:T(8,128)} %param.17) | copy-start | bytes 36868
  91.2 66.0 %copy-start.7 = (f32[24]{0:T(128)S(1)}, f32[24]{0:T(128)}, u32[]{:S(2)}) copy-start(f32[24]{0:T(128)} %param.19) | copy-start | bytes 292
  91.2 66.0 %copy-start.8 = (f32[24]{0:T(128)S(1)}, f32[24]{0:T(128)}, u32[]{:S(2)}) copy-start(f32[24]{0:T(128)} %param.18) | copy-start | bytes 292
  162.8 37.9 %all-to-all-start.4 = ((bf16[32,2,128,128]{3,2,1,0:T(8,128)(2,1)}), bf16[32,2,128,128]{3,2,1,0:T(8,128)(2,1)}, u32[]{:S(2)}, u32[]{:S(2)}) async-start(bf16[32,2,128,128]{3,2,1,0:T(8,128)(2,1)} %bitcast.56), calls=%async_computation.4 | async-start | bytes 4194304 | tf_op jit(solution)/shard_map/all_to_all | solution.py:59
  200.7 76.4 %all-to-all-start.5 = ((bf16[16,3,128,128]{3,2,1,0:T(8,128)(2,1)}), bf16[16,3,128,128]{3,2,1,0:T(8,128)(2,1)}, u32[]{:S(2)}, u32[]{:S(2)}) async-start(bf16[16,3,128,128]{3,2,1,0:T(8,128)(2,1)} %bitcast.59), calls=%async_computation.5 | async-start | bytes 3145728 | tf_op jit(solution)/shard_map/all_to_all | solution.py:62
  285.7 38.3 %all-to-all-start.6 = ((bf16[32,2,128,128]{3,2,1,0:T(8,128)(2,1)}), bf16[32,2,128,128]{3,2,1,0:T(8,128)(2,1)}, u32[]{:S(2)}, u32[]{:S(2)}) async-start(bf16[32,2,128,128]{3,2,1,0:T(8,128)(2,1)} %bitcast.55), calls=%async_computation.6 | async-start | bytes 4194304 | tf_op jit(solution)/shard_map/all_to_all | solution.py:59
  324.0 75.9 %all-to-all-start.7 = ((bf16[16,3,128,128]{3,2,1,0:T(8,128)(2,1)}), bf16[16,3,128,128]{3,2,1,0:T(8,128)(2,1)}, u32[]{:S(2)}, u32[]{:S(2)}) async-start(bf16[16,3,128,128]{3,2,1,0:T(8,128)(2,1)} %bitcast.58), calls=%async_computation.7 | async-start | bytes 3145728 | tf_op jit(solution)/shard_map/all_to_all | solution.py:62
  335.4 66.6 %copy-start.5 = (bf16[24,128,128]{2,1,0:T(8,128)(2,1)S(1)}, bf16[24,128,128]{2,1,0:T(8,128)(2,1)}, u32[]{:S(2)}) copy-start(bf16[24,128,128]{2,1,0:T(8,128)(2,1)} %param.14) | copy-start | bytes 2359300
where the time goes:
time: 412 us; the launch traced here: 406 us
  waiting for transfers between devices  281 us (68%)
  starting transfers between devices  68.7 us (17%)
  local copies, waits for them, and re-layouts  32.1 us (8%)
  matrix products  18.3 us (4%)
  other arithmetic  5.63 us (1%)
    all_to_all x3, waiting for transfers between devices, body(): lax.all_to_all(current[col_wanted], 'oi', split_axis=0, concat_axis=0, ti...  192 us
    all_to_all x3, waiting for transfers between devices, body(): lax.all_to_all(current[row_wanted], 'oj', split_axis=0, concat_axis=0, ti...  77.6 us
    all_to_all x3, starting transfers between devices, body(): lax.all_to_all(current[row_wanted], 'oj', split_axis=0, concat_axis=0, ti...  26.8 us
    all_to_all x3, starting transfers between devices, body(): lax.all_to_all(current[col_wanted], 'oi', split_axis=0, concat_axis=0, ti...  18.5 us
    dot_general x6, matrix products, couple(): jnp.einsum('pac,pdc->pad', first, intersection, preferred_element_type=jn...  18.3 us
    all_to_all x1, starting transfers between devices, body(): lax.all_to_all(col_table, 'oi', split_axis=0, concat_axis=0, tiled=True)  13 us
    all_to_all x1, starting transfers between devices, body(): lax.all_to_all(row_table, 'oj', split_axis=0, concat_axis=0, tiled=True)  10.4 us
  transfers between devices with their start and end apart: 8, of which 8 were waited for; matrix products, arithmetic and copies ran while one was open for 7% of the time, Pallas kernels for 0%

commit v1 on v0

--- a/solution.py
+++ b/solution.py
@@ -4,6 +4,17 @@
 from jax.sharding import PartitionSpec as P
 
 ITERS = 3
+LANES = 4
+STEPS = (
+    ((2, 1), (2, 3)),
+    ((1, 2), (3, 2)),
+    ((0, 0), (2, 2)),
+    ((0, 2), (2, 0)),
+    ((1, 1), (3, 3)),
+    ((1, 3), (3, 1)),
+    ((1, 0), (3, 0)),
+    ((0, 1), (0, 3)),
+)
 
 
 def couple(blocks, intersection):
@@ -21,6 +32,71 @@
     return (target, slot_table.reshape(peer_count, capacity))
 
 
+def ranks(peer):
+    order = jnp.arange(peer.shape[0], dtype=jnp.int32)
+    earlier = (peer[:, None] == peer[None, :]) & (order[None, :] < order[:, None])
+    return jnp.sum(earlier.astype(jnp.int32), axis=1)
+
+
+def row_requests(row_peer, row_slot, me, capacity):
+    codes = lax.all_gather(row_peer * 32 + row_slot, "oj")
+    mine = codes // 32 == me
+    order = jnp.arange(codes.shape[1], dtype=jnp.int32)
+    lower = (order[:, None] < order[None, :]).astype(jnp.float32)
+    rank = jnp.dot(mine.astype(jnp.float32), lower).astype(jnp.int32)
+    wants = mine[:, :, None] & (rank[:, :, None] == jnp.arange(capacity, dtype=jnp.int32))
+    return jnp.sum(jnp.where(wants, (codes % 32)[:, :, None], 0), axis=1)
+
+
+def core_exchange(blocks):
+    return lax.ppermute(blocks, "oj", [(source, source ^ 1) for source in range(32)])
+
+
+def chip_exchange(blocks, offsets):
+    pairs = []
+    for source in range(32):
+        y, x, c = source // 8, source // 2 % 4, source % 2
+        step_y, step_x = offsets[c]
+        pairs.append((source, (y + step_y) % 4 * 8 + (x + step_x) % 4 * 2 + c))
+    return lax.ppermute(blocks, "oj", pairs)
+
+
+def row_plan(row_wanted, row_peer, rank, me):
+    my_y, my_x, my_c = me // 8, me // 2 % 4, me % 2
+    step_y = jnp.array([[offsets[0] for offsets in step] for step in STEPS], jnp.int32)
+    step_x = jnp.array([[offsets[1] for offsets in step] for step in STEPS], jnp.int32)
+    dest = (my_y + step_y) % 4 * 8 + (my_x + step_x) % 4 * 2
+    core = jnp.arange(2, dtype=jnp.int32)
+    dest = dest[:, :, None] + (core[None, :, None] ^ core[None, None, :])
+    slots = row_wanted[dest]
+    near = jnp.where(my_c == 0, slots[:, 0], slots[:, 1]).reshape(-1)
+    far = jnp.where(my_c == 0, slots[:, 1], slots[:, 0]).reshape(-1)
+    off = (my_y - row_peer // 8) % 4 * 4 + (my_x - row_peer // 2) % 4
+    match = off[:, None, None] == (step_y * 4 + step_x)[None, :, :]
+    number = jnp.arange(len(STEPS), dtype=jnp.int32)
+    step = jnp.sum(jnp.where(match, number[None, :, None], 0), axis=(1, 2))
+    carrier = jnp.sum(jnp.where(match, core[None, None, :], 0), axis=(1, 2))
+    target = (carrier ^ my_c) * 32 + step * 4 + (carrier ^ (row_peer % 2)) * 2 + rank
+    return near, far, target
+
+
+def row_exchange(near, far, width):
+    count = len(STEPS)
+    near = near.reshape(count, 4, width, width)
+    far = core_exchange(far).reshape(count, 4, width, width)
+    joined = jnp.concatenate([near, far], axis=1)
+    arrived = []
+    for number, offsets in enumerate(STEPS):
+        outgoing = joined[number]
+        if number >= LANES:
+            outgoing, _ = lax.optimization_barrier((outgoing, arrived[-LANES]))
+        arrived.append(chip_exchange(outgoing, offsets))
+    arrived = [piece.reshape(2, 2, 2, width, width) for piece in arrived]
+    keep = jnp.concatenate([piece[:, 0].reshape(4, width, width) for piece in arrived], axis=0)
+    swap = jnp.concatenate([piece[:, 1].reshape(4, width, width) for piece in arrived], axis=0)
+    return jnp.concatenate([keep, core_exchange(swap)], axis=0)
+
+
 def body(
     amplitudes,
     exchange_ints,
@@ -36,14 +112,15 @@
     col_peer,
     col_slot,
 ):
-    pairs_here = amplitudes.shape[0]
     width = amplitudes.shape[1]
-    row_count = lax.axis_size("oj")
-    col_count = lax.axis_size("oi")
-    row_capacity = max(2, (pairs_here + row_count - 1) // row_count + 1)
-    col_capacity = max(2, (pairs_here + col_count - 1) // col_count + 1)
-    row_target, row_table = layout(row_peer[:, 0], row_slot, row_count, row_capacity)
-    col_target, col_table = layout(col_peer[:, 0], col_slot, col_count, col_capacity)
+    row_capacity, col_capacity = 2, 3
+    me = lax.axis_index("oj")
+    col_target, col_table = layout(col_peer[:, 0], col_slot, lax.axis_size("oi"), col_capacity)
+    col_wanted = lax.all_to_all(col_table, "oi", split_axis=0, concat_axis=0, tiled=True)
+    row_wanted = row_requests(row_peer[:, 0], row_slot, me, row_capacity)
+    near_wanted, far_wanted, row_target = row_plan(
+        row_wanted, row_peer[:, 0], ranks(row_peer[:, 0]), me
+    )
     matches = (
         pair_occ.reshape(-1)[:, None] == jnp.arange(fock_occ.shape[0], dtype=jnp.int32)[None, :]
     )
@@ -51,18 +128,14 @@
     occupied = picked[:, 0] + picked[:, 1]
     denominator = pno_energy[:, :, None] + pno_energy[:, None, :] - occupied[:, None, None]
     ints_wide = exchange_ints.astype(jnp.float32)
-    row_wanted = lax.all_to_all(row_table, "oj", split_axis=0, concat_axis=0, tiled=True)
-    col_wanted = lax.all_to_all(col_table, "oi", split_axis=0, concat_axis=0, tiled=True)
     current = amplitudes
     residual = jnp.zeros(amplitudes.shape, jnp.float32)
     for sweep in range(ITERS):
-        row_fetched = lax.all_to_all(
-            current[row_wanted], "oj", split_axis=0, concat_axis=0, tiled=True
-        )
         col_fetched = lax.all_to_all(
             current[col_wanted], "oi", split_axis=0, concat_axis=0, tiled=True
         )
-        row_term = couple(row_fetched.reshape(-1, width, width)[row_target], row_intersection)
+        row_fetched = row_exchange(current[near_wanted], current[far_wanted], width)
+        row_term = couple(row_fetched[row_target], row_intersection)
         col_term = couple(col_fetched.reshape(-1, width, width)[col_target], col_intersection)
         own_wide = current.astype(jnp.float32)
         residual = (

time: 412 us -> 322 us (0.78)
  waiting for transfers between devices: 281 us -> 26.6 us
  starting transfers between devices: 68.7 us -> 178 us
  local copies, waits for them, and re-layouts: 32.1 us -> 64.1 us
  blocking collectives: 0 us -> 14.5 us
  other arithmetic: 5.63 us -> 12.3 us
    all_to_all x3, waiting for transfers between devices: 192 us -> 14.1 us  [body(): lax.all_to_all(current[col_wanted], 'oi', split_axis=0, concat_axis=0, ti...]
    ppermute x0 -> x30, starting transfers between devices: none -> 128 us  [the longest x24 85.1 us: chip_exchange(): return lax.ppermute(blocks, 'oj', pairs)]
    all_to_all x4 -> x0, waiting for transfers between devices: 80.8 us -> none  [the longest x3 77.6 us: body(): lax.all_to_all(current[row_wanted], 'oj', split_axis=0, concat_axis=0, ti...]
    all_to_all x4 -> x0, starting transfers between devices: 37.2 us -> none  [the longest x3 26.8 us: body(): lax.all_to_all(current[row_wanted], 'oj', split_axis=0, concat_axis=0, ti...]
    unnamed x19 -> x76, local copies, waits for them, and re-layouts: 0.13 us -> 23.8 us
    all_to_all x3, starting transfers between devices: 18.5 us -> 34.4 us  [body(): lax.all_to_all(current[col_wanted], 'oi', split_axis=0, concat_axis=0, ti...]
    unnamed x0 -> x1, blocking collectives: none -> 14.5 us
    ppermute x0 -> x30, waiting for transfers between devices: none -> 12.5 us  [the longest x24 9.93 us: chip_exchange(): return lax.ppermute(blocks, 'oj', pairs)]
  transfers between devices with their start and end apart: 8 -> 34, of which waited for: 8 -> 12; matrix products, arithmetic and copies ran while one was open for 7% -> 20% of each run, Pallas kernels for 0% -> 0%
where the time goes in v1:
time: 322 us; the launch traced here: 317 us
  starting transfers between devices  178 us (55%)
  local copies, waits for them, and re-layouts  64.1 us (20%)
  waiting for transfers between devices  26.6 us (8%)
  matrix products  18.7 us (6%)
  blocking collectives  14.5 us (5%)
  other arithmetic  12.3 us (4%)
    ppermute x24, starting transfers between devices, chip_exchange(): return lax.ppermute(blocks, 'oj', pairs)  85.1 us
    ppermute x6, starting transfers between devices, core_exchange(): lax.ppermute(blocks, 'oj', [(source, source ^ 1) for source in range(32)])  42.7 us
    all_to_all x3, starting transfers between devices, body(): lax.all_to_all(current[col_wanted], 'oi', split_axis=0, concat_axis=0, ti...  34.4 us
    unnamed x76, local copies, waits for them, and re-layouts  23.8 us
    dot_general x6, matrix products, couple(): jnp.einsum('pac,pdc->pad', first, intersection, preferred_element_type=jn...  18.5 us
    all_to_all x1, starting transfers between devices, body(): lax.all_to_all(col_table, 'oi', split_axis=0, concat_axis=0, tiled=True)  15.7 us
    unnamed x1, blocking collectives  14.5 us
    all_to_all x3, waiting for transfers between devices, body(): lax.all_to_all(current[col_wanted], 'oi', split_axis=0, concat_axis=0, ti...  14.1 us
  transfers between devices with their start and end apart: 34, of which 12 were waited for; matrix products, arithmetic and copies ran while one was open for 20% of the time, Pallas kernels for 0%

profile of v1, /device:TPU:1, one launch (start us, length us, event | category | flops | bytes accessed | tf_op | source)
XLA Modules:
  0.0 316.6 jit_solution(15410405042728755733)
XLA Ops:
  4.5 15.7 %all-to-all-start = ((s32[16,1,3]{2,1,0:T(1,128)}), s32[16,1,3]{2,1,0:T(1,128)S(1)}, u32[]{:S(2)}, u32[]{:S(2)}) async-start(s32[16,1,3]{2,1,0:T(1,128)} %bitcast.46), calls=%async_computation | async-start | bytes 16384 | tf_op jit(solution)/shard_map/all_to_all | solution.py:119
  23.0 14.5 %all-reduce = s32[768]{0:T(1024)S(1)} all-reduce(s32[768]{0:T(1024)S(1)} %get-tuple-element.107), channel_id=2, replica_groups=mesh['oi'=16,'oj'=32] {'oj'}, use_global_device_ids=true, to_apply=%add | all-reduce | flops 768 | bytes 6144
  43.3 5.3 %collective-permute-start = (bf16[32,128,128]{2,1,0:T(8,128)(2,1)}, bf16[32,128,128]{2,1,0:T(8,128)(2,1)}, u32[]{:S(2)}, u32[]{:S(2)}) collective-permute-start(bf16[32,128,128]{2,1,0:T(8,128)(2,1)} %gather_fusion.2), channel_id=1, source_target_pairs={{0,1},{1,0},{2,3},{3,2},{4,5},{5,4},{6,7},{7,6},{8,9},{9,8},{10,11... | collective-permute-start | bytes 3145736 | tf_op jit(solution)/shard_map/ppermute | solution.py:52
  50.5 11.9 %all-to-all-start.1 = ((bf16[16,3,128,128]{3,2,1,0:T(8,128)(2,1)}), bf16[16,3,128,128]{3,2,1,0:T(8,128)(2,1)}, u32[]{:S(2)}, u32[]{:S(2)}) async-start(bf16[16,3,128,128]{3,2,1,0:T(8,128)(2,1)} %bitcast.48), calls=%async_computation.1 | async-start | bytes 3145728 | tf_op jit(solution)/shard_map/all_to_all | solution.py:134
  69.8 4.8 %collective-permute-start.2 = (bf16[8,128,128]{2,1,0:T(8,128)(2,1)S(1)}, bf16[8,128,128]{2,1,0:T(8,128)(2,1)S(1)}, u32[]{:S(2)}, u32[]{:S(2)}) collective-permute-start(bf16[8,128,128]{2,1,0:T(8,128)(2,1)S(1)} %get-tuple-element.46), channel_id=1, source_target_pairs={{0,12},{1,29},{2,14},{3,31},{4,8},{5,25},{6,10},{7,27},{8,20},{9,5... | collective-permute-start | bytes 786440 | tf_op jit(solution)/shard_map/ppermute | solution.py:61
  74.6 3.4 %collective-permute-start.3 = (bf16[8,128,128]{2,1,0:T(8,128)(2,1)S(1)}, bf16[8,128,128]{2,1,0:T(8,128)(2,1)S(1)}, u32[]{:S(2)}, u32[]{:S(2)}) collective-permute-start(bf16[8,128,128]{2,1,0:T(8,128)(2,1)S(1)} %get-tuple-element.47), channel_id=1, source_target_pairs={{0,0},{1,21},{2,2},{3,23},{4,4},{5,17},{6,6},{7,19},{8,8},{9,29},{... | collective-permute-start | bytes 786440 | tf_op jit(solution)/shard_map/ppermute | solution.py:61
  78.0 4.8 %collective-permute-start.4 = (bf16[8,128,128]{2,1,0:T(8,128)(2,1)S(1)}, bf16[8,128,128]{2,1,0:T(8,128)(2,1)S(1)}, u32[]{:S(2)}, u32[]{:S(2)}) collective-permute-start(bf16[8,128,128]{2,1,0:T(8,128)(2,1)S(1)} %get-tuple-element.48), channel_id=1, source_target_pairs={{0,4},{1,17},{2,6},{3,19},{4,0},{5,21},{6,2},{7,23},{8,12},{9,25},... | collective-permute-start | bytes 786440 | tf_op jit(solution)/shard_map/ppermute | solution.py:61
  92.1 4.6 %collective-permute-start.8 = (bf16[8,128,128]{2,1,0:T(8,128)(2,1)S(1)}, bf16[8,128,128]{2,1,0:T(8,128)(2,1)S(1)}, u32[]{:S(2)}, u32[]{:S(2)}) collective-permute-start(bf16[8,128,128]{2,1,0:T(8,128)(2,1)S(1)} %get-tuple-element.17), channel_id=1, source_target_pairs={{0,2},{1,7},{2,4},{3,1},{4,6},{5,3},{6,0},{7,5},{8,10},{9,15},{10,... | collective-permute-start | bytes 786440 | tf_op jit(solution)/shard_map/ppermute | solution.py:61
  102.8 10.9 %collective-permute-start.9 = (bf16[32,128,128]{2,1,0:T(8,128)(2,1)}, bf16[32,128,128]{2,1,0:T(8,128)(2,1)S(1)}, u32[]{:S(2)}, u32[]{:S(2)}) collective-permute-start(bf16[32,128,128]{2,1,0:T(8,128)(2,1)} %constant_dynamic-update-slice_fusion), channel_id=1, source_target_pairs={{0,1},{1,0},{2,3},{3,2},{4,5},{5,4},{6,7},{7,6},{8,9},{9,8},{10,11... | collective-permute-start | bytes 3145736 | tf_op jit(solution)/shard_map/ppermute | solution.py:52
  127.8 4.4 %all-to-all-done.1 = bf16[16,3,128,128]{3,2,1,0:T(8,128)(2,1)} async-done(((bf16[16,3,128,128]{3,2,1,0:T(8,128)(2,1)}), bf16[16,3,128,128]{3,2,1,0:T(8,128)(2,1)}, u32[]{:S(2)}, u32[]{:S(2)}) %all-to-all-start.1) | async-done | bytes 1572896 | tf_op jit(solution)/shard_map/all_to_all | solution.py:134
  135.3 3.5 %fusion = bf16[24,128,128]{2,1,0:T(8,128)(2,1)S(1)} fusion(bf16[24,128,128]{2,1,0:T(8,128)(2,1)S(1)} %copy-done.2, bf16[24,128,128]{2,1,0:T(8,128)(2,1)} %param.16, f32[24,128,128]{2,1,0:T(8,128)} %fusion.11, bf16[24,128,128]{2,1,0:T(8,128)(2,1)S(1)} %copy-done, bf16[24,128,128]{2,1,0:T(8,128)(2,1)} %gather_fusion.5, f32[24]{0:T(128)S(1)} %copy-done.11, ...), kind=kOutput, calls=%fused_computation.70 | convolution fusion | flops 206831616 | bytes 5517600 | tf_op jit(solution)/shard_map/pac,pdc->pad/dot_general | solution.py:24
  140.8 10.9 %all-to-all-start.2 = ((bf16[16,3,128,128]{3,2,1,0:T(8,128)(2,1)}), bf16[16,3,128,128]{3,2,1,0:T(8,128)(2,1)}, u32[]{:S(2)}, u32[]{:S(2)}) async-start(bf16[16,3,128,128]{3,2,1,0:T(8,128)(2,1)} %bitcast.268), calls=%async_computation.2 | async-start | bytes 3145728 | tf_op jit(solution)/shard_map/all_to_all | solution.py:134
  163.1 4.8 %collective-permute-start.12 = (bf16[8,128,128]{2,1,0:T(8,128)(2,1)S(1)}, bf16[8,128,128]{2,1,0:T(8,128)(2,1)S(1)}, u32[]{:S(2)}, u32[]{:S(2)}) collective-permute-start(bf16[8,128,128]{2,1,0:T(8,128)(2,1)S(1)} %get-tuple-element.38), channel_id=1, source_target_pairs={{0,12},{1,29},{2,14},{3,31},{4,8},{5,25},{6,10},{7,27},{8,20},{9,5... | collective-permute-start | bytes 786440 | tf_op jit(solution)/shard_map/ppermute | solution.py:61
  171.3 4.8 %collective-permute-start.14 = (bf16[8,128,128]{2,1,0:T(8,128)(2,1)S(1)}, bf16[8,128,128]{2,1,0:T(8,128)(2,1)S(1)}, u32[]{:S(2)}, u32[]{:S(2)}) collective-permute-start(bf16[8,128,128]{2,1,0:T(8,128)(2,1)S(1)} %get-tuple-element.40), channel_id=1, source_target_pairs={{0,4},{1,17},{2,6},{3,19},{4,0},{5,21},{6,2},{7,23},{8,12},{9,25},... | collective-permute-start | bytes 786440 | tf_op jit(solution)/shard_map/ppermute | solution.py:61
  185.5 4.4 %collective-permute-start.18 = (bf16[8,128,128]{2,1,0:T(8,128)(2,1)S(1)}, bf16[8,128,128]{2,1,0:T(8,128)(2,1)S(1)}, u32[]{:S(2)}, u32[]{:S(2)}) collective-permute-start(bf16[8,128,128]{2,1,0:T(8,128)(2,1)S(1)} %get-tuple-element.21), channel_id=1, source_target_pairs={{0,2},{1,7},{2,4},{3,1},{4,6},{5,3},{6,0},{7,5},{8,10},{9,15},{10,... | collective-permute-start | bytes 786440 | tf_op jit(solution)/shard_map/ppermute | solution.py:61
  194.3 12.0 %collective-permute-start.19 = (bf16[32,128,128]{2,1,0:T(8,128)(2,1)S(1)}, bf16[32,128,128]{2,1,0:T(8,128)(2,1)S(1)}, u32[]{:S(2)}, u32[]{:S(2)}) collective-permute-start(bf16[32,128,128]{2,1,0:T(8,128)(2,1)S(1)} %constant_dynamic-update-slice_fusion.17), channel_id=1, source_target_pairs={{0,1},{1,0},{2,3},{3,2},{4,5},{5,4},{6,7},{7,6},{8,9},{9,8},{10,11... | collective-permute-start | bytes 3145736 | tf_op jit(solution)/shard_map/ppermute | solution.py:52
  223.8 3.5 %fusion.1 = bf16[24,128,128]{2,1,0:T(8,128)(2,1)S(1)} fusion(bf16[24,128,128]{2,1,0:T(8,128)(2,1)S(1)} %fusion, bf16[24,128,128]{2,1,0:T(8,128)(2,1)} %param.16, f32[24,128,128]{2,1,0:T(8,128)} %fusion.12, bf16[24,128,128]{2,1,0:T(8,128)(2,1)S(1)} %copy-done, bf16[24,128,128]{2,1,0:T(8,128)(2,1)} %gather_fusion.10, f32[24]{0:T(128)S(1)} %copy-done.11, ...), kind=kOutput, calls=%fused_computation.71 | convolution fusion | flops 206831616 | bytes 5517600 | tf_op jit(solution)/shard_map/pac,pdc->pad/dot_general | solution.py:24
  229.3 11.6 %all-to-all-start.3 = ((bf16[16,3,128,128]{3,2,1,0:T(8,128)(2,1)}), bf16[16,3,128,128]{3,2,1,0:T(8,128)(2,1)}, u32[]{:S(2)}, u32[]{:S(2)}) async-start(bf16[16,3,128,128]{3,2,1,0:T(8,128)(2,1)} %bitcast.267), calls=%async_computation.3 | async-start | bytes 3145728 | tf_op jit(solution)/shard_map/all_to_all | solution.py:134
  252.0 4.8 %collective-permute-start.22 = (bf16[8,128,128]{2,1,0:T(8,128)(2,1)S(1)}, bf16[8,128,128]{2,1,0:T(8,128)(2,1)S(1)}, u32[]{:S(2)}, u32[]{:S(2)}) collective-permute-start(bf16[8,128,128]{2,1,0:T(8,128)(2,1)S(1)} %get-tuple-element.30), channel_id=1, source_target_pairs={{0,12},{1,29},{2,14},{3,31},{4,8},{5,25},{6,10},{7,27},{8,20},{9,5... | collective-permute-start | bytes 786440 | tf_op jit(solution)/shard_map/ppermute | solution.py:61
  260.2 4.8 %collective-permute-start.24 = (bf16[8,128,128]{2,1,0:T(8,128)(2,1)S(1)}, bf16[8,128,128]{2,1,0:T(8,128)(2,1)S(1)}, u32[]{:S(2)}, u32[]{:S(2)}) collective-permute-start(bf16[8,128,128]{2,1,0:T(8,128)(2,1)S(1)} %get-tuple-element.32), channel_id=1, source_target_pairs={{0,4},{1,17},{2,6},{3,19},{4,0},{5,21},{6,2},{7,23},{8,12},{9,25},... | collective-permute-start | bytes 786440 | tf_op jit(solution)/shard_map/ppermute | solution.py:61
  274.4 4.4 %collective-permute-start.28 = (bf16[8,128,128]{2,1,0:T(8,128)(2,1)S(1)}, bf16[8,128,128]{2,1,0:T(8,128)(2,1)S(1)}, u32[]{:S(2)}, u32[]{:S(2)}) collective-permute-start(bf16[8,128,128]{2,1,0:T(8,128)(2,1)S(1)} %get-tuple-element.25), channel_id=1, source_target_pairs={{0,2},{1,7},{2,4},{3,1},{4,6},{5,3},{6,0},{7,5},{8,10},{9,15},{10,... | collective-permute-start | bytes 786440 | tf_op jit(solution)/shard_map/ppermute | solution.py:61
  283.2 9.3 %collective-permute-start.29 = (bf16[32,128,128]{2,1,0:T(8,128)(2,1)S(1)}, bf16[32,128,128]{2,1,0:T(8,128)(2,1)S(1)}, u32[]{:S(2)}, u32[]{:S(2)}) collective-permute-start(bf16[32,128,128]{2,1,0:T(8,128)(2,1)S(1)} %constant_dynamic-update-slice_fusion.34), channel_id=1, source_target_pairs={{0,1},{1,0},{2,3},{3,2},{4,5},{5,4},{6,7},{7,6},{8,9},{9,8},{10,11... | collective-permute-start | bytes 3145736 | tf_op jit(solution)/shard_map/ppermute | solution.py:52
  303.6 6.4 %all-to-all-done.3 = bf16[16,3,128,128]{3,2,1,0:T(8,128)(2,1)} async-done(((bf16[16,3,128,128]{3,2,1,0:T(8,128)(2,1)}), bf16[16,3,128,128]{3,2,1,0:T(8,128)(2,1)}, u32[]{:S(2)}, u32[]{:S(2)}) %all-to-all-start.3) | async-done | bytes 1572896 | tf_op jit(solution)/shard_map/all_to_all | solution.py:134
  312.2 4.4 %fusion.87 = (bf16[24,128,128]{2,1,0:T(8,128)(2,1)}, bf16[24,128,128]{2,1,0:T(8,128)(2,1)}) fusion(f32[24]{0:T(128)S(1)} %copy-done.9, f32[24,128]{1,0:T(8,128)S(1)} %copy-done.10, bf16[24,128,128]{2,1,0:T(8,128)(2,1)S(1)} %fusion.1, bf16[24,128,128]{2,1,0:T(8,128)(2,1)S(1)} %copy-done, bf16[24,128,128]{2,1,0:T(8,128)(2,1)S(1)} %gather_fusion.15, ...), kind=kOutput, calls=%fused_computation.281 | convolution fusion | flops 207224832 | bytes 6304032 | tf_op jit(solution)/shard_map/pac,pdc->pad/dot_general | solution.py:24
  (219 shorter events, 144.3 us)
Async XLA Ops:
  4.5 35.6 %all-to-all-start = ((s32[16,1,3]{2,1,0:T(1,128)}), s32[16,1,3]{2,1,0:T(1,128)S(1)}, u32[]{:S(2)}, u32[]{:S(2)}) async-start(s32[16,1,3]{2,1,0:T(1,128)} %bitcast.46), calls=%async_computation | async-start | bytes 16384 | tf_op jit(solution)/shard_map/all_to_all | solution.py:119
  43.3 22.6 %collective-permute-start = (bf16[32,128,128]{2,1,0:T(8,128)(2,1)}, bf16[32,128,128]{2,1,0:T(8,128)(2,1)}, u32[]{:S(2)}, u32[]{:S(2)}) collective-permute-start(bf16[32,128,128]{2,1,0:T(8,128)(2,1)} %gather_fusion.2), channel_id=1, source_target_pairs={{0,1},{1,0},{2,3},{3,2},{4,5},{5,4},{6,7},{7,6},{8,9},{9,8},{10,11... | collective-permute-start | bytes 3145736 | tf_op jit(solution)/shard_map/ppermute | solution.py:52
  50.5 81.6 %all-to-all-start.1 = ((bf16[16,3,128,128]{3,2,1,0:T(8,128)(2,1)}), bf16[16,3,128,128]{3,2,1,0:T(8,128)(2,1)}, u32[]{:S(2)}, u32[]{:S(2)}) async-start(bf16[16,3,128,128]{3,2,1,0:T(8,128)(2,1)} %bitcast.48), calls=%async_computation.1 | async-start | bytes 3145728 | tf_op jit(solution)/shard_map/all_to_all | solution.py:134
  67.3 16.1 %collective-permute-start.1 = (bf16[8,128,128]{2,1,0:T(8,128)(2,1)S(1)}, bf16[8,128,128]{2,1,0:T(8,128)(2,1)S(1)}, u32[]{:S(2)}, u32[]{:S(2)}) collective-permute-start(bf16[8,128,128]{2,1,0:T(8,128)(2,1)S(1)} %get-tuple-element.45), channel_id=1, source_target_pairs={{0,18},{1,23},{2,20},{3,17},{4,22},{5,19},{6,16},{7,21},{8,26},{9,... | collective-permute-start | bytes 786440 | tf_op jit(solution)/shard_map/ppermute | solution.py:61
  69.8 16.6 %collective-permute-start.2 = (bf16[8,128,128]{2,1,0:T(8,128)(2,1)S(1)}, bf16[8,128,128]{2,1,0:T(8,128)(2,1)S(1)}, u32[]{:S(2)}, u32[]{:S(2)}) collective-permute-start(bf16[8,128,128]{2,1,0:T(8,128)(2,1)S(1)} %get-tuple-element.46), channel_id=1, source_target_pairs={{0,12},{1,29},{2,14},{3,31},{4,8},{5,25},{6,10},{7,27},{8,20},{9,5... | collective-permute-start | bytes 786440 | tf_op jit(solution)/shard_map/ppermute | solution.py:61
  74.6 14.6 %collective-permute-start.3 = (bf16[8,128,128]{2,1,0:T(8,128)(2,1)S(1)}, bf16[8,128,128]{2,1,0:T(8,128)(2,1)S(1)}, u32[]{:S(2)}, u32[]{:S(2)}) collective-permute-start(bf16[8,128,128]{2,1,0:T(8,128)(2,1)S(1)} %get-tuple-element.47), channel_id=1, source_target_pairs={{0,0},{1,21},{2,2},{3,23},{4,4},{5,17},{6,6},{7,19},{8,8},{9,29},{... | collective-permute-start | bytes 786440 | tf_op jit(solution)/shard_map/ppermute | solution.py:61
  78.0 14.1 %collective-permute-start.4 = (bf16[8,128,128]{2,1,0:T(8,128)(2,1)S(1)}, bf16[8,128,128]{2,1,0:T(8,128)(2,1)S(1)}, u32[]{:S(2)}, u32[]{:S(2)}) collective-permute-start(bf16[8,128,128]{2,1,0:T(8,128)(2,1)S(1)} %get-tuple-element.48), channel_id=1, source_target_pairs={{0,4},{1,17},{2,6},{3,19},{4,0},{5,21},{6,2},{7,23},{8,12},{9,25},... | collective-permute-start | bytes 786440 | tf_op jit(solution)/shard_map/ppermute | solution.py:61
  83.4 16.0 %collective-permute-start.5 = (bf16[8,128,128]{2,1,0:T(8,128)(2,1)S(1)}, bf16[8,128,128]{2,1,0:T(8,128)(2,1)S(1)}, u32[]{:S(2)}, u32[]{:S(2)}) collective-permute-start(bf16[8,128,128]{2,1,0:T(8,128)(2,1)S(1)} %get-tuple-element.14), channel_id=1, source_target_pairs={{0,10},{1,31},{2,12},{3,25},{4,14},{5,27},{6,8},{7,29},{8,18},{9,7... | collective-permute-start | bytes 786440 | tf_op jit(solution)/shard_map/ppermute | solution.py:61
  86.4 13.1 %collective-permute-start.6 = (bf16[8,128,128]{2,1,0:T(8,128)(2,1)S(1)}, bf16[8,128,128]{2,1,0:T(8,128)(2,1)S(1)}, u32[]{:S(2)}, u32[]{:S(2)}) collective-permute-start(bf16[8,128,128]{2,1,0:T(8,128)(2,1)S(1)} %get-tuple-element.15), channel_id=1, source_target_pairs={{0,14},{1,27},{2,8},{3,29},{4,10},{5,31},{6,12},{7,25},{8,22},{9,3... | collective-permute-start | bytes 786440 | tf_op jit(solution)/shard_map/ppermute | solution.py:61
  102.8 19.1 %collective-permute-start.9 = (bf16[32,128,128]{2,1,0:T(8,128)(2,1)}, bf16[32,128,128]{2,1,0:T(8,128)(2,1)S(1)}, u32[]{:S(2)}, u32[]{:S(2)}) collective-permute-start(bf16[32,128,128]{2,1,0:T(8,128)(2,1)} %constant_dynamic-update-slice_fusion), channel_id=1, source_target_pairs={{0,1},{1,0},{2,3},{3,2},{4,5},{5,4},{6,7},{7,6},{8,9},{9,8},{10,11... | collective-permute-start | bytes 3145736 | tf_op jit(solution)/shard_map/ppermute | solution.py:52
  140.8 79.9 %all-to-all-start.2 = ((bf16[16,3,128,128]{3,2,1,0:T(8,128)(2,1)}), bf16[16,3,128,128]{3,2,1,0:T(8,128)(2,1)}, u32[]{:S(2)}, u32[]{:S(2)}) async-start(bf16[16,3,128,128]{3,2,1,0:T(8,128)(2,1)} %bitcast.268), calls=%async_computation.2 | async-start | bytes 3145728 | tf_op jit(solution)/shard_map/all_to_all | solution.py:134
  160.6 15.5 %collective-permute-start.11 = (bf16[8,128,128]{2,1,0:T(8,128)(2,1)S(1)}, bf16[8,128,128]{2,1,0:T(8,128)(2,1)S(1)}, u32[]{:S(2)}, u32[]{:S(2)}) collective-permute-start(bf16[8,128,128]{2,1,0:T(8,128)(2,1)S(1)} %get-tuple-element.37), channel_id=1, source_target_pairs={{0,18},{1,23},{2,20},{3,17},{4,22},{5,19},{6,16},{7,21},{8,26},{9,... | collective-permute-start | bytes 786440 | tf_op jit(solution)/shard_map/ppermute | solution.py:61
  163.1 16.0 %collective-permute-start.12 = (bf16[8,128,128]{2,1,0:T(8,128)(2,1)S(1)}, bf16[8,128,128]{2,1,0:T(8,128)(2,1)S(1)}, u32[]{:S(2)}, u32[]{:S(2)}) collective-permute-start(bf16[8,128,128]{2,1,0:T(8,128)(2,1)S(1)} %get-tuple-element.38), channel_id=1, source_target_pairs={{0,12},{1,29},{2,14},{3,31},{4,8},{5,25},{6,10},{7,27},{8,20},{9,5... | collective-permute-start | bytes 786440 | tf_op jit(solution)/shard_map/ppermute | solution.py:61
  167.9 14.7 %collective-permute-start.13 = (bf16[8,128,128]{2,1,0:T(8,128)(2,1)S(1)}, bf16[8,128,128]{2,1,0:T(8,128)(2,1)S(1)}, u32[]{:S(2)}, u32[]{:S(2)}) collective-permute-start(bf16[8,128,128]{2,1,0:T(8,128)(2,1)S(1)} %get-tuple-element.39), channel_id=1, source_target_pairs={{0,0},{1,21},{2,2},{3,23},{4,4},{5,17},{6,6},{7,19},{8,8},{9,29},{... | collective-permute-start | bytes 786440 | tf_op jit(solution)/shard_map/ppermute | solution.py:61
  171.3 14.2 %collective-permute-start.14 = (bf16[8,128,128]{2,1,0:T(8,128)(2,1)S(1)}, bf16[8,128,128]{2,1,0:T(8,128)(2,1)S(1)}, u32[]{:S(2)}, u32[]{:S(2)}) collective-permute-start(bf16[8,128,128]{2,1,0:T(8,128)(2,1)S(1)} %get-tuple-element.40), channel_id=1, source_target_pairs={{0,4},{1,17},{2,6},{3,19},{4,0},{5,21},{6,2},{7,23},{8,12},{9,25},... | collective-permute-start | bytes 786440 | tf_op jit(solution)/shard_map/ppermute | solution.py:61
  176.1 14.0 %collective-permute-start.15 = (bf16[8,128,128]{2,1,0:T(8,128)(2,1)S(1)}, bf16[8,128,128]{2,1,0:T(8,128)(2,1)S(1)}, u32[]{:S(2)}, u32[]{:S(2)}) collective-permute-start(bf16[8,128,128]{2,1,0:T(8,128)(2,1)S(1)} %get-tuple-element.18), channel_id=1, source_target_pairs={{0,10},{1,31},{2,12},{3,25},{4,14},{5,27},{6,8},{7,29},{8,18},{9,7... | collective-permute-start | bytes 786440 | tf_op jit(solution)/shard_map/ppermute | solution.py:61
  194.3 17.3 %collective-permute-start.19 = (bf16[32,128,128]{2,1,0:T(8,128)(2,1)S(1)}, bf16[32,128,128]{2,1,0:T(8,128)(2,1)S(1)}, u32[]{:S(2)}, u32[]{:S(2)}) collective-permute-start(bf16[32,128,128]{2,1,0:T(8,128)(2,1)S(1)} %constant_dynamic-update-slice_fusion.17), channel_id=1, source_target_pairs={{0,1},{1,0},{2,3},{3,2},{4,5},{5,4},{6,7},{7,6},{8,9},{9,8},{10,11... | collective-permute-start | bytes 3145736 | tf_op jit(solution)/shard_map/ppermute | solution.py:52
  229.3 80.7 %all-to-all-start.3 = ((bf16[16,3,128,128]{3,2,1,0:T(8,128)(2,1)}), bf16[16,3,128,128]{3,2,1,0:T(8,128)(2,1)}, u32[]{:S(2)}, u32[]{:S(2)}) async-start(bf16[16,3,128,128]{3,2,1,0:T(8,128)(2,1)} %bitcast.267), calls=%async_computation.3 | async-start | bytes 3145728 | tf_op jit(solution)/shard_map/all_to_all | solution.py:134
  249.5 15.5 %collective-permute-start.21 = (bf16[8,128,128]{2,1,0:T(8,128)(2,1)S(1)}, bf16[8,128,128]{2,1,0:T(8,128)(2,1)S(1)}, u32[]{:S(2)}, u32[]{:S(2)}) collective-permute-start(bf16[8,128,128]{2,1,0:T(8,128)(2,1)S(1)} %get-tuple-element.29), channel_id=1, source_target_pairs={{0,18},{1,23},{2,20},{3,17},{4,22},{5,19},{6,16},{7,21},{8,26},{9,... | collective-permute-start | bytes 786440 | tf_op jit(solution)/shard_map/ppermute | solution.py:61
  252.0 16.0 %collective-permute-start.22 = (bf16[8,128,128]{2,1,0:T(8,128)(2,1)S(1)}, bf16[8,128,128]{2,1,0:T(8,128)(2,1)S(1)}, u32[]{:S(2)}, u32[]{:S(2)}) collective-permute-start(bf16[8,128,128]{2,1,0:T(8,128)(2,1)S(1)} %get-tuple-element.30), channel_id=1, source_target_pairs={{0,12},{1,29},{2,14},{3,31},{4,8},{5,25},{6,10},{7,27},{8,20},{9,5... | collective-permute-start | bytes 786440 | tf_op jit(solution)/shard_map/ppermute | solution.py:61
  256.8 14.7 %collective-permute-start.23 = (bf16[8,128,128]{2,1,0:T(8,128)(2,1)S(1)}, bf16[8,128,128]{2,1,0:T(8,128)(2,1)S(1)}, u32[]{:S(2)}, u32[]{:S(2)}) collective-permute-start(bf16[8,128,128]{2,1,0:T(8,128)(2,1)S(1)} %get-tuple-element.31), channel_id=1, source_target_pairs={{0,0},{1,21},{2,2},{3,23},{4,4},{5,17},{6,6},{7,19},{8,8},{9,29},{... | collective-permute-start | bytes 786440 | tf_op jit(solution)/shard_map/ppermute | solution.py:61
  260.2 14.2 %collective-permute-start.24 = (bf16[8,128,128]{2,1,0:T(8,128)(2,1)S(1)}, bf16[8,128,128]{2,1,0:T(8,128)(2,1)S(1)}, u32[]{:S(2)}, u32[]{:S(2)}) collective-permute-start(bf16[8,128,128]{2,1,0:T(8,128)(2,1)S(1)} %get-tuple-element.32), channel_id=1, source_target_pairs={{0,4},{1,17},{2,6},{3,19},{4,0},{5,21},{6,2},{7,23},{8,12},{9,25},... | collective-permute-start | bytes 786440 | tf_op jit(solution)/shard_map/ppermute | solution.py:61
  265.0 14.0 %collective-permute-start.25 = (bf16[8,128,128]{2,1,0:T(8,128)(2,1)S(1)}, bf16[8,128,128]{2,1,0:T(8,128)(2,1)S(1)}, u32[]{:S(2)}, u32[]{:S(2)}) collective-permute-start(bf16[8,128,128]{2,1,0:T(8,128)(2,1)S(1)} %get-tuple-element.22), channel_id=1, source_target_pairs={{0,10},{1,31},{2,12},{3,25},{4,14},{5,27},{6,8},{7,29},{8,18},{9,7... | collective-permute-start | bytes 786440 | tf_op jit(solution)/shard_map/ppermute | solution.py:61
  283.2 14.6 %collective-permute-start.29 = (bf16[32,128,128]{2,1,0:T(8,128)(2,1)S(1)}, bf16[32,128,128]{2,1,0:T(8,128)(2,1)S(1)}, u32[]{:S(2)}, u32[]{:S(2)}) collective-permute-start(bf16[32,128,128]{2,1,0:T(8,128)(2,1)S(1)} %constant_dynamic-update-slice_fusion.34), channel_id=1, source_target_pairs={{0,1},{1,0},{2,3},{3,2},{4,5},{5,4},{6,7},{7,6},{8,9},{9,8},{10,11... | collective-permute-start | bytes 3145736 | tf_op jit(solution)/shard_map/ppermute | solution.py:52
  (23 other events, 381.3 us)

commit v2 on v1

--- a/solution.py
+++ b/solution.py
@@ -1,6 +1,8 @@
 import jax
 import jax.numpy as jnp
 from jax import lax
+from jax.experimental import pallas as pl
+from jax.experimental.pallas import tpu as pltpu
 from jax.sharding import PartitionSpec as P
 
 ITERS = 3
@@ -24,28 +26,54 @@
     return jnp.einsum("pac,pdc->pad", first, intersection, preferred_element_type=jnp.float32)
 
 
-def layout(peer, slot, peer_count, capacity):
-    marker = (peer[:, None] == jnp.arange(peer_count, dtype=jnp.int32)[None, :]).astype(jnp.int32)
-    before = jnp.sum((jnp.cumsum(marker, axis=0) - marker) * marker, axis=1)
-    target = peer * capacity + before
-    slot_table = jnp.zeros((peer_count * capacity,), jnp.int32).at[target].set(slot)
-    return (target, slot_table.reshape(peer_count, capacity))
-
-
 def ranks(peer):
     order = jnp.arange(peer.shape[0], dtype=jnp.int32)
     earlier = (peer[:, None] == peer[None, :]) & (order[None, :] < order[:, None])
     return jnp.sum(earlier.astype(jnp.int32), axis=1)
 
 
-def row_requests(row_peer, row_slot, me, capacity):
-    codes = lax.all_gather(row_peer * 32 + row_slot, "oj")
-    mine = codes // 32 == me
-    order = jnp.arange(codes.shape[1], dtype=jnp.int32)
-    lower = (order[:, None] < order[None, :]).astype(jnp.float32)
-    rank = jnp.dot(mine.astype(jnp.float32), lower).astype(jnp.int32)
-    wants = mine[:, :, None] & (rank[:, :, None] == jnp.arange(capacity, dtype=jnp.int32))
-    return jnp.sum(jnp.where(wants, (codes % 32)[:, :, None], 0), axis=1)
+def request_table(peer, slot, rank, peer_count, capacity):
+    place = jnp.arange(peer_count * capacity, dtype=jnp.int32)
+    hit = (peer * capacity + rank)[None, :] == place[:, None]
+    return jnp.sum(jnp.where(hit, slot[None, :], 0), axis=1).reshape(peer_count, capacity)
+
+
+def gather_requests(peer, slot):
+    packed = jnp.pad((peer * 32 + slot)[None, :], ((0, 7), (0, 128 - peer.shape[0])), constant_values=-1)
+    return lax.all_gather(packed, "oj", tiled=True)
+
+
+def row_requests_kernel(codes_ref, me_ref, dest_ref, out_ref):
+    codes = codes_ref[...].reshape(32, 8, 128)[:, 0, :]
+    mine = (codes >> 5) == me_ref[0]
+    above = lax.broadcasted_iota(jnp.int32, (128, 128), 0)
+    below = lax.broadcasted_iota(jnp.int32, (128, 128), 1)
+    lower = jnp.where(above < below, 1.0, 0.0).astype(jnp.bfloat16)
+    marks = jnp.where(mine, 1.0, 0.0)
+    rank = jnp.dot(marks.astype(jnp.bfloat16), lower, preferred_element_type=jnp.float32)
+    slot = (codes & 31).astype(jnp.float32) * marks
+    first = jnp.sum(jnp.where(rank < 0.5, slot, 0.0), axis=1, keepdims=True)
+    second = jnp.sum(jnp.where(rank > 0.5, slot, 0.0), axis=1, keepdims=True)
+    places = out_ref.shape[1]
+    device = lax.broadcasted_iota(jnp.int32, (32, places), 0)
+    odd = lax.broadcasted_iota(jnp.int32, (32, places), 1) & 1
+    picked = jnp.where(odd == 0, first, second)
+    picked = jnp.where(device == dest_ref[...], picked, 0.0)
+    out_ref[...] = jnp.sum(picked, axis=0, keepdims=True).astype(jnp.int32)
+
+
+def row_requests(codes, me, dest):
+    return pl.pallas_call(
+        row_requests_kernel,
+        out_shape=jax.ShapeDtypeStruct(dest.shape, jnp.int32),
+        in_specs=[
+            pl.BlockSpec(memory_space=pltpu.VMEM),
+            pl.BlockSpec(memory_space=pltpu.SMEM),
+            pl.BlockSpec(memory_space=pltpu.VMEM),
+        ],
+        out_specs=pl.BlockSpec(memory_space=pltpu.VMEM),
+        name="row_requests",
+    )(codes, me.reshape(1), dest)
 
 
 def core_exchange(blocks):
@@ -61,23 +89,23 @@
     return lax.ppermute(blocks, "oj", pairs)
 
 
-def row_plan(row_wanted, row_peer, rank, me):
+def row_plan(row_peer, rank, me, capacity):
     my_y, my_x, my_c = me // 8, me // 2 % 4, me % 2
     step_y = jnp.array([[offsets[0] for offsets in step] for step in STEPS], jnp.int32)
     step_x = jnp.array([[offsets[1] for offsets in step] for step in STEPS], jnp.int32)
     dest = (my_y + step_y) % 4 * 8 + (my_x + step_x) % 4 * 2
     core = jnp.arange(2, dtype=jnp.int32)
     dest = dest[:, :, None] + (core[None, :, None] ^ core[None, None, :])
-    slots = row_wanted[dest]
-    near = jnp.where(my_c == 0, slots[:, 0], slots[:, 1]).reshape(-1)
-    far = jnp.where(my_c == 0, slots[:, 1], slots[:, 0]).reshape(-1)
+    near = jnp.where(my_c == 0, dest[:, 0], dest[:, 1]).reshape(-1)
+    far = jnp.where(my_c == 0, dest[:, 1], dest[:, 0]).reshape(-1)
+    dest = jnp.repeat(jnp.concatenate([near, far]), capacity)[None, :]
     off = (my_y - row_peer // 8) % 4 * 4 + (my_x - row_peer // 2) % 4
     match = off[:, None, None] == (step_y * 4 + step_x)[None, :, :]
     number = jnp.arange(len(STEPS), dtype=jnp.int32)
     step = jnp.sum(jnp.where(match, number[None, :, None], 0), axis=(1, 2))
     carrier = jnp.sum(jnp.where(match, core[None, None, :], 0), axis=(1, 2))
     target = (carrier ^ my_c) * 32 + step * 4 + (carrier ^ (row_peer % 2)) * 2 + rank
-    return near, far, target
+    return dest, target
 
 
 def row_exchange(near, far, width):
@@ -115,12 +143,16 @@
     width = amplitudes.shape[1]
     row_capacity, col_capacity = 2, 3
     me = lax.axis_index("oj")
-    col_target, col_table = layout(col_peer[:, 0], col_slot, lax.axis_size("oi"), col_capacity)
+    col_rank = ranks(col_peer[:, 0])
+    col_target = col_peer[:, 0] * col_capacity + col_rank
+    col_table = request_table(col_peer[:, 0], col_slot, col_rank, lax.axis_size("oi"), col_capacity)
     col_wanted = lax.all_to_all(col_table, "oi", split_axis=0, concat_axis=0, tiled=True)
-    row_wanted = row_requests(row_peer[:, 0], row_slot, me, row_capacity)
-    near_wanted, far_wanted, row_target = row_plan(
-        row_wanted, row_peer[:, 0], ranks(row_peer[:, 0]), me
-    )
+    codes = gather_requests(row_peer[:, 0], row_slot)
+    row_dest, row_target = row_plan(row_peer[:, 0], ranks(row_peer[:, 0]), me, row_capacity)
+    col_send = amplitudes[col_wanted]
+    codes, col_send = lax.optimization_barrier((codes, col_send))
+    wanted = row_requests(codes, me, row_dest)
+    near_wanted, far_wanted = wanted[0, : wanted.shape[1] // 2], wanted[0, wanted.shape[1] // 2 :]
     matches = (
         pair_occ.reshape(-1)[:, None] == jnp.arange(fock_occ.shape[0], dtype=jnp.int32)[None, :]
     )
@@ -131,9 +163,9 @@
     current = amplitudes
     residual = jnp.zeros(amplitudes.shape, jnp.float32)
     for sweep in range(ITERS):
-        col_fetched = lax.all_to_all(
-            current[col_wanted], "oi", split_axis=0, concat_axis=0, tiled=True
-        )
+        if sweep:
+            col_send = current[col_wanted]
+        col_fetched = lax.all_to_all(col_send, "oi", split_axis=0, concat_axis=0, tiled=True)
         row_fetched = row_exchange(current[near_wanted], current[far_wanted], width)
         row_term = couple(row_fetched[row_target], row_intersection)
         col_term = couple(col_fetched.reshape(-1, width, width)[col_target], col_intersection)

time: 322 us -> 332 us (1.031)
  starting transfers between devices: 178 us -> 151 us
  waiting for transfers between devices: 26.6 us -> 51.3 us
  blocking collectives: 14.5 us -> 27.7 us
    ppermute x6, starting transfers between devices: 42.7 us -> 13.5 us  [core_exchange(): lax.ppermute(blocks, 'oj', [(source, source ^ 1) for source in range(32)])]
    all_gather x0 -> x1, blocking collectives: none -> 27.7 us  [gather_requests(): return lax.all_gather(packed, 'oj', tiled=True)]
    all_to_all x3, waiting for transfers between devices: 14.1 us -> 31.4 us  [body(): lax.all_to_all(col_send, 'oi', split_axis=0, concat_axis=0, tiled=True)]
    unnamed x1 -> x0, blocking collectives: 14.5 us -> none
    ppermute x24, waiting for transfers between devices: 9.93 us -> 17.4 us  [chip_exchange(): return lax.ppermute(blocks, 'oj', pairs)]
    unnamed x76 -> x74, local copies, waits for them, and re-layouts: 23.8 us -> 22.3 us
    gather x4 -> x3, local copies, waits for them, and re-layouts: 6.53 us -> 7.02 us  [the longest x2 3.95 us: body(): col_send = current[col_wanted]]
  transfers between devices with their start and end apart: 34 -> 34, of which waited for: 12 -> 13; matrix products, arithmetic and copies ran while one was open for 20% -> 18% of each run, Pallas kernels for 0% -> 0%
where the time goes in v2:
time: 332 us; the launch traced here: 326 us
  starting transfers between devices  151 us (45%)
  local copies, waits for them, and re-layouts  61.4 us (18%)
  waiting for transfers between devices  51.3 us (15%)
  blocking collectives  27.7 us (8%)
  matrix products  18.6 us (6%)
  other arithmetic  13.1 us (4%)
    ppermute x24, starting transfers between devices, chip_exchange(): return lax.ppermute(blocks, 'oj', pairs)  86.4 us
    all_to_all x3, starting transfers between devices, body(): lax.all_to_all(col_send, 'oi', split_axis=0, concat_axis=0, tiled=True)  34.9 us
    all_to_all x3, waiting for transfers between devices, body(): lax.all_to_all(col_send, 'oi', split_axis=0, concat_axis=0, tiled=True)  31.4 us
    all_gather x1, blocking collectives, gather_requests(): return lax.all_gather(packed, 'oj', tiled=True)  27.7 us
    unnamed x74, local copies, waits for them, and re-layouts  22.3 us
    dot_general x6, matrix products, couple(): jnp.einsum('pac,pdc->pad', first, intersection, preferred_element_type=jn...  18.6 us
    ppermute x24, waiting for transfers between devices, chip_exchange(): return lax.ppermute(blocks, 'oj', pairs)  17.4 us
    all_to_all x1, starting transfers between devices, body(): lax.all_to_all(col_table, 'oi', split_axis=0, concat_axis=0, tiled=True)  15.7 us
  transfers between devices with their start and end apart: 34, of which 13 were waited for; matrix products, arithmetic and copies ran while one was open for 18% of the time, Pallas kernels for 0%

profile of v2, /device:TPU:1, one launch (start us, length us, event | category | flops | bytes accessed | tf_op | source)
XLA Modules:
  0.0 326.0 jit_solution(806171850700390361)
XLA Ops:
  3.7 15.7 %all-to-all-start = ((s32[16,1,3]{2,1,0:T(1,128)}), s32[16,1,3]{2,1,0:T(1,128)S(1)}, u32[]{:S(2)}, u32[]{:S(2)}) async-start(s32[16,1,3]{2,1,0:T(1,128)} %bitcast.3), calls=%async_computation | async-start | bytes 16384 | tf_op jit(solution)/shard_map/all_to_all | solution.py:149
  21.3 27.7 %all_gather.3.codes_ref = s32[256,128]{1,0:T(8,128)} all-gather(s32[8,128]{1,0:T(8,128)S(1)} %pad.4), channel_id=1, replica_groups=mesh['oi'=16,'oj'=32] {'oj'}, dimensions={0}, use_global_device_ids=true | all-gather | bytes 135168 | tf_op jit(solution)/shard_map/all_gather | solution.py:43
  60.1 11.8 %all-to-all-start.1 = ((bf16[16,3,128,128]{3,2,1,0:T(8,128)(2,1)}), bf16[16,3,128,128]{3,2,1,0:T(8,128)(2,1)}, u32[]{:S(2)}, u32[]{:S(2)}) async-start(bf16[16,3,128,128]{3,2,1,0:T(8,128)(2,1)} %bitcast.266), calls=%async_computation.1 | async-start | bytes 3145728 | tf_op jit(solution)/shard_map/all_to_all | solution.py:168
  76.0 4.9 %collective-permute-start.1 = (bf16[8,128,128]{2,1,0:T(8,128)(2,1)S(1)}, bf16[8,128,128]{2,1,0:T(8,128)(2,1)S(1)}, u32[]{:S(2)}, u32[]{:S(2)}) collective-permute-start(bf16[8,128,128]{2,1,0:T(8,128)(2,1)S(1)} %get-tuple-element.49), channel_id=1, source_target_pairs={{0,18},{1,23},{2,20},{3,17},{4,22},{5,19},{6,16},{7,21},{8,26},{9,... | collective-permute-start | bytes 786440 | tf_op jit(solution)/shard_map/ppermute | solution.py:89
  83.7 5.2 %collective-permute-start.3 = (bf16[8,128,128]{2,1,0:T(8,128)(2,1)S(1)}, bf16[8,128,128]{2,1,0:T(8,128)(2,1)S(1)}, u32[]{:S(2)}, u32[]{:S(2)}) collective-permute-start(bf16[8,128,128]{2,1,0:T(8,128)(2,1)S(1)} %get-tuple-element.51), channel_id=1, source_target_pairs={{0,0},{1,21},{2,2},{3,23},{4,4},{5,17},{6,6},{7,19},{8,8},{9,29},{... | collective-permute-start | bytes 786440 | tf_op jit(solution)/shard_map/ppermute | solution.py:89
  95.8 3.7 %collective-permute-start.6 = (bf16[8,128,128]{2,1,0:T(8,128)(2,1)S(1)}, bf16[8,128,128]{2,1,0:T(8,128)(2,1)S(1)}, u32[]{:S(2)}, u32[]{:S(2)}) collective-permute-start(bf16[8,128,128]{2,1,0:T(8,128)(2,1)S(1)} %get-tuple-element.18), channel_id=1, source_target_pairs={{0,14},{1,27},{2,8},{3,29},{4,10},{5,31},{6,12},{7,25},{8,22},{9,3... | collective-permute-start | bytes 786440 | tf_op jit(solution)/shard_map/ppermute | solution.py:89
  100.3 4.0 %collective-permute-start.7 = (bf16[8,128,128]{2,1,0:T(8,128)(2,1)S(1)}, bf16[8,128,128]{2,1,0:T(8,128)(2,1)S(1)}, u32[]{:S(2)}, u32[]{:S(2)}) collective-permute-start(bf16[8,128,128]{2,1,0:T(8,128)(2,1)S(1)} %get-tuple-element.19), channel_id=1, source_target_pairs={{0,8},{1,25},{2,10},{3,27},{4,12},{5,29},{6,14},{7,31},{8,16},{9,1... | collective-permute-start | bytes 786440 | tf_op jit(solution)/shard_map/ppermute | solution.py:89
  129.9 11.1 %all-to-all-done.1 = bf16[16,3,128,128]{3,2,1,0:T(8,128)(2,1)} async-done(((bf16[16,3,128,128]{3,2,1,0:T(8,128)(2,1)}), bf16[16,3,128,128]{3,2,1,0:T(8,128)(2,1)}, u32[]{:S(2)}, u32[]{:S(2)}) %all-to-all-start.1) | async-done | bytes 1572896 | tf_op jit(solution)/shard_map/all_to_all | solution.py:168
  149.6 11.5 %all-to-all-start.2 = ((bf16[16,3,128,128]{3,2,1,0:T(8,128)(2,1)}), bf16[16,3,128,128]{3,2,1,0:T(8,128)(2,1)}, u32[]{:S(2)}, u32[]{:S(2)}) async-start(bf16[16,3,128,128]{3,2,1,0:T(8,128)(2,1)} %bitcast.268), calls=%async_computation.2 | async-start | bytes 3145728 | tf_op jit(solution)/shard_map/all_to_all | solution.py:168
  170.0 4.9 %collective-permute-start.11 = (bf16[8,128,128]{2,1,0:T(8,128)(2,1)S(1)}, bf16[8,128,128]{2,1,0:T(8,128)(2,1)S(1)}, u32[]{:S(2)}, u32[]{:S(2)}) collective-permute-start(bf16[8,128,128]{2,1,0:T(8,128)(2,1)S(1)} %get-tuple-element.41), channel_id=1, source_target_pairs={{0,18},{1,23},{2,20},{3,17},{4,22},{5,19},{6,16},{7,21},{8,26},{9,... | collective-permute-start | bytes 786440 | tf_op jit(solution)/shard_map/ppermute | solution.py:89
  177.7 5.2 %collective-permute-start.13 = (bf16[8,128,128]{2,1,0:T(8,128)(2,1)S(1)}, bf16[8,128,128]{2,1,0:T(8,128)(2,1)S(1)}, u32[]{:S(2)}, u32[]{:S(2)}) collective-permute-start(bf16[8,128,128]{2,1,0:T(8,128)(2,1)S(1)} %get-tuple-element.43), channel_id=1, source_target_pairs={{0,0},{1,21},{2,2},{3,23},{4,4},{5,17},{6,6},{7,19},{8,8},{9,29},{... | collective-permute-start | bytes 786440 | tf_op jit(solution)/shard_map/ppermute | solution.py:89
  183.0 3.7 %collective-permute-start.14 = (bf16[8,128,128]{2,1,0:T(8,128)(2,1)S(1)}, bf16[8,128,128]{2,1,0:T(8,128)(2,1)S(1)}, u32[]{:S(2)}, u32[]{:S(2)}) collective-permute-start(bf16[8,128,128]{2,1,0:T(8,128)(2,1)S(1)} %get-tuple-element.44), channel_id=1, source_target_pairs={{0,4},{1,17},{2,6},{3,19},{4,0},{5,21},{6,2},{7,23},{8,12},{9,25},... | collective-permute-start | bytes 786440 | tf_op jit(solution)/shard_map/ppermute | solution.py:89
  189.2 3.7 %collective-permute-start.16 = (bf16[8,128,128]{2,1,0:T(8,128)(2,1)S(1)}, bf16[8,128,128]{2,1,0:T(8,128)(2,1)S(1)}, u32[]{:S(2)}, u32[]{:S(2)}) collective-permute-start(bf16[8,128,128]{2,1,0:T(8,128)(2,1)S(1)} %get-tuple-element.23), channel_id=1, source_target_pairs={{0,14},{1,27},{2,8},{3,29},{4,10},{5,31},{6,12},{7,25},{8,22},{9,3... | collective-permute-start | bytes 786440 | tf_op jit(solution)/shard_map/ppermute | solution.py:89
  194.2 4.2 %collective-permute-start.17 = (bf16[8,128,128]{2,1,0:T(8,128)(2,1)S(1)}, bf16[8,128,128]{2,1,0:T(8,128)(2,1)S(1)}, u32[]{:S(2)}, u32[]{:S(2)}) collective-permute-start(bf16[8,128,128]{2,1,0:T(8,128)(2,1)S(1)} %get-tuple-element.24), channel_id=1, source_target_pairs={{0,8},{1,25},{2,10},{3,27},{4,12},{5,29},{6,14},{7,31},{8,16},{9,1... | collective-permute-start | bytes 786440 | tf_op jit(solution)/shard_map/ppermute | solution.py:89
  202.6 4.3 %collective-permute-done.18 = bf16[8,128,128]{2,1,0:T(8,128)(2,1)S(1)} collective-permute-done((bf16[8,128,128]{2,1,0:T(8,128)(2,1)S(1)}, bf16[8,128,128]{2,1,0:T(8,128)(2,1)S(1)}, u32[]{:S(2)}, u32[]{:S(2)}) %collective-permute-start.18) | collective-permute-done | bytes 262176 | tf_op jit(solution)/shard_map/ppermute | solution.py:89
  220.2 9.9 %all-to-all-done.2 = bf16[16,3,128,128]{3,2,1,0:T(8,128)(2,1)} async-done(((bf16[16,3,128,128]{3,2,1,0:T(8,128)(2,1)}), bf16[16,3,128,128]{3,2,1,0:T(8,128)(2,1)}, u32[]{:S(2)}, u32[]{:S(2)}) %all-to-all-start.2) | async-done | bytes 1572896 | tf_op jit(solution)/shard_map/all_to_all | solution.py:168
  238.7 11.6 %all-to-all-start.3 = ((bf16[16,3,128,128]{3,2,1,0:T(8,128)(2,1)}), bf16[16,3,128,128]{3,2,1,0:T(8,128)(2,1)}, u32[]{:S(2)}, u32[]{:S(2)}) async-start(bf16[16,3,128,128]{3,2,1,0:T(8,128)(2,1)} %bitcast.267), calls=%async_computation.3 | async-start | bytes 3145728 | tf_op jit(solution)/shard_map/all_to_all | solution.py:168
  258.9 4.9 %collective-permute-start.21 = (bf16[8,128,128]{2,1,0:T(8,128)(2,1)S(1)}, bf16[8,128,128]{2,1,0:T(8,128)(2,1)S(1)}, u32[]{:S(2)}, u32[]{:S(2)}) collective-permute-start(bf16[8,128,128]{2,1,0:T(8,128)(2,1)S(1)} %get-tuple-element.33), channel_id=1, source_target_pairs={{0,18},{1,23},{2,20},{3,17},{4,22},{5,19},{6,16},{7,21},{8,26},{9,... | collective-permute-start | bytes 786440 | tf_op jit(solution)/shard_map/ppermute | solution.py:89
  266.6 5.2 %collective-permute-start.23 = (bf16[8,128,128]{2,1,0:T(8,128)(2,1)S(1)}, bf16[8,128,128]{2,1,0:T(8,128)(2,1)S(1)}, u32[]{:S(2)}, u32[]{:S(2)}) collective-permute-start(bf16[8,128,128]{2,1,0:T(8,128)(2,1)S(1)} %get-tuple-element.35), channel_id=1, source_target_pairs={{0,0},{1,21},{2,2},{3,23},{4,4},{5,17},{6,6},{7,19},{8,8},{9,29},{... | collective-permute-start | bytes 786440 | tf_op jit(solution)/shard_map/ppermute | solution.py:89
  278.0 3.7 %collective-permute-start.26 = (bf16[8,128,128]{2,1,0:T(8,128)(2,1)S(1)}, bf16[8,128,128]{2,1,0:T(8,128)(2,1)S(1)}, u32[]{:S(2)}, u32[]{:S(2)}) collective-permute-start(bf16[8,128,128]{2,1,0:T(8,128)(2,1)S(1)} %get-tuple-element.27), channel_id=1, source_target_pairs={{0,14},{1,27},{2,8},{3,29},{4,10},{5,31},{6,12},{7,25},{8,22},{9,3... | collective-permute-start | bytes 786440 | tf_op jit(solution)/shard_map/ppermute | solution.py:89
  283.1 4.2 %collective-permute-start.27 = (bf16[8,128,128]{2,1,0:T(8,128)(2,1)S(1)}, bf16[8,128,128]{2,1,0:T(8,128)(2,1)S(1)}, u32[]{:S(2)}, u32[]{:S(2)}) collective-permute-start(bf16[8,128,128]{2,1,0:T(8,128)(2,1)S(1)} %get-tuple-element.28), channel_id=1, source_target_pairs={{0,8},{1,25},{2,10},{3,27},{4,12},{5,29},{6,14},{7,31},{8,16},{9,1... | collective-permute-start | bytes 786440 | tf_op jit(solution)/shard_map/ppermute | solution.py:89
  291.5 4.3 %collective-permute-done.28 = bf16[8,128,128]{2,1,0:T(8,128)(2,1)S(1)} collective-permute-done((bf16[8,128,128]{2,1,0:T(8,128)(2,1)S(1)}, bf16[8,128,128]{2,1,0:T(8,128)(2,1)S(1)}, u32[]{:S(2)}, u32[]{:S(2)}) %collective-permute-start.28) | collective-permute-done | bytes 262176 | tf_op jit(solution)/shard_map/ppermute | solution.py:89
  308.9 10.4 %all-to-all-done.3 = bf16[16,3,128,128]{3,2,1,0:T(8,128)(2,1)} async-done(((bf16[16,3,128,128]{3,2,1,0:T(8,128)(2,1)}), bf16[16,3,128,128]{3,2,1,0:T(8,128)(2,1)}, u32[]{:S(2)}, u32[]{:S(2)}) %all-to-all-start.3) | async-done | bytes 1572896 | tf_op jit(solution)/shard_map/all_to_all | solution.py:168
  321.6 4.4 %fusion.81 = (bf16[24,128,128]{2,1,0:T(8,128)(2,1)}, bf16[24,128,128]{2,1,0:T(8,128)(2,1)}) fusion(f32[24]{0:T(128)S(1)} %copy-done.9, f32[24,128]{1,0:T(8,128)S(1)} %copy-done.10, bf16[24,128,128]{2,1,0:T(8,128)(2,1)S(1)} %fusion.1, bf16[24,128,128]{2,1,0:T(8,128)(2,1)S(1)} %copy-done, bf16[24,128,128]{2,1,0:T(8,128)(2,1)S(1)} %gather_fusion.14, ...), kind=kOutput, calls=%fused_computation.263 | convolution fusion | flops 207224832 | bytes 6304032 | tf_op jit(solution)/shard_map/pac,pdc->pad/dot_general | solution.py:26
  (207 shorter events, 143.9 us)
Async XLA Ops:
  3.7 46.0 %all-to-all-start = ((s32[16,1,3]{2,1,0:T(1,128)}), s32[16,1,3]{2,1,0:T(1,128)S(1)}, u32[]{:S(2)}, u32[]{:S(2)}) async-start(s32[16,1,3]{2,1,0:T(1,128)} %bitcast.3), calls=%async_computation | async-start | bytes 16384 | tf_op jit(solution)/shard_map/all_to_all | solution.py:149
  57.9 16.6 %collective-permute-start = (bf16[32,128,128]{2,1,0:T(8,128)(2,1)}, bf16[32,128,128]{2,1,0:T(8,128)(2,1)}, u32[]{:S(2)}, u32[]{:S(2)}) collective-permute-start(bf16[32,128,128]{2,1,0:T(8,128)(2,1)} %gather_fusion.2), channel_id=1, source_target_pairs={{0,1},{1,0},{2,3},{3,2},{4,5},{5,4},{6,7},{7,6},{8,9},{9,8},{10,11... | collective-permute-start | bytes 3145736 | tf_op jit(solution)/shard_map/ppermute | solution.py:80
  60.1 80.9 %all-to-all-start.1 = ((bf16[16,3,128,128]{3,2,1,0:T(8,128)(2,1)}), bf16[16,3,128,128]{3,2,1,0:T(8,128)(2,1)}, u32[]{:S(2)}, u32[]{:S(2)}) async-start(bf16[16,3,128,128]{3,2,1,0:T(8,128)(2,1)} %bitcast.266), calls=%async_computation.1 | async-start | bytes 3145728 | tf_op jit(solution)/shard_map/all_to_all | solution.py:168
  76.0 17.2 %collective-permute-start.1 = (bf16[8,128,128]{2,1,0:T(8,128)(2,1)S(1)}, bf16[8,128,128]{2,1,0:T(8,128)(2,1)S(1)}, u32[]{:S(2)}, u32[]{:S(2)}) collective-permute-start(bf16[8,128,128]{2,1,0:T(8,128)(2,1)S(1)} %get-tuple-element.49), channel_id=1, source_target_pairs={{0,18},{1,23},{2,20},{3,17},{4,22},{5,19},{6,16},{7,21},{8,26},{9,... | collective-permute-start | bytes 786440 | tf_op jit(solution)/shard_map/ppermute | solution.py:89
  81.0 14.8 %collective-permute-start.2 = (bf16[8,128,128]{2,1,0:T(8,128)(2,1)S(1)}, bf16[8,128,128]{2,1,0:T(8,128)(2,1)S(1)}, u32[]{:S(2)}, u32[]{:S(2)}) collective-permute-start(bf16[8,128,128]{2,1,0:T(8,128)(2,1)S(1)} %get-tuple-element.50), channel_id=1, source_target_pairs={{0,12},{1,29},{2,14},{3,31},{4,8},{5,25},{6,10},{7,27},{8,20},{9,5... | collective-permute-start | bytes 786440 | tf_op jit(solution)/shard_map/ppermute | solution.py:89
  83.7 16.6 %collective-permute-start.3 = (bf16[8,128,128]{2,1,0:T(8,128)(2,1)S(1)}, bf16[8,128,128]{2,1,0:T(8,128)(2,1)S(1)}, u32[]{:S(2)}, u32[]{:S(2)}) collective-permute-start(bf16[8,128,128]{2,1,0:T(8,128)(2,1)S(1)} %get-tuple-element.51), channel_id=1, source_target_pairs={{0,0},{1,21},{2,2},{3,23},{4,4},{5,17},{6,6},{7,19},{8,8},{9,29},{... | collective-permute-start | bytes 786440 | tf_op jit(solution)/shard_map/ppermute | solution.py:89
  88.9 15.4 %collective-permute-start.4 = (bf16[8,128,128]{2,1,0:T(8,128)(2,1)S(1)}, bf16[8,128,128]{2,1,0:T(8,128)(2,1)S(1)}, u32[]{:S(2)}, u32[]{:S(2)}) collective-permute-start(bf16[8,128,128]{2,1,0:T(8,128)(2,1)S(1)} %get-tuple-element.52), channel_id=1, source_target_pairs={{0,4},{1,17},{2,6},{3,19},{4,0},{5,21},{6,2},{7,23},{8,12},{9,25},... | collective-permute-start | bytes 786440 | tf_op jit(solution)/shard_map/ppermute | solution.py:89
  93.2 15.8 %collective-permute-start.5 = (bf16[8,128,128]{2,1,0:T(8,128)(2,1)S(1)}, bf16[8,128,128]{2,1,0:T(8,128)(2,1)S(1)}, u32[]{:S(2)}, u32[]{:S(2)}) collective-permute-start(bf16[8,128,128]{2,1,0:T(8,128)(2,1)S(1)} %get-tuple-element.17), channel_id=1, source_target_pairs={{0,10},{1,31},{2,12},{3,25},{4,14},{5,27},{6,8},{7,29},{8,18},{9,7... | collective-permute-start | bytes 786440 | tf_op jit(solution)/shard_map/ppermute | solution.py:89
  95.8 13.3 %collective-permute-start.6 = (bf16[8,128,128]{2,1,0:T(8,128)(2,1)S(1)}, bf16[8,128,128]{2,1,0:T(8,128)(2,1)S(1)}, u32[]{:S(2)}, u32[]{:S(2)}) collective-permute-start(bf16[8,128,128]{2,1,0:T(8,128)(2,1)S(1)} %get-tuple-element.18), channel_id=1, source_target_pairs={{0,14},{1,27},{2,8},{3,29},{4,10},{5,31},{6,12},{7,25},{8,22},{9,3... | collective-permute-start | bytes 786440 | tf_op jit(solution)/shard_map/ppermute | solution.py:89
  113.8 10.2 %collective-permute-start.9 = (bf16[32,128,128]{2,1,0:T(8,128)(2,1)}, bf16[32,128,128]{2,1,0:T(8,128)(2,1)S(1)}, u32[]{:S(2)}, u32[]{:S(2)}) collective-permute-start(bf16[32,128,128]{2,1,0:T(8,128)(2,1)} %constant_dynamic-update-slice_fusion), channel_id=1, source_target_pairs={{0,1},{1,0},{2,3},{3,2},{4,5},{5,4},{6,7},{7,6},{8,9},{9,8},{10,11... | collective-permute-start | bytes 3145736 | tf_op jit(solution)/shard_map/ppermute | solution.py:80
  149.6 80.6 %all-to-all-start.2 = ((bf16[16,3,128,128]{3,2,1,0:T(8,128)(2,1)}), bf16[16,3,128,128]{3,2,1,0:T(8,128)(2,1)}, u32[]{:S(2)}, u32[]{:S(2)}) async-start(bf16[16,3,128,128]{3,2,1,0:T(8,128)(2,1)} %bitcast.268), calls=%async_computation.2 | async-start | bytes 3145728 | tf_op jit(solution)/shard_map/all_to_all | solution.py:168
  170.0 16.6 %collective-permute-start.11 = (bf16[8,128,128]{2,1,0:T(8,128)(2,1)S(1)}, bf16[8,128,128]{2,1,0:T(8,128)(2,1)S(1)}, u32[]{:S(2)}, u32[]{:S(2)}) collective-permute-start(bf16[8,128,128]{2,1,0:T(8,128)(2,1)S(1)} %get-tuple-element.41), channel_id=1, source_target_pairs={{0,18},{1,23},{2,20},{3,17},{4,22},{5,19},{6,16},{7,21},{8,26},{9,... | collective-permute-start | bytes 786440 | tf_op jit(solution)/shard_map/ppermute | solution.py:89
  175.0 14.2 %collective-permute-start.12 = (bf16[8,128,128]{2,1,0:T(8,128)(2,1)S(1)}, bf16[8,128,128]{2,1,0:T(8,128)(2,1)S(1)}, u32[]{:S(2)}, u32[]{:S(2)}) collective-permute-start(bf16[8,128,128]{2,1,0:T(8,128)(2,1)S(1)} %get-tuple-element.42), channel_id=1, source_target_pairs={{0,12},{1,29},{2,14},{3,31},{4,8},{5,25},{6,10},{7,27},{8,20},{9,5... | collective-permute-start | bytes 786440 | tf_op jit(solution)/shard_map/ppermute | solution.py:89
  177.7 16.5 %collective-permute-start.13 = (bf16[8,128,128]{2,1,0:T(8,128)(2,1)S(1)}, bf16[8,128,128]{2,1,0:T(8,128)(2,1)S(1)}, u32[]{:S(2)}, u32[]{:S(2)}) collective-permute-start(bf16[8,128,128]{2,1,0:T(8,128)(2,1)S(1)} %get-tuple-element.43), channel_id=1, source_target_pairs={{0,0},{1,21},{2,2},{3,23},{4,4},{5,17},{6,6},{7,19},{8,8},{9,29},{... | collective-permute-start | bytes 786440 | tf_op jit(solution)/shard_map/ppermute | solution.py:89
  183.0 15.5 %collective-permute-start.14 = (bf16[8,128,128]{2,1,0:T(8,128)(2,1)S(1)}, bf16[8,128,128]{2,1,0:T(8,128)(2,1)S(1)}, u32[]{:S(2)}, u32[]{:S(2)}) collective-permute-start(bf16[8,128,128]{2,1,0:T(8,128)(2,1)S(1)} %get-tuple-element.44), channel_id=1, source_target_pairs={{0,4},{1,17},{2,6},{3,19},{4,0},{5,21},{6,2},{7,23},{8,12},{9,25},... | collective-permute-start | bytes 786440 | tf_op jit(solution)/shard_map/ppermute | solution.py:89
  186.7 13.9 %collective-permute-start.15 = (bf16[8,128,128]{2,1,0:T(8,128)(2,1)S(1)}, bf16[8,128,128]{2,1,0:T(8,128)(2,1)S(1)}, u32[]{:S(2)}, u32[]{:S(2)}) collective-permute-start(bf16[8,128,128]{2,1,0:T(8,128)(2,1)S(1)} %get-tuple-element.22), channel_id=1, source_target_pairs={{0,10},{1,31},{2,12},{3,25},{4,14},{5,27},{6,8},{7,29},{8,18},{9,7... | collective-permute-start | bytes 786440 | tf_op jit(solution)/shard_map/ppermute | solution.py:89
  189.2 11.4 %collective-permute-start.16 = (bf16[8,128,128]{2,1,0:T(8,128)(2,1)S(1)}, bf16[8,128,128]{2,1,0:T(8,128)(2,1)S(1)}, u32[]{:S(2)}, u32[]{:S(2)}) collective-permute-start(bf16[8,128,128]{2,1,0:T(8,128)(2,1)S(1)} %get-tuple-element.23), channel_id=1, source_target_pairs={{0,14},{1,27},{2,8},{3,29},{4,10},{5,31},{6,12},{7,25},{8,22},{9,3... | collective-permute-start | bytes 786440 | tf_op jit(solution)/shard_map/ppermute | solution.py:89
  238.7 80.6 %all-to-all-start.3 = ((bf16[16,3,128,128]{3,2,1,0:T(8,128)(2,1)}), bf16[16,3,128,128]{3,2,1,0:T(8,128)(2,1)}, u32[]{:S(2)}, u32[]{:S(2)}) async-start(bf16[16,3,128,128]{3,2,1,0:T(8,128)(2,1)} %bitcast.267), calls=%async_computation.3 | async-start | bytes 3145728 | tf_op jit(solution)/shard_map/all_to_all | solution.py:168
  258.9 16.6 %collective-permute-start.21 = (bf16[8,128,128]{2,1,0:T(8,128)(2,1)S(1)}, bf16[8,128,128]{2,1,0:T(8,128)(2,1)S(1)}, u32[]{:S(2)}, u32[]{:S(2)}) collective-permute-start(bf16[8,128,128]{2,1,0:T(8,128)(2,1)S(1)} %get-tuple-element.33), channel_id=1, source_target_pairs={{0,18},{1,23},{2,20},{3,17},{4,22},{5,19},{6,16},{7,21},{8,26},{9,... | collective-permute-start | bytes 786440 | tf_op jit(solution)/shard_map/ppermute | solution.py:89
  263.9 14.2 %collective-permute-start.22 = (bf16[8,128,128]{2,1,0:T(8,128)(2,1)S(1)}, bf16[8,128,128]{2,1,0:T(8,128)(2,1)S(1)}, u32[]{:S(2)}, u32[]{:S(2)}) collective-permute-start(bf16[8,128,128]{2,1,0:T(8,128)(2,1)S(1)} %get-tuple-element.34), channel_id=1, source_target_pairs={{0,12},{1,29},{2,14},{3,31},{4,8},{5,25},{6,10},{7,27},{8,20},{9,5... | collective-permute-start | bytes 786440 | tf_op jit(solution)/shard_map/ppermute | solution.py:89
  266.6 16.5 %collective-permute-start.23 = (bf16[8,128,128]{2,1,0:T(8,128)(2,1)S(1)}, bf16[8,128,128]{2,1,0:T(8,128)(2,1)S(1)}, u32[]{:S(2)}, u32[]{:S(2)}) collective-permute-start(bf16[8,128,128]{2,1,0:T(8,128)(2,1)S(1)} %get-tuple-element.35), channel_id=1, source_target_pairs={{0,0},{1,21},{2,2},{3,23},{4,4},{5,17},{6,6},{7,19},{8,8},{9,29},{... | collective-permute-start | bytes 786440 | tf_op jit(solution)/shard_map/ppermute | solution.py:89
  271.8 15.5 %collective-permute-start.24 = (bf16[8,128,128]{2,1,0:T(8,128)(2,1)S(1)}, bf16[8,128,128]{2,1,0:T(8,128)(2,1)S(1)}, u32[]{:S(2)}, u32[]{:S(2)}) collective-permute-start(bf16[8,128,128]{2,1,0:T(8,128)(2,1)S(1)} %get-tuple-element.36), channel_id=1, source_target_pairs={{0,4},{1,17},{2,6},{3,19},{4,0},{5,21},{6,2},{7,23},{8,12},{9,25},... | collective-permute-start | bytes 786440 | tf_op jit(solution)/shard_map/ppermute | solution.py:89
  275.5 13.9 %collective-permute-start.25 = (bf16[8,128,128]{2,1,0:T(8,128)(2,1)S(1)}, bf16[8,128,128]{2,1,0:T(8,128)(2,1)S(1)}, u32[]{:S(2)}, u32[]{:S(2)}) collective-permute-start(bf16[8,128,128]{2,1,0:T(8,128)(2,1)S(1)} %get-tuple-element.26), channel_id=1, source_target_pairs={{0,10},{1,31},{2,12},{3,25},{4,14},{5,27},{6,8},{7,29},{8,18},{9,7... | collective-permute-start | bytes 786440 | tf_op jit(solution)/shard_map/ppermute | solution.py:89
  278.0 11.4 %collective-permute-start.26 = (bf16[8,128,128]{2,1,0:T(8,128)(2,1)S(1)}, bf16[8,128,128]{2,1,0:T(8,128)(2,1)S(1)}, u32[]{:S(2)}, u32[]{:S(2)}) collective-permute-start(bf16[8,128,128]{2,1,0:T(8,128)(2,1)S(1)} %get-tuple-element.27), channel_id=1, source_target_pairs={{0,14},{1,27},{2,8},{3,29},{4,10},{5,31},{6,12},{7,25},{8,22},{9,3... | collective-permute-start | bytes 786440 | tf_op jit(solution)/shard_map/ppermute | solution.py:89
  (24 other events, 425.2 us)

commit v3 on v1

--- a/solution.py
+++ b/solution.py
@@ -1,6 +1,8 @@
 import jax
 import jax.numpy as jnp
 from jax import lax
+from jax.experimental import pallas as pl
+from jax.experimental.pallas import tpu as pltpu
 from jax.sharding import PartitionSpec as P
 
 ITERS = 3
@@ -95,6 +97,92 @@
     keep = jnp.concatenate([piece[:, 0].reshape(4, width, width) for piece in arrived], axis=0)
     swap = jnp.concatenate([piece[:, 1].reshape(4, width, width) for piece in arrived], axis=0)
     return jnp.concatenate([keep, core_exchange(swap)], axis=0)
+
+
+def finish_kernel(
+    target_ref,
+    wanted_ref,
+    occupied_ref,
+    fock_ref,
+    fetched_ref,
+    inter_ref,
+    base_ref,
+    own_ref,
+    energy_ref,
+    energy_t_ref,
+    new_ref,
+    second_ref,
+    block_ref,
+    in_sem,
+    out_sem,
+):
+    pairs = own_ref.shape[0]
+    arrivals = []
+    for pair in range(pairs):
+        arrivals.append(
+            pltpu.make_async_copy(
+                fetched_ref.at[target_ref[pair]], block_ref.at[pair], in_sem.at[pair]
+            )
+        )
+        arrivals[-1].start()
+    for pair in range(pairs):
+        inter = inter_ref[pair]
+        arrivals[pair].wait()
+        first = jnp.dot(inter, block_ref[pair], preferred_element_type=jnp.float32)
+        term = lax.dot_general(
+            first.astype(jnp.bfloat16),
+            inter,
+            (((1,), (1,)), ((), ())),
+            preferred_element_type=jnp.float32,
+        )
+        denominator = (
+            energy_t_ref[:, pair : pair + 1] + energy_ref[pair : pair + 1, :] - occupied_ref[pair]
+        )
+        residual = base_ref[pair] - fock_ref[pair] * term
+        new = own_ref[pair].astype(jnp.float32) - residual / denominator
+        new_ref[pair] = new.astype(jnp.bfloat16)
+        if out_sem is None:
+            second_ref[pair] = residual.astype(jnp.bfloat16)
+    if out_sem is not None:
+        sends = []
+        for place in range(second_ref.shape[0]):
+            sends.append(
+                pltpu.make_async_copy(
+                    new_ref.at[wanted_ref[place]], second_ref.at[place], out_sem.at[place]
+                )
+            )
+            sends[-1].start()
+        for send in sends:
+            send.wait()
+
+
+def last_kernel(*refs):
+    finish_kernel(*refs, None)
+
+
+def finish(target, wanted, occupied, fock, fetched, inter, base, own, energy, last):
+    pairs = own.shape[0]
+    smem, vmem = pl.BlockSpec(memory_space=pltpu.SMEM), pl.BlockSpec(memory_space=pltpu.VMEM)
+    hbm = pl.BlockSpec(memory_space=pltpu.HBM)
+    scratch = [pltpu.VMEM(own.shape, jnp.bfloat16), pltpu.SemaphoreType.DMA((pairs,))]
+    if not last:
+        scratch.append(pltpu.SemaphoreType.DMA((fetched.shape[0],)))
+    if last:
+        second_shape = jax.ShapeDtypeStruct(own.shape, jnp.bfloat16)
+    else:
+        second_shape = pltpu.HBM(fetched.shape, jnp.bfloat16)
+    return pl.pallas_call(
+        last_kernel if last else finish_kernel,
+        out_shape=(
+            jax.ShapeDtypeStruct(own.shape, jnp.bfloat16),
+            second_shape,
+        ),
+        in_specs=[smem] * 4 + [hbm] + [vmem] * 5,
+        out_specs=(vmem, vmem if last else hbm),
+        scratch_shapes=scratch,
+        compiler_params=pltpu.CompilerParams(vmem_limit_bytes=24 * 2**20),
+        name="finish_last" if last else "finish",
+    )(target, wanted, occupied, fock, fetched, inter, base, own, energy, energy.T)
 
 
 def body(
@@ -129,23 +217,29 @@
     denominator = pno_energy[:, :, None] + pno_energy[:, None, :] - occupied[:, None, None]
     ints_wide = exchange_ints.astype(jnp.float32)
     current = amplitudes
-    residual = jnp.zeros(amplitudes.shape, jnp.float32)
+    col_send = current[col_wanted.reshape(-1)]
     for sweep in range(ITERS):
-        col_fetched = lax.all_to_all(
-            current[col_wanted], "oi", split_axis=0, concat_axis=0, tiled=True
-        )
+        col_fetched = lax.all_to_all(col_send, "oi", split_axis=0, concat_axis=0, tiled=True)
         row_fetched = row_exchange(current[near_wanted], current[far_wanted], width)
         row_term = couple(row_fetched[row_target], row_intersection)
-        col_term = couple(col_fetched.reshape(-1, width, width)[col_target], col_intersection)
-        own_wide = current.astype(jnp.float32)
-        residual = (
+        base = (
             ints_wide
-            + denominator * own_wide
+            + denominator * current.astype(jnp.float32)
             - row_fock[:, None, None] * row_term
-            - col_fock[:, None, None] * col_term
-        )
-        current = (own_wide - residual / denominator).astype(jnp.bfloat16)
-    return (current, residual.astype(jnp.bfloat16))
+        )
+        current, col_send = finish(
+            col_target,
+            col_wanted.reshape(-1),
+            occupied,
+            col_fock,
+            col_fetched.reshape(-1, width, width),
+            col_intersection,
+            base,
+            current,
+            pno_energy,
+            sweep == ITERS - 1,
+        )
+    return (current, col_send)
 
 
 def solution(mesh):

time: 322 us -> 331 us (1.028)
  Pallas kernels: 0 us -> 28.4 us
  matrix products: 18.7 us -> 11.3 us
  local copies, waits for them, and re-layouts: 64.1 us -> 56.9 us
  waiting for transfers between devices: 26.6 us -> 20.1 us
    pallas_call x0 -> x3, Pallas kernels: none -> 28.4 us  [finish(): pl.pallas_call(last_kernel if last else finish_kernel, out_shape=(jax.Sha...]
    gather x6 -> x1, local copies, waits for them, and re-layouts: 14.3 us -> 1.97 us  [body(): col_send = current[col_wanted.reshape(-1)]]
    dot_general x6 -> x3, matrix products: 18.5 us -> 11.1 us  [couple(): jnp.einsum('pac,pdc->pad', first, intersection, preferred_element_type=jn...]
    all_to_all x3, waiting for transfers between devices: 14.1 us -> 7.35 us  [body(): lax.all_to_all(col_send, 'oi', split_axis=0, concat_axis=0, tiled=True)]
    ppermute x6, starting transfers between devices: 42.7 us -> 46.1 us  [core_exchange(): lax.ppermute(blocks, 'oj', [(source, source ^ 1) for source in range(32)])]
    unnamed x76 -> x85, local copies, waits for them, and re-layouts: 23.8 us -> 26.7 us
  transfers between devices with their start and end apart: 34 -> 34, of which waited for: 12 -> 12; matrix products, arithmetic and copies ran while one was open for 20% -> 22% of each run, Pallas kernels for 0% -> 0%
where the time goes in v3:
time: 331 us; the launch traced here: 326 us
  starting transfers between devices  181 us (55%)
  local copies, waits for them, and re-layouts  56.9 us (17%)
  Pallas kernels  28.4 us (9%)
  waiting for transfers between devices  20.1 us (6%)
  blocking collectives  14.5 us (4%)
  matrix products  11.3 us (3%)
  other arithmetic  10.7 us (3%)
    ppermute x24, starting transfers between devices, chip_exchange(): return lax.ppermute(blocks, 'oj', pairs)  84.9 us
    ppermute x6, starting transfers between devices, core_exchange(): lax.ppermute(blocks, 'oj', [(source, source ^ 1) for source in range(32)])  46.1 us
    all_to_all x3, starting transfers between devices, body(): lax.all_to_all(col_send, 'oi', split_axis=0, concat_axis=0, tiled=True)  34.5 us
    pallas_call x3, Pallas kernels, finish(): pl.pallas_call(last_kernel if last else finish_kernel, out_shape=(jax.Sha...  28.4 us
    unnamed x85, local copies, waits for them, and re-layouts  26.7 us
    all_to_all x1, starting transfers between devices, body(): lax.all_to_all(col_table, 'oi', split_axis=0, concat_axis=0, tiled=True)  15.7 us
    unnamed x1, blocking collectives  14.5 us
    dot_general x3, matrix products, couple(): jnp.einsum('pac,pdc->pad', first, intersection, preferred_element_type=jn...  11.1 us
  transfers between devices with their start and end apart: 34, of which 12 were waited for; matrix products, arithmetic and copies ran while one was open for 22% of the time, Pallas kernels for 0%

profile of v3, /device:TPU:1, one launch (start us, length us, event | category | flops | bytes accessed | tf_op | source)
XLA Modules:
  0.0 325.7 jit_solution(13603445949177283084)
XLA Ops:
  4.5 15.7 %all-to-all-start = ((s32[16,1,3]{2,1,0:T(1,128)}), s32[16,1,3]{2,1,0:T(1,128)S(1)}, u32[]{:S(2)}, u32[]{:S(2)}) async-start(s32[16,1,3]{2,1,0:T(1,128)} %bitcast.3), calls=%async_computation | async-start | bytes 16384 | tf_op jit(solution)/shard_map/all_to_all | solution.py:207
  23.1 14.5 %all-reduce = s32[768]{0:T(1024)S(1)} all-reduce(s32[768]{0:T(1024)S(1)} %get-tuple-element.113), channel_id=2, replica_groups=mesh['oi'=16,'oj'=32] {'oj'}, use_global_device_ids=true, to_apply=%add | all-reduce | flops 768 | bytes 6144
  43.2 5.3 %collective-permute-start = (bf16[32,128,128]{2,1,0:T(8,128)(2,1)}, bf16[32,128,128]{2,1,0:T(8,128)(2,1)}, u32[]{:S(2)}, u32[]{:S(2)}) collective-permute-start(bf16[32,128,128]{2,1,0:T(8,128)(2,1)} %gather_fusion.3), channel_id=1, source_target_pairs={{0,1},{1,0},{2,3},{3,2},{4,5},{5,4},{6,7},{7,6},{8,9},{9,8},{10,11... | collective-permute-start | bytes 3145736 | tf_op jit(solution)/shard_map/ppermute | solution.py:54
  50.6 11.9 %all-to-all-start.1 = ((bf16[48,128,128]{2,1,0:T(8,128)(2,1)}), bf16[48,128,128]{2,1,0:T(8,128)(2,1)}, u32[]{:S(2)}, u32[]{:S(2)}) async-start(bf16[48,128,128]{2,1,0:T(8,128)(2,1)} %gather_fusion), calls=%async_computation.1 | async-start | bytes 3145728 | tf_op jit(solution)/shard_map/all_to_all | solution.py:222
  68.4 4.8 %collective-permute-start.2 = (bf16[8,128,128]{2,1,0:T(8,128)(2,1)S(1)}, bf16[8,128,128]{2,1,0:T(8,128)(2,1)S(1)}, u32[]{:S(2)}, u32[]{:S(2)}) collective-permute-start(bf16[8,128,128]{2,1,0:T(8,128)(2,1)S(1)} %get-tuple-element.54), channel_id=1, source_target_pairs={{0,12},{1,29},{2,14},{3,31},{4,8},{5,25},{6,10},{7,27},{8,20},{9,5... | collective-permute-start | bytes 786440 | tf_op jit(solution)/shard_map/ppermute | solution.py:63
  76.6 4.8 %collective-permute-start.4 = (bf16[8,128,128]{2,1,0:T(8,128)(2,1)S(1)}, bf16[8,128,128]{2,1,0:T(8,128)(2,1)S(1)}, u32[]{:S(2)}, u32[]{:S(2)}) collective-permute-start(bf16[8,128,128]{2,1,0:T(8,128)(2,1)S(1)} %get-tuple-element.56), channel_id=1, source_target_pairs={{0,4},{1,17},{2,6},{3,19},{4,0},{5,21},{6,2},{7,23},{8,12},{9,25},... | collective-permute-start | bytes 786440 | tf_op jit(solution)/shard_map/ppermute | solution.py:63
  90.7 4.6 %collective-permute-start.8 = (bf16[8,128,128]{2,1,0:T(8,128)(2,1)S(1)}, bf16[8,128,128]{2,1,0:T(8,128)(2,1)S(1)}, u32[]{:S(2)}, u32[]{:S(2)}) collective-permute-start(bf16[8,128,128]{2,1,0:T(8,128)(2,1)S(1)} %get-tuple-element.21), channel_id=1, source_target_pairs={{0,2},{1,7},{2,4},{3,1},{4,6},{5,3},{6,0},{7,5},{8,10},{9,15},{10,... | collective-permute-start | bytes 786440 | tf_op jit(solution)/shard_map/ppermute | solution.py:63
  100.8 11.0 %collective-permute-start.9 = (bf16[32,128,128]{2,1,0:T(8,128)(2,1)}, bf16[32,128,128]{2,1,0:T(8,128)(2,1)}, u32[]{:S(2)}, u32[]{:S(2)}) collective-permute-start(bf16[32,128,128]{2,1,0:T(8,128)(2,1)} %constant_dynamic-update-slice_fusion), channel_id=1, source_target_pairs={{0,1},{1,0},{2,3},{3,2},{4,5},{5,4},{6,7},{7,6},{8,9},{9,8},{10,11... | collective-permute-start | bytes 3145736 | tf_op jit(solution)/shard_map/ppermute | solution.py:54
  124.3 3.8 %fusion.base_ref = f32[24,128,128]{2,1,0:T(8,128)} fusion(bf16[24,128,128]{2,1,0:T(8,128)(2,1)S(1)} %copy-done.8, bf16[24,128,128]{2,1,0:T(8,128)(2,1)S(1)} %copy-done.1, bf16[24,128,128]{2,1,0:T(8,128)(2,1)S(1)} %copy-done, bf16[24,128,128]{2,1,0:T(8,128)(2,1)} %gather_fusion.4, f32[24]{0:T(128)S(1)} %copy-done.12, f32[24]{0:T(128)S(1)} %fusion.51.occupied_ref.refs_2_, ...), kind=kOutput, calls=%fused_computation.59 | convolution fusion | flops 204865536 | bytes 4731072 | tf_op jit(solution)/shard_map/pac,pdc->pad/dot_general | solution.py:26
  128.0 4.3 %all-to-all-done.1.fetched_ref = bf16[48,128,128]{2,1,0:T(8,128)(2,1)} async-done(((bf16[48,128,128]{2,1,0:T(8,128)(2,1)}), bf16[48,128,128]{2,1,0:T(8,128)(2,1)}, u32[]{:S(2)}, u32[]{:S(2)}) %all-to-all-start.1) | async-done | bytes 1572896 | tf_op jit(solution)/shard_map/all_to_all | solution.py:222
  133.7 9.6 %finish.2 = (bf16[24,128,128]{2,1,0:T(8,128)(2,1)S(1)}, bf16[48,128,128]{2,1,0:T(8,128)(2,1)}) custom-call(s32[24]{0:T(128)S(1)} %multiply_add_fusion.target_ref.refs_0_, s32[48]{0:T(128)S(1)} %reshape.333.wanted_ref.refs_1_, f32[24]{0:T(128)S(1)} %fusion.51.occupied_ref.refs_2_, f32[24]{0:T(128)S(1)} %copy-done.7, ...), custom_call_target="tpu_custom_call" | custom-call | tf_op jit(solution)/shard_map/finish/pallas_call | solution.py:174
  143.3 10.9 %all-to-all-start.2 = ((bf16[48,128,128]{2,1,0:T(8,128)(2,1)}), bf16[48,128,128]{2,1,0:T(8,128)(2,1)}, u32[]{:S(2)}, u32[]{:S(2)}) async-start(bf16[48,128,128]{2,1,0:T(8,128)(2,1)} %get-tuple-element.22), calls=%async_computation.2 | async-start | bytes 3145728 | tf_op jit(solution)/shard_map/all_to_all | solution.py:222
  165.5 4.8 %collective-permute-start.12 = (bf16[8,128,128]{2,1,0:T(8,128)(2,1)S(1)}, bf16[8,128,128]{2,1,0:T(8,128)(2,1)S(1)}, u32[]{:S(2)}, u32[]{:S(2)}) collective-permute-start(bf16[8,128,128]{2,1,0:T(8,128)(2,1)S(1)} %get-tuple-element.46), channel_id=1, source_target_pairs={{0,12},{1,29},{2,14},{3,31},{4,8},{5,25},{6,10},{7,27},{8,20},{9,5... | collective-permute-start | bytes 786440 | tf_op jit(solution)/shard_map/ppermute | solution.py:63
  173.7 4.8 %collective-permute-start.14 = (bf16[8,128,128]{2,1,0:T(8,128)(2,1)S(1)}, bf16[8,128,128]{2,1,0:T(8,128)(2,1)S(1)}, u32[]{:S(2)}, u32[]{:S(2)}) collective-permute-start(bf16[8,128,128]{2,1,0:T(8,128)(2,1)S(1)} %get-tuple-element.48), channel_id=1, source_target_pairs={{0,4},{1,17},{2,6},{3,19},{4,0},{5,21},{6,2},{7,23},{8,12},{9,25},... | collective-permute-start | bytes 786440 | tf_op jit(solution)/shard_map/ppermute | solution.py:63
  187.9 4.4 %collective-permute-start.18 = (bf16[8,128,128]{2,1,0:T(8,128)(2,1)S(1)}, bf16[8,128,128]{2,1,0:T(8,128)(2,1)S(1)}, u32[]{:S(2)}, u32[]{:S(2)}) collective-permute-start(bf16[8,128,128]{2,1,0:T(8,128)(2,1)S(1)} %get-tuple-element.27), channel_id=1, source_target_pairs={{0,2},{1,7},{2,4},{3,1},{4,6},{5,3},{6,0},{7,5},{8,10},{9,15},{10,... | collective-permute-start | bytes 786440 | tf_op jit(solution)/shard_map/ppermute | solution.py:63
  196.7 12.0 %collective-permute-start.19 = (bf16[32,128,128]{2,1,0:T(8,128)(2,1)S(1)}, bf16[32,128,128]{2,1,0:T(8,128)(2,1)S(1)}, u32[]{:S(2)}, u32[]{:S(2)}) collective-permute-start(bf16[32,128,128]{2,1,0:T(8,128)(2,1)S(1)} %constant_dynamic-update-slice_fusion.17), channel_id=1, source_target_pairs={{0,1},{1,0},{2,3},{3,2},{4,5},{5,4},{6,7},{7,6},{8,9},{9,8},{10,11... | collective-permute-start | bytes 3145736 | tf_op jit(solution)/shard_map/ppermute | solution.py:54
  218.2 3.7 %fusion.1.base_ref = f32[24,128,128]{2,1,0:T(8,128)} fusion(bf16[24,128,128]{2,1,0:T(8,128)(2,1)S(1)} %copy-done.9, bf16[24,128,128]{2,1,0:T(8,128)(2,1)S(1)} %get-tuple-element.23.own_ref, bf16[24,128,128]{2,1,0:T(8,128)(2,1)S(1)} %copy-done, bf16[24,128,128]{2,1,0:T(8,128)(2,1)} %gather_fusion.7, f32[24]{0:T(128)S(1)} %copy-done.12, ...), kind=kOutput, calls=%fused_computation.60 | convolution fusion | flops 204865536 | bytes 4731072 | tf_op jit(solution)/shard_map/pac,pdc->pad/dot_general | solution.py:26
  224.7 9.6 %finish.3 = (bf16[24,128,128]{2,1,0:T(8,128)(2,1)S(1)}, bf16[48,128,128]{2,1,0:T(8,128)(2,1)}) custom-call(s32[24]{0:T(128)S(1)} %multiply_add_fusion.target_ref.refs_0_, s32[48]{0:T(128)S(1)} %reshape.333.wanted_ref.refs_1_, f32[24]{0:T(128)S(1)} %fusion.51.occupied_ref.refs_2_, f32[24]{0:T(128)S(1)} %copy-done.7, ...), custom_call_target="tpu_custom_call" | custom-call | tf_op jit(solution)/shard_map/finish/pallas_call | solution.py:174
  234.3 11.6 %all-to-all-start.3 = ((bf16[48,128,128]{2,1,0:T(8,128)(2,1)}), bf16[48,128,128]{2,1,0:T(8,128)(2,1)}, u32[]{:S(2)}, u32[]{:S(2)}) async-start(bf16[48,128,128]{2,1,0:T(8,128)(2,1)} %get-tuple-element.28), calls=%async_computation.3 | async-start | bytes 3145728 | tf_op jit(solution)/shard_map/all_to_all | solution.py:222
  256.9 4.8 %collective-permute-start.22 = (bf16[8,128,128]{2,1,0:T(8,128)(2,1)S(1)}, bf16[8,128,128]{2,1,0:T(8,128)(2,1)S(1)}, u32[]{:S(2)}, u32[]{:S(2)}) collective-permute-start(bf16[8,128,128]{2,1,0:T(8,128)(2,1)S(1)} %get-tuple-element.38), channel_id=1, source_target_pairs={{0,12},{1,29},{2,14},{3,31},{4,8},{5,25},{6,10},{7,27},{8,20},{9,5... | collective-permute-start | bytes 786440 | tf_op jit(solution)/shard_map/ppermute | solution.py:63
  265.1 4.8 %collective-permute-start.24 = (bf16[8,128,128]{2,1,0:T(8,128)(2,1)S(1)}, bf16[8,128,128]{2,1,0:T(8,128)(2,1)S(1)}, u32[]{:S(2)}, u32[]{:S(2)}) collective-permute-start(bf16[8,128,128]{2,1,0:T(8,128)(2,1)S(1)} %get-tuple-element.40), channel_id=1, source_target_pairs={{0,4},{1,17},{2,6},{3,19},{4,0},{5,21},{6,2},{7,23},{8,12},{9,25},... | collective-permute-start | bytes 786440 | tf_op jit(solution)/shard_map/ppermute | solution.py:63
  279.3 4.3 %collective-permute-start.28 = (bf16[8,128,128]{2,1,0:T(8,128)(2,1)S(1)}, bf16[8,128,128]{2,1,0:T(8,128)(2,1)S(1)}, u32[]{:S(2)}, u32[]{:S(2)}) collective-permute-start(bf16[8,128,128]{2,1,0:T(8,128)(2,1)S(1)} %get-tuple-element.33), channel_id=1, source_target_pairs={{0,2},{1,7},{2,4},{3,1},{4,6},{5,3},{6,0},{7,5},{8,10},{9,15},{10,... | collective-permute-start | bytes 786440 | tf_op jit(solution)/shard_map/ppermute | solution.py:63
  287.6 12.6 %collective-permute-start.29 = (bf16[32,128,128]{2,1,0:T(8,128)(2,1)S(1)}, bf16[32,128,128]{2,1,0:T(8,128)(2,1)S(1)}, u32[]{:S(2)}, u32[]{:S(2)}) collective-permute-start(bf16[32,128,128]{2,1,0:T(8,128)(2,1)S(1)} %constant_dynamic-update-slice_fusion.34), channel_id=1, source_target_pairs={{0,1},{1,0},{2,3},{3,2},{4,5},{5,4},{6,7},{7,6},{8,9},{9,8},{10,11... | collective-permute-start | bytes 3145736 | tf_op jit(solution)/shard_map/ppermute | solution.py:54
  316.4 9.2 %finish_last.1 = (bf16[24,128,128]{2,1,0:T(8,128)(2,1)}, bf16[24,128,128]{2,1,0:T(8,128)(2,1)}) custom-call(s32[24]{0:T(128)S(1)} %multiply_add_fusion.target_ref.refs_0_, s32[48]{0:T(128)S(1)} %reshape.333.wanted_ref.refs_1_, f32[24]{0:T(128)S(1)} %fusion.51.occupied_ref.refs_2_, f32[24]{0:T(128)S(1)} %copy-done.7, ...), custom_call_target="tpu_custom_call" | custom-call | tf_op jit(solution)/shard_map/finish_last/pallas_call | solution.py:174
  (224 shorter events, 135.5 us)
Async XLA Ops:
  4.5 44.0 %all-to-all-start = ((s32[16,1,3]{2,1,0:T(1,128)}), s32[16,1,3]{2,1,0:T(1,128)S(1)}, u32[]{:S(2)}, u32[]{:S(2)}) async-start(s32[16,1,3]{2,1,0:T(1,128)} %bitcast.3), calls=%async_computation | async-start | bytes 16384 | tf_op jit(solution)/shard_map/all_to_all | solution.py:207
  43.2 21.2 %collective-permute-start = (bf16[32,128,128]{2,1,0:T(8,128)(2,1)}, bf16[32,128,128]{2,1,0:T(8,128)(2,1)}, u32[]{:S(2)}, u32[]{:S(2)}) collective-permute-start(bf16[32,128,128]{2,1,0:T(8,128)(2,1)} %gather_fusion.3), channel_id=1, source_target_pairs={{0,1},{1,0},{2,3},{3,2},{4,5},{5,4},{6,7},{7,6},{8,9},{9,8},{10,11... | collective-permute-start | bytes 3145736 | tf_op jit(solution)/shard_map/ppermute | solution.py:54
  50.6 81.6 %all-to-all-start.1 = ((bf16[48,128,128]{2,1,0:T(8,128)(2,1)}), bf16[48,128,128]{2,1,0:T(8,128)(2,1)}, u32[]{:S(2)}, u32[]{:S(2)}) async-start(bf16[48,128,128]{2,1,0:T(8,128)(2,1)} %gather_fusion), calls=%async_computation.1 | async-start | bytes 3145728 | tf_op jit(solution)/shard_map/all_to_all | solution.py:222
  65.9 15.7 %collective-permute-start.1 = (bf16[8,128,128]{2,1,0:T(8,128)(2,1)S(1)}, bf16[8,128,128]{2,1,0:T(8,128)(2,1)S(1)}, u32[]{:S(2)}, u32[]{:S(2)}) collective-permute-start(bf16[8,128,128]{2,1,0:T(8,128)(2,1)S(1)} %get-tuple-element.53), channel_id=1, source_target_pairs={{0,18},{1,23},{2,20},{3,17},{4,22},{5,19},{6,16},{7,21},{8,26},{9,... | collective-permute-start | bytes 786440 | tf_op jit(solution)/shard_map/ppermute | solution.py:63
  68.4 16.2 %collective-permute-start.2 = (bf16[8,128,128]{2,1,0:T(8,128)(2,1)S(1)}, bf16[8,128,128]{2,1,0:T(8,128)(2,1)S(1)}, u32[]{:S(2)}, u32[]{:S(2)}) collective-permute-start(bf16[8,128,128]{2,1,0:T(8,128)(2,1)S(1)} %get-tuple-element.54), channel_id=1, source_target_pairs={{0,12},{1,29},{2,14},{3,31},{4,8},{5,25},{6,10},{7,27},{8,20},{9,5... | collective-permute-start | bytes 786440 | tf_op jit(solution)/shard_map/ppermute | solution.py:63
  73.2 14.6 %collective-permute-start.3 = (bf16[8,128,128]{2,1,0:T(8,128)(2,1)S(1)}, bf16[8,128,128]{2,1,0:T(8,128)(2,1)S(1)}, u32[]{:S(2)}, u32[]{:S(2)}) collective-permute-start(bf16[8,128,128]{2,1,0:T(8,128)(2,1)S(1)} %get-tuple-element.55), channel_id=1, source_target_pairs={{0,0},{1,21},{2,2},{3,23},{4,4},{5,17},{6,6},{7,19},{8,8},{9,29},{... | collective-permute-start | bytes 786440 | tf_op jit(solution)/shard_map/ppermute | solution.py:63
  76.6 14.1 %collective-permute-start.4 = (bf16[8,128,128]{2,1,0:T(8,128)(2,1)S(1)}, bf16[8,128,128]{2,1,0:T(8,128)(2,1)S(1)}, u32[]{:S(2)}, u32[]{:S(2)}) collective-permute-start(bf16[8,128,128]{2,1,0:T(8,128)(2,1)S(1)} %get-tuple-element.56), channel_id=1, source_target_pairs={{0,4},{1,17},{2,6},{3,19},{4,0},{5,21},{6,2},{7,23},{8,12},{9,25},... | collective-permute-start | bytes 786440 | tf_op jit(solution)/shard_map/ppermute | solution.py:63
  81.7 16.4 %collective-permute-start.5 = (bf16[8,128,128]{2,1,0:T(8,128)(2,1)S(1)}, bf16[8,128,128]{2,1,0:T(8,128)(2,1)S(1)}, u32[]{:S(2)}, u32[]{:S(2)}) collective-permute-start(bf16[8,128,128]{2,1,0:T(8,128)(2,1)S(1)} %get-tuple-element.18), channel_id=1, source_target_pairs={{0,10},{1,31},{2,12},{3,25},{4,14},{5,27},{6,8},{7,29},{8,18},{9,7... | collective-permute-start | bytes 786440 | tf_op jit(solution)/shard_map/ppermute | solution.py:63
  84.6 13.5 %collective-permute-start.6 = (bf16[8,128,128]{2,1,0:T(8,128)(2,1)S(1)}, bf16[8,128,128]{2,1,0:T(8,128)(2,1)S(1)}, u32[]{:S(2)}, u32[]{:S(2)}) collective-permute-start(bf16[8,128,128]{2,1,0:T(8,128)(2,1)S(1)} %get-tuple-element.19), channel_id=1, source_target_pairs={{0,14},{1,27},{2,8},{3,29},{4,10},{5,31},{6,12},{7,25},{8,22},{9,3... | collective-permute-start | bytes 786440 | tf_op jit(solution)/shard_map/ppermute | solution.py:63
  100.8 18.0 %collective-permute-start.9 = (bf16[32,128,128]{2,1,0:T(8,128)(2,1)}, bf16[32,128,128]{2,1,0:T(8,128)(2,1)}, u32[]{:S(2)}, u32[]{:S(2)}) collective-permute-start(bf16[32,128,128]{2,1,0:T(8,128)(2,1)} %constant_dynamic-update-slice_fusion), channel_id=1, source_target_pairs={{0,1},{1,0},{2,3},{3,2},{4,5},{5,4},{6,7},{7,6},{8,9},{9,8},{10,11... | collective-permute-start | bytes 3145736 | tf_op jit(solution)/shard_map/ppermute | solution.py:54
  143.3 80.0 %all-to-all-start.2 = ((bf16[48,128,128]{2,1,0:T(8,128)(2,1)}), bf16[48,128,128]{2,1,0:T(8,128)(2,1)}, u32[]{:S(2)}, u32[]{:S(2)}) async-start(bf16[48,128,128]{2,1,0:T(8,128)(2,1)} %get-tuple-element.22), calls=%async_computation.2 | async-start | bytes 3145728 | tf_op jit(solution)/shard_map/all_to_all | solution.py:222
  163.0 15.5 %collective-permute-start.11 = (bf16[8,128,128]{2,1,0:T(8,128)(2,1)S(1)}, bf16[8,128,128]{2,1,0:T(8,128)(2,1)S(1)}, u32[]{:S(2)}, u32[]{:S(2)}) collective-permute-start(bf16[8,128,128]{2,1,0:T(8,128)(2,1)S(1)} %get-tuple-element.45), channel_id=1, source_target_pairs={{0,18},{1,23},{2,20},{3,17},{4,22},{5,19},{6,16},{7,21},{8,26},{9,... | collective-permute-start | bytes 786440 | tf_op jit(solution)/shard_map/ppermute | solution.py:63
  165.5 16.0 %collective-permute-start.12 = (bf16[8,128,128]{2,1,0:T(8,128)(2,1)S(1)}, bf16[8,128,128]{2,1,0:T(8,128)(2,1)S(1)}, u32[]{:S(2)}, u32[]{:S(2)}) collective-permute-start(bf16[8,128,128]{2,1,0:T(8,128)(2,1)S(1)} %get-tuple-element.46), channel_id=1, source_target_pairs={{0,12},{1,29},{2,14},{3,31},{4,8},{5,25},{6,10},{7,27},{8,20},{9,5... | collective-permute-start | bytes 786440 | tf_op jit(solution)/shard_map/ppermute | solution.py:63
  170.3 14.7 %collective-permute-start.13 = (bf16[8,128,128]{2,1,0:T(8,128)(2,1)S(1)}, bf16[8,128,128]{2,1,0:T(8,128)(2,1)S(1)}, u32[]{:S(2)}, u32[]{:S(2)}) collective-permute-start(bf16[8,128,128]{2,1,0:T(8,128)(2,1)S(1)} %get-tuple-element.47), channel_id=1, source_target_pairs={{0,0},{1,21},{2,2},{3,23},{4,4},{5,17},{6,6},{7,19},{8,8},{9,29},{... | collective-permute-start | bytes 786440 | tf_op jit(solution)/shard_map/ppermute | solution.py:63
  173.7 14.2 %collective-permute-start.14 = (bf16[8,128,128]{2,1,0:T(8,128)(2,1)S(1)}, bf16[8,128,128]{2,1,0:T(8,128)(2,1)S(1)}, u32[]{:S(2)}, u32[]{:S(2)}) collective-permute-start(bf16[8,128,128]{2,1,0:T(8,128)(2,1)S(1)} %get-tuple-element.48), channel_id=1, source_target_pairs={{0,4},{1,17},{2,6},{3,19},{4,0},{5,21},{6,2},{7,23},{8,12},{9,25},... | collective-permute-start | bytes 786440 | tf_op jit(solution)/shard_map/ppermute | solution.py:63
  178.6 14.0 %collective-permute-start.15 = (bf16[8,128,128]{2,1,0:T(8,128)(2,1)S(1)}, bf16[8,128,128]{2,1,0:T(8,128)(2,1)S(1)}, u32[]{:S(2)}, u32[]{:S(2)}) collective-permute-start(bf16[8,128,128]{2,1,0:T(8,128)(2,1)S(1)} %get-tuple-element.24), channel_id=1, source_target_pairs={{0,10},{1,31},{2,12},{3,25},{4,14},{5,27},{6,8},{7,29},{8,18},{9,7... | collective-permute-start | bytes 786440 | tf_op jit(solution)/shard_map/ppermute | solution.py:63
  196.7 17.3 %collective-permute-start.19 = (bf16[32,128,128]{2,1,0:T(8,128)(2,1)S(1)}, bf16[32,128,128]{2,1,0:T(8,128)(2,1)S(1)}, u32[]{:S(2)}, u32[]{:S(2)}) collective-permute-start(bf16[32,128,128]{2,1,0:T(8,128)(2,1)S(1)} %constant_dynamic-update-slice_fusion.17), channel_id=1, source_target_pairs={{0,1},{1,0},{2,3},{3,2},{4,5},{5,4},{6,7},{7,6},{8,9},{9,8},{10,11... | collective-permute-start | bytes 3145736 | tf_op jit(solution)/shard_map/ppermute | solution.py:54
  234.3 80.7 %all-to-all-start.3 = ((bf16[48,128,128]{2,1,0:T(8,128)(2,1)}), bf16[48,128,128]{2,1,0:T(8,128)(2,1)}, u32[]{:S(2)}, u32[]{:S(2)}) async-start(bf16[48,128,128]{2,1,0:T(8,128)(2,1)} %get-tuple-element.28), calls=%async_computation.3 | async-start | bytes 3145728 | tf_op jit(solution)/shard_map/all_to_all | solution.py:222
  254.4 15.5 %collective-permute-start.21 = (bf16[8,128,128]{2,1,0:T(8,128)(2,1)S(1)}, bf16[8,128,128]{2,1,0:T(8,128)(2,1)S(1)}, u32[]{:S(2)}, u32[]{:S(2)}) collective-permute-start(bf16[8,128,128]{2,1,0:T(8,128)(2,1)S(1)} %get-tuple-element.37), channel_id=1, source_target_pairs={{0,18},{1,23},{2,20},{3,17},{4,22},{5,19},{6,16},{7,21},{8,26},{9,... | collective-permute-start | bytes 786440 | tf_op jit(solution)/shard_map/ppermute | solution.py:63
  256.9 16.0 %collective-permute-start.22 = (bf16[8,128,128]{2,1,0:T(8,128)(2,1)S(1)}, bf16[8,128,128]{2,1,0:T(8,128)(2,1)S(1)}, u32[]{:S(2)}, u32[]{:S(2)}) collective-permute-start(bf16[8,128,128]{2,1,0:T(8,128)(2,1)S(1)} %get-tuple-element.38), channel_id=1, source_target_pairs={{0,12},{1,29},{2,14},{3,31},{4,8},{5,25},{6,10},{7,27},{8,20},{9,5... | collective-permute-start | bytes 786440 | tf_op jit(solution)/shard_map/ppermute | solution.py:63
  261.7 14.7 %collective-permute-start.23 = (bf16[8,128,128]{2,1,0:T(8,128)(2,1)S(1)}, bf16[8,128,128]{2,1,0:T(8,128)(2,1)S(1)}, u32[]{:S(2)}, u32[]{:S(2)}) collective-permute-start(bf16[8,128,128]{2,1,0:T(8,128)(2,1)S(1)} %get-tuple-element.39), channel_id=1, source_target_pairs={{0,0},{1,21},{2,2},{3,23},{4,4},{5,17},{6,6},{7,19},{8,8},{9,29},{... | collective-permute-start | bytes 786440 | tf_op jit(solution)/shard_map/ppermute | solution.py:63
  265.1 14.2 %collective-permute-start.24 = (bf16[8,128,128]{2,1,0:T(8,128)(2,1)S(1)}, bf16[8,128,128]{2,1,0:T(8,128)(2,1)S(1)}, u32[]{:S(2)}, u32[]{:S(2)}) collective-permute-start(bf16[8,128,128]{2,1,0:T(8,128)(2,1)S(1)} %get-tuple-element.40), channel_id=1, source_target_pairs={{0,4},{1,17},{2,6},{3,19},{4,0},{5,21},{6,2},{7,23},{8,12},{9,25},... | collective-permute-start | bytes 786440 | tf_op jit(solution)/shard_map/ppermute | solution.py:63
  270.0 13.9 %collective-permute-start.25 = (bf16[8,128,128]{2,1,0:T(8,128)(2,1)S(1)}, bf16[8,128,128]{2,1,0:T(8,128)(2,1)S(1)}, u32[]{:S(2)}, u32[]{:S(2)}) collective-permute-start(bf16[8,128,128]{2,1,0:T(8,128)(2,1)S(1)} %get-tuple-element.30), channel_id=1, source_target_pairs={{0,10},{1,31},{2,12},{3,25},{4,14},{5,27},{6,8},{7,29},{8,18},{9,7... | collective-permute-start | bytes 786440 | tf_op jit(solution)/shard_map/ppermute | solution.py:63
  287.6 17.9 %collective-permute-start.29 = (bf16[32,128,128]{2,1,0:T(8,128)(2,1)S(1)}, bf16[32,128,128]{2,1,0:T(8,128)(2,1)S(1)}, u32[]{:S(2)}, u32[]{:S(2)}) collective-permute-start(bf16[32,128,128]{2,1,0:T(8,128)(2,1)S(1)} %constant_dynamic-update-slice_fusion.34), channel_id=1, source_target_pairs={{0,1},{1,0},{2,3},{3,2},{4,5},{5,4},{6,7},{7,6},{8,9},{9,8},{10,11... | collective-permute-start | bytes 3145736 | tf_op jit(solution)/shard_map/ppermute | solution.py:54
  (27 other events, 388.0 us)

commit v4 on v3

--- a/solution.py
+++ b/solution.py
@@ -6,6 +6,7 @@
 from jax.sharding import PartitionSpec as P
 
 ITERS = 3
+GROUP = 8
 LANES = 4
 STEPS = (
     ((2, 1), (2, 3)),
@@ -26,18 +27,16 @@
     return jnp.einsum("pac,pdc->pad", first, intersection, preferred_element_type=jnp.float32)
 
 
-def layout(peer, slot, peer_count, capacity):
-    marker = (peer[:, None] == jnp.arange(peer_count, dtype=jnp.int32)[None, :]).astype(jnp.int32)
-    before = jnp.sum((jnp.cumsum(marker, axis=0) - marker) * marker, axis=1)
-    target = peer * capacity + before
-    slot_table = jnp.zeros((peer_count * capacity,), jnp.int32).at[target].set(slot)
-    return (target, slot_table.reshape(peer_count, capacity))
-
-
 def ranks(peer):
     order = jnp.arange(peer.shape[0], dtype=jnp.int32)
     earlier = (peer[:, None] == peer[None, :]) & (order[None, :] < order[:, None])
     return jnp.sum(earlier.astype(jnp.int32), axis=1)
+
+
+def request_table(peer, slot, rank, peer_count, capacity):
+    place = jnp.arange(peer_count * capacity, dtype=jnp.int32)
+    hit = (peer * capacity + rank)[None, :] == place[:, None]
+    return jnp.sum(jnp.where(hit, slot[None, :], 0), axis=1).reshape(peer_count, capacity)
 
 
 def row_requests(row_peer, row_slot, me, capacity):
@@ -104,56 +103,104 @@
     wanted_ref,
     occupied_ref,
     fock_ref,
+    energy_ref,
+    energy_t_ref,
     fetched_ref,
     inter_ref,
     base_ref,
     own_ref,
-    energy_ref,
-    energy_t_ref,
     new_ref,
     second_ref,
-    block_ref,
+    block_scr,
+    inter_scr,
+    base_scr,
+    own_scr,
+    new_scr,
+    second_scr,
     in_sem,
+    group_sem,
     out_sem,
+    send_sem,
 ):
-    pairs = own_ref.shape[0]
-    arrivals = []
-    for pair in range(pairs):
-        arrivals.append(
+    pairs = own_scr.shape[0]
+    last = send_sem is None
+    groups = [(start, min(GROUP, pairs - start)) for start in range(0, pairs, GROUP)]
+    waits = []
+    for number, (start, size) in enumerate(groups):
+        copies = [
             pltpu.make_async_copy(
-                fetched_ref.at[target_ref[pair]], block_ref.at[pair], in_sem.at[pair]
-            )
-        )
-        arrivals[-1].start()
-    for pair in range(pairs):
-        inter = inter_ref[pair]
-        arrivals[pair].wait()
-        first = jnp.dot(inter, block_ref[pair], preferred_element_type=jnp.float32)
-        term = lax.dot_general(
-            first.astype(jnp.bfloat16),
-            inter,
-            (((1,), (1,)), ((), ())),
-            preferred_element_type=jnp.float32,
-        )
-        denominator = (
-            energy_t_ref[:, pair : pair + 1] + energy_ref[pair : pair + 1, :] - occupied_ref[pair]
-        )
-        residual = base_ref[pair] - fock_ref[pair] * term
-        new = own_ref[pair].astype(jnp.float32) - residual / denominator
-        new_ref[pair] = new.astype(jnp.bfloat16)
-        if out_sem is None:
-            second_ref[pair] = residual.astype(jnp.bfloat16)
-    if out_sem is not None:
-        sends = []
+                source.at[pl.ds(start, size)],
+                buffer.at[pl.ds(start, size)],
+                group_sem.at[kind, number],
+            )
+            for kind, (source, buffer) in enumerate(
+                ((inter_ref, inter_scr), (own_ref, own_scr), (base_ref, base_scr))
+            )
+        ]
+        for pair in range(start, start + size):
+            copies.append(
+                pltpu.make_async_copy(
+                    fetched_ref.at[target_ref[pair]], block_scr.at[pair], in_sem.at[pair]
+                )
+            )
+        for copy in copies:
+            copy.start()
+        waits.append(copies)
+    leaving = []
+    for number, (start, size) in enumerate(groups):
+        for copy in waits[number]:
+            copy.wait()
+        group = range(start, start + size)
+        firsts = [
+            jnp.dot(inter_scr[pair], block_scr[pair], preferred_element_type=jnp.float32).astype(
+                jnp.bfloat16
+            )
+            for pair in group
+        ]
+        terms = [
+            lax.dot_general(
+                first,
+                inter_scr[pair],
+                (((1,), (1,)), ((), ())),
+                preferred_element_type=jnp.float32,
+            )
+            for pair, first in zip(group, firsts)
+        ]
+        for pair, term in zip(group, terms):
+            denominator = (
+                energy_t_ref[:, pair : pair + 1]
+                + energy_ref[pair : pair + 1, :]
+                - occupied_ref[pair]
+            )
+            residual = base_scr[pair] - fock_ref[pair] * term
+            new = own_scr[pair].astype(jnp.float32) - residual / denominator
+            new_scr[pair] = new.astype(jnp.bfloat16)
+            if last:
+                second_scr[pair] = residual.astype(jnp.bfloat16)
+        results = [(new_scr, new_ref)] + ([(second_scr, second_ref)] if last else [])
+        for kind, (buffer, out) in enumerate(results):
+            leaving.append(
+                pltpu.make_async_copy(
+                    buffer.at[pl.ds(start, size)],
+                    out.at[pl.ds(start, size)],
+                    out_sem.at[kind, number],
+                )
+            )
+            leaving[-1].start()
+    if not last:
         for place in range(second_ref.shape[0]):
-            sends.append(
+            leaving.append(
                 pltpu.make_async_copy(
-                    new_ref.at[wanted_ref[place]], second_ref.at[place], out_sem.at[place]
+                    new_scr.at[wanted_ref[place]], second_ref.at[place], send_sem.at[place]
                 )
             )
-            sends[-1].start()
-        for send in sends:
-            send.wait()
+            leaving[-1].start()
+    for copy in leaving:
+        copy.wait()
+
+
+def middle_kernel(*refs):
+    finish_kernel(*refs[:17], None, *refs[17:])
 
 
 def last_kernel(*refs):
@@ -162,27 +209,31 @@
 
 def finish(target, wanted, occupied, fock, fetched, inter, base, own, energy, last):
     pairs = own.shape[0]
+    count = -(-pairs // GROUP)
     smem, vmem = pl.BlockSpec(memory_space=pltpu.SMEM), pl.BlockSpec(memory_space=pltpu.VMEM)
     hbm = pl.BlockSpec(memory_space=pltpu.HBM)
-    scratch = [pltpu.VMEM(own.shape, jnp.bfloat16), pltpu.SemaphoreType.DMA((pairs,))]
+    narrow = pltpu.VMEM(own.shape, jnp.bfloat16)
+    scratch = [narrow, narrow, pltpu.VMEM(own.shape, jnp.float32), narrow, narrow]
+    if last:
+        scratch.append(narrow)
+    scratch += [
+        pltpu.SemaphoreType.DMA((pairs,)),
+        pltpu.SemaphoreType.DMA((3, count)),
+        pltpu.SemaphoreType.DMA((2, count)),
+    ]
     if not last:
         scratch.append(pltpu.SemaphoreType.DMA((fetched.shape[0],)))
-    if last:
-        second_shape = jax.ShapeDtypeStruct(own.shape, jnp.bfloat16)
-    else:
-        second_shape = pltpu.HBM(fetched.shape, jnp.bfloat16)
     return pl.pallas_call(
-        last_kernel if last else finish_kernel,
+        last_kernel if last else middle_kernel,
         out_shape=(
-            jax.ShapeDtypeStruct(own.shape, jnp.bfloat16),
-            second_shape,
+            pltpu.HBM(own.shape, jnp.bfloat16),
+            pltpu.HBM(own.shape if last else fetched.shape, jnp.bfloat16),
         ),
-        in_specs=[smem] * 4 + [hbm] + [vmem] * 5,
-        out_specs=(vmem, vmem if last else hbm),
+        in_specs=[smem] * 4 + [vmem] * 2 + [hbm] * 4,
+        out_specs=(hbm, hbm),
         scratch_shapes=scratch,
-        compiler_params=pltpu.CompilerParams(vmem_limit_bytes=24 * 2**20),
         name="finish_last" if last else "finish",
-    )(target, wanted, occupied, fock, fetched, inter, base, own, energy, energy.T)
+    )(target, wanted, occupied, fock, energy, energy.T, fetched, inter, base, own)
 
 
 def body(
@@ -203,7 +254,9 @@
     width = amplitudes.shape[1]
     row_capacity, col_capacity = 2, 3
     me = lax.axis_index("oj")
-    col_target, col_table = layout(col_peer[:, 0], col_slot, lax.axis_size("oi"), col_capacity)
+    col_rank = ranks(col_peer[:, 0])
+    col_target = col_peer[:, 0] * col_capacity + col_rank
+    col_table = request_table(col_peer[:, 0], col_slot, col_rank, lax.axis_size("oi"), col_capacity)
     col_wanted = lax.all_to_all(col_table, "oi", split_axis=0, concat_axis=0, tiled=True)
     row_wanted = row_requests(row_peer[:, 0], row_slot, me, row_capacity)
     near_wanted, far_wanted, row_target = row_plan(

time: 331 us -> 315 us (0.952)
  Pallas kernels: 28.4 us -> 16.5 us
  local copies, waits for them, and re-layouts: 56.9 us -> 53 us
    pallas_call x3, Pallas kernels: 28.4 us -> 16.5 us  [finish(): pl.pallas_call(last_kernel if last else middle_kernel, out_shape=(pltpu.H...]
    unnamed x85 -> x91, local copies, waits for them, and re-layouts: 26.7 us -> 24.7 us
  transfers between devices with their start and end apart: 34 -> 34, of which waited for: 12 -> 11; matrix products, arithmetic and copies ran while one was open for 22% -> 23% of each run, Pallas kernels for 0% -> 0%
where the time goes in v4:
time: 315 us; the launch traced here: 310 us
  starting transfers between devices  178 us (57%)
  local copies, waits for them, and re-layouts  53 us (17%)
  waiting for transfers between devices  23.3 us (7%)
  Pallas kernels  16.5 us (5%)
  blocking collectives  14.5 us (5%)
  other arithmetic  13.1 us (4%)
  matrix products  8.45 us (3%)
    ppermute x24, starting transfers between devices, chip_exchange(): return lax.ppermute(blocks, 'oj', pairs)  85.1 us
    ppermute x6, starting transfers between devices, core_exchange(): lax.ppermute(blocks, 'oj', [(source, source ^ 1) for source in range(32)])  42.8 us
    all_to_all x3, starting transfers between devices, body(): lax.all_to_all(col_send, 'oi', split_axis=0, concat_axis=0, tiled=True)  34.6 us
    unnamed x91, local copies, waits for them, and re-layouts  24.7 us
    pallas_call x3, Pallas kernels, finish(): pl.pallas_call(last_kernel if last else middle_kernel, out_shape=(pltpu.H...  16.5 us
    all_to_all x1, starting transfers between devices, body(): lax.all_to_all(col_table, 'oi', split_axis=0, concat_axis=0, tiled=True)  15.7 us
    unnamed x1, blocking collectives  14.5 us
    ppermute x24, waiting for transfers between devices, chip_exchange(): return lax.ppermute(blocks, 'oj', pairs)  10.3 us
  transfers between devices with their start and end apart: 34, of which 11 were waited for; matrix products, arithmetic and copies ran while one was open for 23% of the time, Pallas kernels for 0%

profile of v4, /device:TPU:1, one launch (start us, length us, event | category | flops | bytes accessed | tf_op | source)
XLA Modules:
  0.0 309.7 jit_solution(8598005955607493219)
XLA Ops:
  4.3 15.7 %all-to-all-start = ((s32[16,1,3]{2,1,0:T(1,128)}), s32[16,1,3]{2,1,0:T(1,128)S(1)}, u32[]{:S(2)}, u32[]{:S(2)}) async-start(s32[16,1,3]{2,1,0:T(1,128)} %bitcast.1), calls=%async_computation | async-start | bytes 16384 | tf_op jit(solution)/shard_map/all_to_all | solution.py:260
  22.8 14.5 %all-reduce = s32[768]{0:T(1024)S(1)} all-reduce(s32[768]{0:T(1024)S(1)} %get-tuple-element.113), channel_id=2, replica_groups=mesh['oi'=16,'oj'=32] {'oj'}, use_global_device_ids=true, to_apply=%add | all-reduce | flops 768 | bytes 6144
  43.1 5.3 %collective-permute-start = (bf16[32,128,128]{2,1,0:T(8,128)(2,1)}, bf16[32,128,128]{2,1,0:T(8,128)(2,1)}, u32[]{:S(2)}, u32[]{:S(2)}) collective-permute-start(bf16[32,128,128]{2,1,0:T(8,128)(2,1)} %gather_fusion.3), channel_id=1, source_target_pairs={{0,1},{1,0},{2,3},{3,2},{4,5},{5,4},{6,7},{7,6},{8,9},{9,8},{10,11... | collective-permute-start | bytes 3145736 | tf_op jit(solution)/shard_map/ppermute | solution.py:53
  50.5 11.9 %all-to-all-start.1 = ((bf16[48,128,128]{2,1,0:T(8,128)(2,1)}), bf16[48,128,128]{2,1,0:T(8,128)(2,1)}, u32[]{:S(2)}, u32[]{:S(2)}) async-start(bf16[48,128,128]{2,1,0:T(8,128)(2,1)} %gather_fusion), calls=%async_computation.1 | async-start | bytes 3145728 | tf_op jit(solution)/shard_map/all_to_all | solution.py:275
  68.2 4.8 %collective-permute-start.2 = (bf16[8,128,128]{2,1,0:T(8,128)(2,1)S(1)}, bf16[8,128,128]{2,1,0:T(8,128)(2,1)S(1)}, u32[]{:S(2)}, u32[]{:S(2)}) collective-permute-start(bf16[8,128,128]{2,1,0:T(8,128)(2,1)S(1)} %get-tuple-element.54), channel_id=1, source_target_pairs={{0,12},{1,29},{2,14},{3,31},{4,8},{5,25},{6,10},{7,27},{8,20},{9,5... | collective-permute-start | bytes 786440 | tf_op jit(solution)/shard_map/ppermute | solution.py:62
  76.4 4.8 %collective-permute-start.4 = (bf16[8,128,128]{2,1,0:T(8,128)(2,1)S(1)}, bf16[8,128,128]{2,1,0:T(8,128)(2,1)S(1)}, u32[]{:S(2)}, u32[]{:S(2)}) collective-permute-start(bf16[8,128,128]{2,1,0:T(8,128)(2,1)S(1)} %get-tuple-element.56), channel_id=1, source_target_pairs={{0,4},{1,17},{2,6},{3,19},{4,0},{5,21},{6,2},{7,23},{8,12},{9,25},... | collective-permute-start | bytes 786440 | tf_op jit(solution)/shard_map/ppermute | solution.py:62
  90.5 4.6 %collective-permute-start.8 = (bf16[8,128,128]{2,1,0:T(8,128)(2,1)S(1)}, bf16[8,128,128]{2,1,0:T(8,128)(2,1)S(1)}, u32[]{:S(2)}, u32[]{:S(2)}) collective-permute-start(bf16[8,128,128]{2,1,0:T(8,128)(2,1)S(1)} %get-tuple-element.21), channel_id=1, source_target_pairs={{0,2},{1,7},{2,4},{3,1},{4,6},{5,3},{6,0},{7,5},{8,10},{9,15},{10,... | collective-permute-start | bytes 786440 | tf_op jit(solution)/shard_map/ppermute | solution.py:62
  101.3 11.0 %collective-permute-start.9 = (bf16[32,128,128]{2,1,0:T(8,128)(2,1)}, bf16[32,128,128]{2,1,0:T(8,128)(2,1)S(1)}, u32[]{:S(2)}, u32[]{:S(2)}) collective-permute-start(bf16[32,128,128]{2,1,0:T(8,128)(2,1)} %constant_dynamic-update-slice_fusion), channel_id=1, source_target_pairs={{0,1},{1,0},{2,3},{3,2},{4,5},{5,4},{6,7},{7,6},{8,9},{9,8},{10,11... | collective-permute-start | bytes 3145736 | tf_op jit(solution)/shard_map/ppermute | solution.py:53
  132.2 5.8 %finish.2 = (bf16[24,128,128]{2,1,0:T(8,128)(2,1)}, bf16[48,128,128]{2,1,0:T(8,128)(2,1)}) custom-call(s32[24]{0:T(128)} %copy-done.16, s32[48]{0:T(128)} %reshape.342.refs_1_, f32[24]{0:T(128)} %copy-done.10, f32[24]{0:T(128)} %refs_3_.5, f32[24,128]{1,0:T(8,128)} %refs_4_.5, f32[128,24]{1,0:T(8,128)} %bitcast.250, ...), custom_call_target="tpu_custom_call" | custom-call | tf_op jit(solution)/shard_map/finish/pallas_call | solution.py:226
  138.0 11.0 %all-to-all-start.2 = ((bf16[48,128,128]{2,1,0:T(8,128)(2,1)}), bf16[48,128,128]{2,1,0:T(8,128)(2,1)}, u32[]{:S(2)}, u32[]{:S(2)}) async-start(bf16[48,128,128]{2,1,0:T(8,128)(2,1)} %get-tuple-element.22), calls=%async_computation.2 | async-start | bytes 3145728 | tf_op jit(solution)/shard_map/all_to_all | solution.py:275
  160.1 4.8 %collective-permute-start.12 = (bf16[8,128,128]{2,1,0:T(8,128)(2,1)S(1)}, bf16[8,128,128]{2,1,0:T(8,128)(2,1)S(1)}, u32[]{:S(2)}, u32[]{:S(2)}) collective-permute-start(bf16[8,128,128]{2,1,0:T(8,128)(2,1)S(1)} %get-tuple-element.46), channel_id=1, source_target_pairs={{0,12},{1,29},{2,14},{3,31},{4,8},{5,25},{6,10},{7,27},{8,20},{9,5... | collective-permute-start | bytes 786440 | tf_op jit(solution)/shard_map/ppermute | solution.py:62
  164.9 3.4 %collective-permute-start.13 = (bf16[8,128,128]{2,1,0:T(8,128)(2,1)S(1)}, bf16[8,128,128]{2,1,0:T(8,128)(2,1)S(1)}, u32[]{:S(2)}, u32[]{:S(2)}) collective-permute-start(bf16[8,128,128]{2,1,0:T(8,128)(2,1)S(1)} %get-tuple-element.47), channel_id=1, source_target_pairs={{0,0},{1,21},{2,2},{3,23},{4,4},{5,17},{6,6},{7,19},{8,8},{9,29},{... | collective-permute-start | bytes 786440 | tf_op jit(solution)/shard_map/ppermute | solution.py:62
  168.3 4.8 %collective-permute-start.14 = (bf16[8,128,128]{2,1,0:T(8,128)(2,1)S(1)}, bf16[8,128,128]{2,1,0:T(8,128)(2,1)S(1)}, u32[]{:S(2)}, u32[]{:S(2)}) collective-permute-start(bf16[8,128,128]{2,1,0:T(8,128)(2,1)S(1)} %get-tuple-element.48), channel_id=1, source_target_pairs={{0,4},{1,17},{2,6},{3,19},{4,0},{5,21},{6,2},{7,23},{8,12},{9,25},... | collective-permute-start | bytes 786440 | tf_op jit(solution)/shard_map/ppermute | solution.py:62
  182.5 4.4 %collective-permute-start.18 = (bf16[8,128,128]{2,1,0:T(8,128)(2,1)S(1)}, bf16[8,128,128]{2,1,0:T(8,128)(2,1)S(1)}, u32[]{:S(2)}, u32[]{:S(2)}) collective-permute-start(bf16[8,128,128]{2,1,0:T(8,128)(2,1)S(1)} %get-tuple-element.27), channel_id=1, source_target_pairs={{0,2},{1,7},{2,4},{3,1},{4,6},{5,3},{6,0},{7,5},{8,10},{9,15},{10,... | collective-permute-start | bytes 786440 | tf_op jit(solution)/shard_map/ppermute | solution.py:62
  191.2 9.5 %collective-permute-start.19 = (bf16[32,128,128]{2,1,0:T(8,128)(2,1)S(1)}, bf16[32,128,128]{2,1,0:T(8,128)(2,1)S(1)}, u32[]{:S(2)}, u32[]{:S(2)}) collective-permute-start(bf16[32,128,128]{2,1,0:T(8,128)(2,1)S(1)} %constant_dynamic-update-slice_fusion.17), channel_id=1, source_target_pairs={{0,1},{1,0},{2,3},{3,2},{4,5},{5,4},{6,7},{7,6},{8,9},{9,8},{10,11... | collective-permute-start | bytes 3145736 | tf_op jit(solution)/shard_map/ppermute | solution.py:53
  212.1 5.9 %all-to-all-done.2.refs_6_ = bf16[48,128,128]{2,1,0:T(8,128)(2,1)} async-done(((bf16[48,128,128]{2,1,0:T(8,128)(2,1)}), bf16[48,128,128]{2,1,0:T(8,128)(2,1)}, u32[]{:S(2)}, u32[]{:S(2)}) %all-to-all-start.2) | async-done | bytes 1572896 | tf_op jit(solution)/shard_map/all_to_all | solution.py:275
  218.0 5.9 %finish.3 = (bf16[24,128,128]{2,1,0:T(8,128)(2,1)}, bf16[48,128,128]{2,1,0:T(8,128)(2,1)}) custom-call(s32[24]{0:T(128)} %copy-done.16, s32[48]{0:T(128)} %reshape.342.refs_1_, f32[24]{0:T(128)} %copy-done.10, f32[24]{0:T(128)} %refs_3_.5, f32[24,128]{1,0:T(8,128)} %refs_4_.5, f32[128,24]{1,0:T(8,128)} %bitcast.251, ...), custom_call_target="tpu_custom_call" | custom-call | tf_op jit(solution)/shard_map/finish/pallas_call | solution.py:226
  223.9 11.7 %all-to-all-start.3 = ((bf16[48,128,128]{2,1,0:T(8,128)(2,1)}), bf16[48,128,128]{2,1,0:T(8,128)(2,1)}, u32[]{:S(2)}, u32[]{:S(2)}) async-start(bf16[48,128,128]{2,1,0:T(8,128)(2,1)} %get-tuple-element.28), calls=%async_computation.3 | async-start | bytes 3145728 | tf_op jit(solution)/shard_map/all_to_all | solution.py:275
  246.7 4.8 %collective-permute-start.22 = (bf16[8,128,128]{2,1,0:T(8,128)(2,1)S(1)}, bf16[8,128,128]{2,1,0:T(8,128)(2,1)S(1)}, u32[]{:S(2)}, u32[]{:S(2)}) collective-permute-start(bf16[8,128,128]{2,1,0:T(8,128)(2,1)S(1)} %get-tuple-element.38), channel_id=1, source_target_pairs={{0,12},{1,29},{2,14},{3,31},{4,8},{5,25},{6,10},{7,27},{8,20},{9,5... | collective-permute-start | bytes 786440 | tf_op jit(solution)/shard_map/ppermute | solution.py:62
  254.9 4.8 %collective-permute-start.24 = (bf16[8,128,128]{2,1,0:T(8,128)(2,1)S(1)}, bf16[8,128,128]{2,1,0:T(8,128)(2,1)S(1)}, u32[]{:S(2)}, u32[]{:S(2)}) collective-permute-start(bf16[8,128,128]{2,1,0:T(8,128)(2,1)S(1)} %get-tuple-element.40), channel_id=1, source_target_pairs={{0,4},{1,17},{2,6},{3,19},{4,0},{5,21},{6,2},{7,23},{8,12},{9,25},... | collective-permute-start | bytes 786440 | tf_op jit(solution)/shard_map/ppermute | solution.py:62
  269.1 4.4 %collective-permute-start.28 = (bf16[8,128,128]{2,1,0:T(8,128)(2,1)S(1)}, bf16[8,128,128]{2,1,0:T(8,128)(2,1)S(1)}, u32[]{:S(2)}, u32[]{:S(2)}) collective-permute-start(bf16[8,128,128]{2,1,0:T(8,128)(2,1)S(1)} %get-tuple-element.33), channel_id=1, source_target_pairs={{0,2},{1,7},{2,4},{3,1},{4,6},{5,3},{6,0},{7,5},{8,10},{9,15},{10,... | collective-permute-start | bytes 786440 | tf_op jit(solution)/shard_map/ppermute | solution.py:62
  277.9 11.8 %collective-permute-start.29 = (bf16[32,128,128]{2,1,0:T(8,128)(2,1)S(1)}, bf16[32,128,128]{2,1,0:T(8,128)(2,1)S(1)}, u32[]{:S(2)}, u32[]{:S(2)}) collective-permute-start(bf16[32,128,128]{2,1,0:T(8,128)(2,1)S(1)} %constant_dynamic-update-slice_fusion.34), channel_id=1, source_target_pairs={{0,1},{1,0},{2,3},{3,2},{4,5},{5,4},{6,7},{7,6},{8,9},{9,8},{10,11... | collective-permute-start | bytes 3145736 | tf_op jit(solution)/shard_map/ppermute | solution.py:53
  301.1 3.6 %all-to-all-done.3.refs_6_ = bf16[48,128,128]{2,1,0:T(8,128)(2,1)} async-done(((bf16[48,128,128]{2,1,0:T(8,128)(2,1)}), bf16[48,128,128]{2,1,0:T(8,128)(2,1)}, u32[]{:S(2)}, u32[]{:S(2)}) %all-to-all-start.3) | async-done | bytes 1572896 | tf_op jit(solution)/shard_map/all_to_all | solution.py:275
  304.7 4.9 %finish_last.1 = (bf16[24,128,128]{2,1,0:T(8,128)(2,1)}, bf16[24,128,128]{2,1,0:T(8,128)(2,1)}) custom-call(s32[24]{0:T(128)} %copy-done.16, s32[48]{0:T(128)} %reshape.342.refs_1_, f32[24]{0:T(128)} %copy-done.10, f32[24]{0:T(128)} %refs_3_.5, f32[24,128]{1,0:T(8,128)} %refs_4_.5, f32[128,24]{1,0:T(8,128)} %bitcast.252, ...), custom_call_target="tpu_custom_call" | custom-call | tf_op jit(solution)/shard_map/finish_last/pallas_call | solution.py:226
  (227 shorter events, 133.1 us)
Async XLA Ops:
  4.3 44.0 %all-to-all-start = ((s32[16,1,3]{2,1,0:T(1,128)}), s32[16,1,3]{2,1,0:T(1,128)S(1)}, u32[]{:S(2)}, u32[]{:S(2)}) async-start(s32[16,1,3]{2,1,0:T(1,128)} %bitcast.1), calls=%async_computation | async-start | bytes 16384 | tf_op jit(solution)/shard_map/all_to_all | solution.py:260
  43.1 21.2 %collective-permute-start = (bf16[32,128,128]{2,1,0:T(8,128)(2,1)}, bf16[32,128,128]{2,1,0:T(8,128)(2,1)}, u32[]{:S(2)}, u32[]{:S(2)}) collective-permute-start(bf16[32,128,128]{2,1,0:T(8,128)(2,1)} %gather_fusion.3), channel_id=1, source_target_pairs={{0,1},{1,0},{2,3},{3,2},{4,5},{5,4},{6,7},{7,6},{8,9},{9,8},{10,11... | collective-permute-start | bytes 3145736 | tf_op jit(solution)/shard_map/ppermute | solution.py:53
  50.5 81.7 %all-to-all-start.1 = ((bf16[48,128,128]{2,1,0:T(8,128)(2,1)}), bf16[48,128,128]{2,1,0:T(8,128)(2,1)}, u32[]{:S(2)}, u32[]{:S(2)}) async-start(bf16[48,128,128]{2,1,0:T(8,128)(2,1)} %gather_fusion), calls=%async_computation.1 | async-start | bytes 3145728 | tf_op jit(solution)/shard_map/all_to_all | solution.py:275
  65.7 15.7 %collective-permute-start.1 = (bf16[8,128,128]{2,1,0:T(8,128)(2,1)S(1)}, bf16[8,128,128]{2,1,0:T(8,128)(2,1)S(1)}, u32[]{:S(2)}, u32[]{:S(2)}) collective-permute-start(bf16[8,128,128]{2,1,0:T(8,128)(2,1)S(1)} %get-tuple-element.53), channel_id=1, source_target_pairs={{0,18},{1,23},{2,20},{3,17},{4,22},{5,19},{6,16},{7,21},{8,26},{9,... | collective-permute-start | bytes 786440 | tf_op jit(solution)/shard_map/ppermute | solution.py:62
  68.2 16.2 %collective-permute-start.2 = (bf16[8,128,128]{2,1,0:T(8,128)(2,1)S(1)}, bf16[8,128,128]{2,1,0:T(8,128)(2,1)S(1)}, u32[]{:S(2)}, u32[]{:S(2)}) collective-permute-start(bf16[8,128,128]{2,1,0:T(8,128)(2,1)S(1)} %get-tuple-element.54), channel_id=1, source_target_pairs={{0,12},{1,29},{2,14},{3,31},{4,8},{5,25},{6,10},{7,27},{8,20},{9,5... | collective-permute-start | bytes 786440 | tf_op jit(solution)/shard_map/ppermute | solution.py:62
  73.0 14.6 %collective-permute-start.3 = (bf16[8,128,128]{2,1,0:T(8,128)(2,1)S(1)}, bf16[8,128,128]{2,1,0:T(8,128)(2,1)S(1)}, u32[]{:S(2)}, u32[]{:S(2)}) collective-permute-start(bf16[8,128,128]{2,1,0:T(8,128)(2,1)S(1)} %get-tuple-element.55), channel_id=1, source_target_pairs={{0,0},{1,21},{2,2},{3,23},{4,4},{5,17},{6,6},{7,19},{8,8},{9,29},{... | collective-permute-start | bytes 786440 | tf_op jit(solution)/shard_map/ppermute | solution.py:62
  76.4 14.1 %collective-permute-start.4 = (bf16[8,128,128]{2,1,0:T(8,128)(2,1)S(1)}, bf16[8,128,128]{2,1,0:T(8,128)(2,1)S(1)}, u32[]{:S(2)}, u32[]{:S(2)}) collective-permute-start(bf16[8,128,128]{2,1,0:T(8,128)(2,1)S(1)} %get-tuple-element.56), channel_id=1, source_target_pairs={{0,4},{1,17},{2,6},{3,19},{4,0},{5,21},{6,2},{7,23},{8,12},{9,25},... | collective-permute-start | bytes 786440 | tf_op jit(solution)/shard_map/ppermute | solution.py:62
  81.5 16.4 %collective-permute-start.5 = (bf16[8,128,128]{2,1,0:T(8,128)(2,1)S(1)}, bf16[8,128,128]{2,1,0:T(8,128)(2,1)S(1)}, u32[]{:S(2)}, u32[]{:S(2)}) collective-permute-start(bf16[8,128,128]{2,1,0:T(8,128)(2,1)S(1)} %get-tuple-element.18), channel_id=1, source_target_pairs={{0,10},{1,31},{2,12},{3,25},{4,14},{5,27},{6,8},{7,29},{8,18},{9,7... | collective-permute-start | bytes 786440 | tf_op jit(solution)/shard_map/ppermute | solution.py:62
  84.4 13.5 %collective-permute-start.6 = (bf16[8,128,128]{2,1,0:T(8,128)(2,1)S(1)}, bf16[8,128,128]{2,1,0:T(8,128)(2,1)S(1)}, u32[]{:S(2)}, u32[]{:S(2)}) collective-permute-start(bf16[8,128,128]{2,1,0:T(8,128)(2,1)S(1)} %get-tuple-element.19), channel_id=1, source_target_pairs={{0,14},{1,27},{2,8},{3,29},{4,10},{5,31},{6,12},{7,25},{8,22},{9,3... | collective-permute-start | bytes 786440 | tf_op jit(solution)/shard_map/ppermute | solution.py:62
  101.3 24.2 %collective-permute-start.9 = (bf16[32,128,128]{2,1,0:T(8,128)(2,1)}, bf16[32,128,128]{2,1,0:T(8,128)(2,1)S(1)}, u32[]{:S(2)}, u32[]{:S(2)}) collective-permute-start(bf16[32,128,128]{2,1,0:T(8,128)(2,1)} %constant_dynamic-update-slice_fusion), channel_id=1, source_target_pairs={{0,1},{1,0},{2,3},{3,2},{4,5},{5,4},{6,7},{7,6},{8,9},{9,8},{10,11... | collective-permute-start | bytes 3145736 | tf_op jit(solution)/shard_map/ppermute | solution.py:53
  138.0 80.0 %all-to-all-start.2 = ((bf16[48,128,128]{2,1,0:T(8,128)(2,1)}), bf16[48,128,128]{2,1,0:T(8,128)(2,1)}, u32[]{:S(2)}, u32[]{:S(2)}) async-start(bf16[48,128,128]{2,1,0:T(8,128)(2,1)} %get-tuple-element.22), calls=%async_computation.2 | async-start | bytes 3145728 | tf_op jit(solution)/shard_map/all_to_all | solution.py:275
  157.6 15.5 %collective-permute-start.11 = (bf16[8,128,128]{2,1,0:T(8,128)(2,1)S(1)}, bf16[8,128,128]{2,1,0:T(8,128)(2,1)S(1)}, u32[]{:S(2)}, u32[]{:S(2)}) collective-permute-start(bf16[8,128,128]{2,1,0:T(8,128)(2,1)S(1)} %get-tuple-element.45), channel_id=1, source_target_pairs={{0,18},{1,23},{2,20},{3,17},{4,22},{5,19},{6,16},{7,21},{8,26},{9,... | collective-permute-start | bytes 786440 | tf_op jit(solution)/shard_map/ppermute | solution.py:62
  160.1 16.0 %collective-permute-start.12 = (bf16[8,128,128]{2,1,0:T(8,128)(2,1)S(1)}, bf16[8,128,128]{2,1,0:T(8,128)(2,1)S(1)}, u32[]{:S(2)}, u32[]{:S(2)}) collective-permute-start(bf16[8,128,128]{2,1,0:T(8,128)(2,1)S(1)} %get-tuple-element.46), channel_id=1, source_target_pairs={{0,12},{1,29},{2,14},{3,31},{4,8},{5,25},{6,10},{7,27},{8,20},{9,5... | collective-permute-start | bytes 786440 | tf_op jit(solution)/shard_map/ppermute | solution.py:62
  164.9 14.7 %collective-permute-start.13 = (bf16[8,128,128]{2,1,0:T(8,128)(2,1)S(1)}, bf16[8,128,128]{2,1,0:T(8,128)(2,1)S(1)}, u32[]{:S(2)}, u32[]{:S(2)}) collective-permute-start(bf16[8,128,128]{2,1,0:T(8,128)(2,1)S(1)} %get-tuple-element.47), channel_id=1, source_target_pairs={{0,0},{1,21},{2,2},{3,23},{4,4},{5,17},{6,6},{7,19},{8,8},{9,29},{... | collective-permute-start | bytes 786440 | tf_op jit(solution)/shard_map/ppermute | solution.py:62
  168.3 14.2 %collective-permute-start.14 = (bf16[8,128,128]{2,1,0:T(8,128)(2,1)S(1)}, bf16[8,128,128]{2,1,0:T(8,128)(2,1)S(1)}, u32[]{:S(2)}, u32[]{:S(2)}) collective-permute-start(bf16[8,128,128]{2,1,0:T(8,128)(2,1)S(1)} %get-tuple-element.48), channel_id=1, source_target_pairs={{0,4},{1,17},{2,6},{3,19},{4,0},{5,21},{6,2},{7,23},{8,12},{9,25},... | collective-permute-start | bytes 786440 | tf_op jit(solution)/shard_map/ppermute | solution.py:62
  173.1 14.0 %collective-permute-start.15 = (bf16[8,128,128]{2,1,0:T(8,128)(2,1)S(1)}, bf16[8,128,128]{2,1,0:T(8,128)(2,1)S(1)}, u32[]{:S(2)}, u32[]{:S(2)}) collective-permute-start(bf16[8,128,128]{2,1,0:T(8,128)(2,1)S(1)} %get-tuple-element.24), channel_id=1, source_target_pairs={{0,10},{1,31},{2,12},{3,25},{4,14},{5,27},{6,8},{7,29},{8,18},{9,7... | collective-permute-start | bytes 786440 | tf_op jit(solution)/shard_map/ppermute | solution.py:62
  191.2 14.8 %collective-permute-start.19 = (bf16[32,128,128]{2,1,0:T(8,128)(2,1)S(1)}, bf16[32,128,128]{2,1,0:T(8,128)(2,1)S(1)}, u32[]{:S(2)}, u32[]{:S(2)}) collective-permute-start(bf16[32,128,128]{2,1,0:T(8,128)(2,1)S(1)} %constant_dynamic-update-slice_fusion.17), channel_id=1, source_target_pairs={{0,1},{1,0},{2,3},{3,2},{4,5},{5,4},{6,7},{7,6},{8,9},{9,8},{10,11... | collective-permute-start | bytes 3145736 | tf_op jit(solution)/shard_map/ppermute | solution.py:53
  223.9 80.8 %all-to-all-start.3 = ((bf16[48,128,128]{2,1,0:T(8,128)(2,1)}), bf16[48,128,128]{2,1,0:T(8,128)(2,1)}, u32[]{:S(2)}, u32[]{:S(2)}) async-start(bf16[48,128,128]{2,1,0:T(8,128)(2,1)} %get-tuple-element.28), calls=%async_computation.3 | async-start | bytes 3145728 | tf_op jit(solution)/shard_map/all_to_all | solution.py:275
  244.2 15.5 %collective-permute-start.21 = (bf16[8,128,128]{2,1,0:T(8,128)(2,1)S(1)}, bf16[8,128,128]{2,1,0:T(8,128)(2,1)S(1)}, u32[]{:S(2)}, u32[]{:S(2)}) collective-permute-start(bf16[8,128,128]{2,1,0:T(8,128)(2,1)S(1)} %get-tuple-element.37), channel_id=1, source_target_pairs={{0,18},{1,23},{2,20},{3,17},{4,22},{5,19},{6,16},{7,21},{8,26},{9,... | collective-permute-start | bytes 786440 | tf_op jit(solution)/shard_map/ppermute | solution.py:62
  246.7 16.0 %collective-permute-start.22 = (bf16[8,128,128]{2,1,0:T(8,128)(2,1)S(1)}, bf16[8,128,128]{2,1,0:T(8,128)(2,1)S(1)}, u32[]{:S(2)}, u32[]{:S(2)}) collective-permute-start(bf16[8,128,128]{2,1,0:T(8,128)(2,1)S(1)} %get-tuple-element.38), channel_id=1, source_target_pairs={{0,12},{1,29},{2,14},{3,31},{4,8},{5,25},{6,10},{7,27},{8,20},{9,5... | collective-permute-start | bytes 786440 | tf_op jit(solution)/shard_map/ppermute | solution.py:62
  251.5 14.7 %collective-permute-start.23 = (bf16[8,128,128]{2,1,0:T(8,128)(2,1)S(1)}, bf16[8,128,128]{2,1,0:T(8,128)(2,1)S(1)}, u32[]{:S(2)}, u32[]{:S(2)}) collective-permute-start(bf16[8,128,128]{2,1,0:T(8,128)(2,1)S(1)} %get-tuple-element.39), channel_id=1, source_target_pairs={{0,0},{1,21},{2,2},{3,23},{4,4},{5,17},{6,6},{7,19},{8,8},{9,29},{... | collective-permute-start | bytes 786440 | tf_op jit(solution)/shard_map/ppermute | solution.py:62
  254.9 14.2 %collective-permute-start.24 = (bf16[8,128,128]{2,1,0:T(8,128)(2,1)S(1)}, bf16[8,128,128]{2,1,0:T(8,128)(2,1)S(1)}, u32[]{:S(2)}, u32[]{:S(2)}) collective-permute-start(bf16[8,128,128]{2,1,0:T(8,128)(2,1)S(1)} %get-tuple-element.40), channel_id=1, source_target_pairs={{0,4},{1,17},{2,6},{3,19},{4,0},{5,21},{6,2},{7,23},{8,12},{9,25},... | collective-permute-start | bytes 786440 | tf_op jit(solution)/shard_map/ppermute | solution.py:62
  259.8 14.0 %collective-permute-start.25 = (bf16[8,128,128]{2,1,0:T(8,128)(2,1)S(1)}, bf16[8,128,128]{2,1,0:T(8,128)(2,1)S(1)}, u32[]{:S(2)}, u32[]{:S(2)}) collective-permute-start(bf16[8,128,128]{2,1,0:T(8,128)(2,1)S(1)} %get-tuple-element.30), channel_id=1, source_target_pairs={{0,10},{1,31},{2,12},{3,25},{4,14},{5,27},{6,8},{7,29},{8,18},{9,7... | collective-permute-start | bytes 786440 | tf_op jit(solution)/shard_map/ppermute | solution.py:62
  277.9 17.1 %collective-permute-start.29 = (bf16[32,128,128]{2,1,0:T(8,128)(2,1)S(1)}, bf16[32,128,128]{2,1,0:T(8,128)(2,1)S(1)}, u32[]{:S(2)}, u32[]{:S(2)}) collective-permute-start(bf16[32,128,128]{2,1,0:T(8,128)(2,1)S(1)} %constant_dynamic-update-slice_fusion.34), channel_id=1, source_target_pairs={{0,1},{1,0},{2,3},{3,2},{4,5},{5,4},{6,7},{7,6},{8,9},{9,8},{10,11... | collective-permute-start | bytes 3145736 | tf_op jit(solution)/shard_map/ppermute | solution.py:53
  (30 other events, 438.2 us)

commit v5 on v4

--- a/solution.py
+++ b/solution.py
@@ -1,3 +1,5 @@
+import functools
+
 import jax
 import jax.numpy as jnp
 from jax import lax
@@ -92,10 +94,42 @@
         if number >= LANES:
             outgoing, _ = lax.optimization_barrier((outgoing, arrived[-LANES]))
         arrived.append(chip_exchange(outgoing, offsets))
-    arrived = [piece.reshape(2, 2, 2, width, width) for piece in arrived]
-    keep = jnp.concatenate([piece[:, 0].reshape(4, width, width) for piece in arrived], axis=0)
-    swap = jnp.concatenate([piece[:, 1].reshape(4, width, width) for piece in arrived], axis=0)
-    return jnp.concatenate([keep, core_exchange(swap)], axis=0)
+    swapped = core_exchange(collect(arrived, 1, None))
+    return collect(arrived, 0, swapped)
+
+
+def collect_kernel(*refs, part, whole):
+    *pieces, out_ref, sems = refs
+    copies = []
+    places = [(source, first, 2) for source in pieces[: len(STEPS)] for first in (2 * part, 2 * part + 4)]
+    if whole:
+        places.append((pieces[-1], 0, whole))
+    at = 0
+    for number, (source, first, size) in enumerate(places):
+        copies.append(
+            pltpu.make_async_copy(
+                source.at[pl.ds(first, size)], out_ref.at[pl.ds(at, size)], sems.at[number]
+            )
+        )
+        copies[-1].start()
+        at += size
+    for copy in copies:
+        copy.wait()
+
+
+def collect(pieces, part, extra):
+    whole = 0 if extra is None else extra.shape[0]
+    operands = list(pieces) + ([] if extra is None else [extra])
+    count = 4 * len(pieces) + whole
+    hbm = pl.BlockSpec(memory_space=pltpu.HBM)
+    return pl.pallas_call(
+        functools.partial(collect_kernel, part=part, whole=whole),
+        out_shape=pltpu.HBM((count,) + pieces[0].shape[1:], pieces[0].dtype),
+        in_specs=[hbm] * len(operands),
+        out_specs=hbm,
+        scratch_shapes=[pltpu.SemaphoreType.DMA((2 * len(pieces) + 1,))],
+        name="collect_kept" if whole else "collect_swapped",
+    )(*operands)
 
 
 def finish_kernel(

time: 315 us -> 589 us (1.87)
  Pallas kernels: 16.5 us -> 310 us
  blocking collectives: 14.5 us -> 42.7 us
  local copies, waits for them, and re-layouts: 53 us -> 25.9 us
  starting transfers between devices: 178 us -> 160 us
  waiting for transfers between devices: 23.3 us -> 29.3 us
    pallas_call x0 -> x6, Pallas kernels: none -> 293 us  [collect(): pl.pallas_call(functools.partial(collect_kernel, part=part, whole=whole),...]
    all_to_all x0 -> x1, blocking collectives: none -> 26.8 us  [body(): lax.all_to_all(col_table, 'oi', split_axis=0, concat_axis=0, tiled=True)]
    unnamed x91 -> x82, local copies, waits for them, and re-layouts: 24.7 us -> 5.48 us
    all_to_all x1 -> x0, starting transfers between devices: 15.7 us -> none  [body(): lax.all_to_all(col_table, 'oi', split_axis=0, concat_axis=0, tiled=True)]
    all_to_all x3, waiting for transfers between devices: 9.48 us -> 0.01 us  [body(): lax.all_to_all(col_send, 'oi', split_axis=0, concat_axis=0, tiled=True)]
    ppermute x24, waiting for transfers between devices: 10.3 us -> 19.2 us  [chip_exchange(): return lax.ppermute(blocks, 'oj', pairs)]
    ppermute x6, waiting for transfers between devices: 3.47 us -> 10.1 us  [core_exchange(): lax.ppermute(blocks, 'oj', [(source, source ^ 1) for source in range(32)])]
    all_to_all x3, starting transfers between devices: 34.6 us -> 28.2 us  [body(): lax.all_to_all(col_send, 'oi', split_axis=0, concat_axis=0, tiled=True)]
  transfers between devices with their start and end apart: 34 -> 33, of which waited for: 11 -> 14; matrix products, arithmetic and copies ran while one was open for 23% -> 6% of each run, Pallas kernels for 0% -> 50%
where the time goes in v5:
time: 589 us; the launch traced here: 587 us
  Pallas kernels  310 us (53%)
  starting transfers between devices  160 us (27%)
  blocking collectives  42.7 us (7%)
  waiting for transfers between devices  29.3 us (5%)
  local copies, waits for them, and re-layouts  25.9 us (4%)
  other arithmetic  9.03 us (2%)
  matrix products  7.72 us (1%)
    pallas_call x6, Pallas kernels, collect(): pl.pallas_call(functools.partial(collect_kernel, part=part, whole=whole),...  293 us
    ppermute x24, starting transfers between devices, chip_exchange(): return lax.ppermute(blocks, 'oj', pairs)  87.2 us
    ppermute x6, starting transfers between devices, core_exchange(): lax.ppermute(blocks, 'oj', [(source, source ^ 1) for source in range(32)])  44.6 us
    all_to_all x3, starting transfers between devices, body(): lax.all_to_all(col_send, 'oi', split_axis=0, concat_axis=0, tiled=True)  28.2 us
    all_to_all x1, blocking collectives, body(): lax.all_to_all(col_table, 'oi', split_axis=0, concat_axis=0, tiled=True)  26.8 us
    ppermute x24, waiting for transfers between devices, chip_exchange(): return lax.ppermute(blocks, 'oj', pairs)  19.2 us
    pallas_call x3, Pallas kernels, finish(): pl.pallas_call(last_kernel if last else middle_kernel, out_shape=(pltpu.H...  16.5 us
    unnamed x1, blocking collectives  15.9 us
  transfers between devices with their start and end apart: 33, of which 14 were waited for; matrix products, arithmetic and copies ran while one was open for 6% of the time, Pallas kernels for 50%

profile of v5, /device:TPU:1, one launch (start us, length us, event | category | flops | bytes accessed | tf_op | source)
XLA Modules:
  0.0 587.2 jit_solution(11469425241968437754)
XLA Ops:
  3.1 26.8 %all_to_all.24 = s32[16,1,3]{2,1,0:T(1,128)S(1)} all-to-all(s32[16,1,3]{2,1,0:T(1,128)S(1)} %bitcast.119), channel_id=1, replica_groups=mesh['oi'=16,'oj'=32] {'oi'}, dimensions={0} | all-to-all | bytes 384 | tf_op jit(solution)/shard_map/all_to_all | solution.py:294
  40.1 15.9 %all-reduce = s32[768]{0:T(1024)S(1)} all-reduce(s32[768]{0:T(1024)S(1)} %get-tuple-element.65), channel_id=2, replica_groups=mesh['oi'=16,'oj'=32] {'oj'}, use_global_device_ids=true, to_apply=%add | all-reduce | flops 768 | bytes 6144
  59.4 5.0 collective-permute-start
  71.0 4.8 collective-permute-start.2
  79.2 4.8 collective-permute-start.4
  93.5 4.6 collective-permute-start.8
  102.2 33.0 %collect_swapped.3 = bf16[32,128,128]{2,1,0:T(8,128)(2,1)} custom-call(bf16[8,128,128]{2,1,0:T(8,128)(2,1)} %copy-done.11, bf16[8,128,128]{2,1,0:T(8,128)(2,1)} %copy-done.12, bf16[8,128,128]{2,1,0:T(8,128)(2,1)} %copy-done.13, bf16[8,128,128]{2,1,0:T(8,128)(2,1)} %copy-done.14, bf16[8,128,128]{2,1,0:T(8,128)(2,1)} %copy-done.15, ...), custom_call_target="tpu_custom_call" | custom-call | tf_op jit(solution)/shard_map/collect_swapped/pallas_call | solution.py:125
  135.2 12.1 %collective-permute-start.9 = (bf16[32,128,128]{2,1,0:T(8,128)(2,1)}, bf16[32,128,128]{2,1,0:T(8,128)(2,1)S(1)}, u32[]{:S(2)}, u32[]{:S(2)}) collective-permute-start(bf16[32,128,128]{2,1,0:T(8,128)(2,1)} %collect_swapped.3), channel_id=1, source_target_pairs={{0,1},{1,0},{2,3},{3,2},{4,5},{5,4},{6,7},{7,6},{8,9},{9,8},{10,11... | collective-permute-start | bytes 3145736 | tf_op jit(solution)/shard_map/ppermute | solution.py:55
  152.6 64.8 %collect_kept.3 = bf16[64,128,128]{2,1,0:T(8,128)(2,1)} custom-call(bf16[8,128,128]{2,1,0:T(8,128)(2,1)} %copy-done.11, bf16[8,128,128]{2,1,0:T(8,128)(2,1)} %copy-done.12, bf16[8,128,128]{2,1,0:T(8,128)(2,1)} %copy-done.13, bf16[8,128,128]{2,1,0:T(8,128)(2,1)} %copy-done.14, bf16[8,128,128]{2,1,0:T(8,128)(2,1)} %copy-done.15, ...), custom_call_target="tpu_custom_call" | custom-call | tf_op jit(solution)/shard_map/collect_kept/pallas_call | solution.py:125
  222.3 5.8 finish.2
  228.1 11.7 %all-to-all-start.2 = ((bf16[48,128,128]{2,1,0:T(8,128)(2,1)}), bf16[48,128,128]{2,1,0:T(8,128)(2,1)}, u32[]{:S(2)}, u32[]{:S(2)}) async-start(bf16[48,128,128]{2,1,0:T(8,128)(2,1)} %get-tuple-element.22), calls=%async_computation.2 | async-start | bytes 3145728 | tf_op jit(solution)/shard_map/all_to_all | solution.py:309
  283.5 33.0 %collect_swapped.4 = bf16[32,128,128]{2,1,0:T(8,128)(2,1)} custom-call(bf16[8,128,128]{2,1,0:T(8,128)(2,1)} %copy-done.18, bf16[8,128,128]{2,1,0:T(8,128)(2,1)} %copy-done.20, bf16[8,128,128]{2,1,0:T(8,128)(2,1)} %copy-done.22, bf16[8,128,128]{2,1,0:T(8,128)(2,1)} %copy-done.24, bf16[8,128,128]{2,1,0:T(8,128)(2,1)} %collective-permute-done.15.refs_4_, ...), custom_call_target="tpu_custom_call" | custom-call | tf_op jit(solution)/shard_map/collect_swapped/pallas_call | solution.py:125
  316.5 12.3 %collective-permute-start.19 = (bf16[32,128,128]{2,1,0:T(8,128)(2,1)}, bf16[32,128,128]{2,1,0:T(8,128)(2,1)S(1)}, u32[]{:S(2)}, u32[]{:S(2)}) collective-permute-start(bf16[32,128,128]{2,1,0:T(8,128)(2,1)} %collect_swapped.4), channel_id=1, source_target_pairs={{0,1},{1,0},{2,3},{3,2},{4,5},{5,4},{6,7},{7,6},{8,9},{9,8},{10,11... | collective-permute-start | bytes 3145736 | tf_op jit(solution)/shard_map/ppermute | solution.py:55
  332.1 64.8 %collect_kept.4 = bf16[64,128,128]{2,1,0:T(8,128)(2,1)} custom-call(bf16[8,128,128]{2,1,0:T(8,128)(2,1)} %copy-done.18, bf16[8,128,128]{2,1,0:T(8,128)(2,1)} %copy-done.20, bf16[8,128,128]{2,1,0:T(8,128)(2,1)} %copy-done.22, bf16[8,128,128]{2,1,0:T(8,128)(2,1)} %copy-done.24, bf16[8,128,128]{2,1,0:T(8,128)(2,1)} %collective-permute-done.15.refs_4_, ...), custom_call_target="tpu_custom_call" | custom-call | tf_op jit(solution)/shard_map/collect_kept/pallas_call | solution.py:125
  401.7 5.9 finish.3
  407.6 11.9 %all-to-all-start.3 = ((bf16[48,128,128]{2,1,0:T(8,128)(2,1)}), bf16[48,128,128]{2,1,0:T(8,128)(2,1)}, u32[]{:S(2)}, u32[]{:S(2)}) async-start(bf16[48,128,128]{2,1,0:T(8,128)(2,1)} %get-tuple-element.28), calls=%async_computation.3 | async-start | bytes 3145728 | tf_op jit(solution)/shard_map/all_to_all | solution.py:309
  434.1 5.2 collective-permute-start.23
  443.0 4.9 collective-permute-start.25
  450.1 5.3 collective-permute-start.27
  460.3 5.3 collective-permute-done.28.refs_7_
  465.6 33.0 %collect_swapped.5 = bf16[32,128,128]{2,1,0:T(8,128)(2,1)} custom-call(bf16[8,128,128]{2,1,0:T(8,128)(2,1)} %copy-done.19, bf16[8,128,128]{2,1,0:T(8,128)(2,1)} %copy-done.21, bf16[8,128,128]{2,1,0:T(8,128)(2,1)} %copy-done.23, bf16[8,128,128]{2,1,0:T(8,128)(2,1)} %copy-done.25, bf16[8,128,128]{2,1,0:T(8,128)(2,1)} %collective-permute-done.25.refs_4_, ...), custom_call_target="tpu_custom_call" | custom-call | tf_op jit(solution)/shard_map/collect_swapped/pallas_call | solution.py:125
  498.6 10.4 %collective-permute-start.29 = (bf16[32,128,128]{2,1,0:T(8,128)(2,1)}, bf16[32,128,128]{2,1,0:T(8,128)(2,1)S(1)}, u32[]{:S(2)}, u32[]{:S(2)}) collective-permute-start(bf16[32,128,128]{2,1,0:T(8,128)(2,1)} %collect_swapped.5), channel_id=1, source_target_pairs={{0,1},{1,0},{2,3},{3,2},{4,5},{5,4},{6,7},{7,6},{8,9},{9,8},{10,11... | collective-permute-start | bytes 3145736 | tf_op jit(solution)/shard_map/ppermute | solution.py:55
  512.5 64.8 %collect_kept.5 = bf16[64,128,128]{2,1,0:T(8,128)(2,1)} custom-call(bf16[8,128,128]{2,1,0:T(8,128)(2,1)} %copy-done.19, bf16[8,128,128]{2,1,0:T(8,128)(2,1)} %copy-done.21, bf16[8,128,128]{2,1,0:T(8,128)(2,1)} %copy-done.23, bf16[8,128,128]{2,1,0:T(8,128)(2,1)} %copy-done.25, bf16[8,128,128]{2,1,0:T(8,128)(2,1)} %collective-permute-done.25.refs_4_, ...), custom_call_target="tpu_custom_call" | custom-call | tf_op jit(solution)/shard_map/collect_kept/pallas_call | solution.py:125
  582.1 4.9 finish_last.1
  (194 shorter events, 133.6 us)
Async XLA Ops:
  33.2 189.1 %all-to-all-start.1 = ((bf16[48,128,128]{2,1,0:T(8,128)(2,1)}), bf16[48,128,128]{2,1,0:T(8,128)(2,1)}, u32[]{:S(2)}, u32[]{:S(2)}) async-start(bf16[48,128,128]{2,1,0:T(8,128)(2,1)} %gather_fusion), calls=%async_computation.1 | async-start | bytes 3145728 | tf_op jit(solution)/shard_map/all_to_all | solution.py:309
  68.5 15.5 %collective-permute-start.1 = (bf16[8,128,128]{2,1,0:T(8,128)(2,1)S(1)}, bf16[8,128,128]{2,1,0:T(8,128)(2,1)S(1)}, u32[]{:S(2)}, u32[]{:S(2)}) collective-permute-start(bf16[8,128,128]{2,1,0:T(8,128)(2,1)S(1)} %get-tuple-element.53), channel_id=1, source_target_pairs={{0,18},{1,23},{2,20},{3,17},{4,22},{5,19},{6,16},{7,21},{8,26},{9,... | collective-permute-start | bytes 786440 | tf_op jit(solution)/shard_map/ppermute | solution.py:64
  71.0 16.0 %collective-permute-start.2 = (bf16[8,128,128]{2,1,0:T(8,128)(2,1)S(1)}, bf16[8,128,128]{2,1,0:T(8,128)(2,1)S(1)}, u32[]{:S(2)}, u32[]{:S(2)}) collective-permute-start(bf16[8,128,128]{2,1,0:T(8,128)(2,1)S(1)} %get-tuple-element.54), channel_id=1, source_target_pairs={{0,12},{1,29},{2,14},{3,31},{4,8},{5,25},{6,10},{7,27},{8,20},{9,5... | collective-permute-start | bytes 786440 | tf_op jit(solution)/shard_map/ppermute | solution.py:64
  75.8 14.7 %collective-permute-start.3 = (bf16[8,128,128]{2,1,0:T(8,128)(2,1)S(1)}, bf16[8,128,128]{2,1,0:T(8,128)(2,1)S(1)}, u32[]{:S(2)}, u32[]{:S(2)}) collective-permute-start(bf16[8,128,128]{2,1,0:T(8,128)(2,1)S(1)} %get-tuple-element.55), channel_id=1, source_target_pairs={{0,0},{1,21},{2,2},{3,23},{4,4},{5,17},{6,6},{7,19},{8,8},{9,29},{... | collective-permute-start | bytes 786440 | tf_op jit(solution)/shard_map/ppermute | solution.py:64
  79.2 14.2 %collective-permute-start.4 = (bf16[8,128,128]{2,1,0:T(8,128)(2,1)S(1)}, bf16[8,128,128]{2,1,0:T(8,128)(2,1)S(1)}, u32[]{:S(2)}, u32[]{:S(2)}) collective-permute-start(bf16[8,128,128]{2,1,0:T(8,128)(2,1)S(1)} %get-tuple-element.56), channel_id=1, source_target_pairs={{0,4},{1,17},{2,6},{3,19},{4,0},{5,21},{6,2},{7,23},{8,12},{9,25},... | collective-permute-start | bytes 786440 | tf_op jit(solution)/shard_map/ppermute | solution.py:64
  84.0 14.0 %collective-permute-start.5 = (bf16[8,128,128]{2,1,0:T(8,128)(2,1)S(1)}, bf16[8,128,128]{2,1,0:T(8,128)(2,1)S(1)}, u32[]{:S(2)}, u32[]{:S(2)}) collective-permute-start(bf16[8,128,128]{2,1,0:T(8,128)(2,1)S(1)} %get-tuple-element.18), channel_id=1, source_target_pairs={{0,10},{1,31},{2,12},{3,25},{4,14},{5,27},{6,8},{7,29},{8,18},{9,7... | collective-permute-start | bytes 786440 | tf_op jit(solution)/shard_map/ppermute | solution.py:64
  87.0 11.1 %collective-permute-start.6 = (bf16[8,128,128]{2,1,0:T(8,128)(2,1)S(1)}, bf16[8,128,128]{2,1,0:T(8,128)(2,1)S(1)}, u32[]{:S(2)}, u32[]{:S(2)}) collective-permute-start(bf16[8,128,128]{2,1,0:T(8,128)(2,1)S(1)} %get-tuple-element.19), channel_id=1, source_target_pairs={{0,14},{1,27},{2,8},{3,29},{4,10},{5,31},{6,12},{7,25},{8,22},{9,3... | collective-permute-start | bytes 786440 | tf_op jit(solution)/shard_map/ppermute | solution.py:64
  135.2 16.4 %collective-permute-start.9 = (bf16[32,128,128]{2,1,0:T(8,128)(2,1)}, bf16[32,128,128]{2,1,0:T(8,128)(2,1)S(1)}, u32[]{:S(2)}, u32[]{:S(2)}) collective-permute-start(bf16[32,128,128]{2,1,0:T(8,128)(2,1)} %collect_swapped.3), channel_id=1, source_target_pairs={{0,1},{1,0},{2,3},{3,2},{4,5},{5,4},{6,7},{7,6},{8,9},{9,8},{10,11... | collective-permute-start | bytes 3145736 | tf_op jit(solution)/shard_map/ppermute | solution.py:55
  228.1 173.6 %all-to-all-start.2 = ((bf16[48,128,128]{2,1,0:T(8,128)(2,1)}), bf16[48,128,128]{2,1,0:T(8,128)(2,1)}, u32[]{:S(2)}, u32[]{:S(2)}) async-start(bf16[48,128,128]{2,1,0:T(8,128)(2,1)} %get-tuple-element.22), calls=%async_computation.2 | async-start | bytes 3145728 | tf_op jit(solution)/shard_map/all_to_all | solution.py:309
  247.9 16.0 %collective-permute-start.11 = (bf16[8,128,128]{2,1,0:T(8,128)(2,1)S(1)}, bf16[8,128,128]{2,1,0:T(8,128)(2,1)S(1)}, u32[]{:S(2)}, u32[]{:S(2)}) collective-permute-start(bf16[8,128,128]{2,1,0:T(8,128)(2,1)S(1)} %get-tuple-element.45), channel_id=1, source_target_pairs={{0,18},{1,23},{2,20},{3,17},{4,22},{5,19},{6,16},{7,21},{8,26},{9,... | collective-permute-start | bytes 786440 | tf_op jit(solution)/shard_map/ppermute | solution.py:64
  251.9 15.7 %collective-permute-start.12 = (bf16[8,128,128]{2,1,0:T(8,128)(2,1)S(1)}, bf16[8,128,128]{2,1,0:T(8,128)(2,1)S(1)}, u32[]{:S(2)}, u32[]{:S(2)}) collective-permute-start(bf16[8,128,128]{2,1,0:T(8,128)(2,1)S(1)} %get-tuple-element.46), channel_id=1, source_target_pairs={{0,12},{1,29},{2,14},{3,31},{4,8},{5,25},{6,10},{7,27},{8,20},{9,5... | collective-permute-start | bytes 786440 | tf_op jit(solution)/shard_map/ppermute | solution.py:64
  255.6 15.1 %collective-permute-start.13 = (bf16[8,128,128]{2,1,0:T(8,128)(2,1)S(1)}, bf16[8,128,128]{2,1,0:T(8,128)(2,1)S(1)}, u32[]{:S(2)}, u32[]{:S(2)}) collective-permute-start(bf16[8,128,128]{2,1,0:T(8,128)(2,1)S(1)} %get-tuple-element.47), channel_id=1, source_target_pairs={{0,0},{1,21},{2,2},{3,23},{4,4},{5,17},{6,6},{7,19},{8,8},{9,29},{... | collective-permute-start | bytes 786440 | tf_op jit(solution)/shard_map/ppermute | solution.py:64
  259.6 15.6 %collective-permute-start.14 = (bf16[8,128,128]{2,1,0:T(8,128)(2,1)S(1)}, bf16[8,128,128]{2,1,0:T(8,128)(2,1)S(1)}, u32[]{:S(2)}, u32[]{:S(2)}) collective-permute-start(bf16[8,128,128]{2,1,0:T(8,128)(2,1)S(1)} %get-tuple-element.48), channel_id=1, source_target_pairs={{0,4},{1,17},{2,6},{3,19},{4,0},{5,21},{6,2},{7,23},{8,12},{9,25},... | collective-permute-start | bytes 786440 | tf_op jit(solution)/shard_map/ppermute | solution.py:64
  263.9 13.2 %collective-permute-start.15 = (bf16[8,128,128]{2,1,0:T(8,128)(2,1)S(1)}, bf16[8,128,128]{2,1,0:T(8,128)(2,1)}, u32[]{:S(2)}, u32[]{:S(2)}) collective-permute-start(bf16[8,128,128]{2,1,0:T(8,128)(2,1)S(1)} %get-tuple-element.24), channel_id=1, source_target_pairs={{0,10},{1,31},{2,12},{3,25},{4,14},{5,27},{6,8},{7,29},{8,18},{9,7... | collective-permute-start | bytes 786440 | tf_op jit(solution)/shard_map/ppermute | solution.py:64
  316.5 14.6 %collective-permute-start.19 = (bf16[32,128,128]{2,1,0:T(8,128)(2,1)}, bf16[32,128,128]{2,1,0:T(8,128)(2,1)S(1)}, u32[]{:S(2)}, u32[]{:S(2)}) collective-permute-start(bf16[32,128,128]{2,1,0:T(8,128)(2,1)} %collect_swapped.4), channel_id=1, source_target_pairs={{0,1},{1,0},{2,3},{3,2},{4,5},{5,4},{6,7},{7,6},{8,9},{9,8},{10,11... | collective-permute-start | bytes 3145736 | tf_op jit(solution)/shard_map/ppermute | solution.py:55
  407.6 174.5 %all-to-all-start.3 = ((bf16[48,128,128]{2,1,0:T(8,128)(2,1)}), bf16[48,128,128]{2,1,0:T(8,128)(2,1)}, u32[]{:S(2)}, u32[]{:S(2)}) async-start(bf16[48,128,128]{2,1,0:T(8,128)(2,1)} %get-tuple-element.28), calls=%async_computation.3 | async-start | bytes 3145728 | tf_op jit(solution)/shard_map/all_to_all | solution.py:309
  427.9 15.1 %collective-permute-start.21 = (bf16[8,128,128]{2,1,0:T(8,128)(2,1)S(1)}, bf16[8,128,128]{2,1,0:T(8,128)(2,1)S(1)}, u32[]{:S(2)}, u32[]{:S(2)}) collective-permute-start(bf16[8,128,128]{2,1,0:T(8,128)(2,1)S(1)} %get-tuple-element.37), channel_id=1, source_target_pairs={{0,18},{1,23},{2,20},{3,17},{4,22},{5,19},{6,16},{7,21},{8,26},{9,... | collective-permute-start | bytes 786440 | tf_op jit(solution)/shard_map/ppermute | solution.py:64
  432.1 15.7 %collective-permute-start.22 = (bf16[8,128,128]{2,1,0:T(8,128)(2,1)S(1)}, bf16[8,128,128]{2,1,0:T(8,128)(2,1)S(1)}, u32[]{:S(2)}, u32[]{:S(2)}) collective-permute-start(bf16[8,128,128]{2,1,0:T(8,128)(2,1)S(1)} %get-tuple-element.38), channel_id=1, source_target_pairs={{0,12},{1,29},{2,14},{3,31},{4,8},{5,25},{6,10},{7,27},{8,20},{9,5... | collective-permute-start | bytes 786440 | tf_op jit(solution)/shard_map/ppermute | solution.py:64
  434.1 16.0 %collective-permute-start.23 = (bf16[8,128,128]{2,1,0:T(8,128)(2,1)S(1)}, bf16[8,128,128]{2,1,0:T(8,128)(2,1)S(1)}, u32[]{:S(2)}, u32[]{:S(2)}) collective-permute-start(bf16[8,128,128]{2,1,0:T(8,128)(2,1)S(1)} %get-tuple-element.39), channel_id=1, source_target_pairs={{0,0},{1,21},{2,2},{3,23},{4,4},{5,17},{6,6},{7,19},{8,8},{9,29},{... | collective-permute-start | bytes 786440 | tf_op jit(solution)/shard_map/ppermute | solution.py:64
  439.3 16.1 %collective-permute-start.24 = (bf16[8,128,128]{2,1,0:T(8,128)(2,1)S(1)}, bf16[8,128,128]{2,1,0:T(8,128)(2,1)S(1)}, u32[]{:S(2)}, u32[]{:S(2)}) collective-permute-start(bf16[8,128,128]{2,1,0:T(8,128)(2,1)S(1)} %get-tuple-element.40), channel_id=1, source_target_pairs={{0,4},{1,17},{2,6},{3,19},{4,0},{5,21},{6,2},{7,23},{8,12},{9,25},... | collective-permute-start | bytes 786440 | tf_op jit(solution)/shard_map/ppermute | solution.py:64
  443.0 15.2 %collective-permute-start.25 = (bf16[8,128,128]{2,1,0:T(8,128)(2,1)S(1)}, bf16[8,128,128]{2,1,0:T(8,128)(2,1)}, u32[]{:S(2)}, u32[]{:S(2)}) collective-permute-start(bf16[8,128,128]{2,1,0:T(8,128)(2,1)S(1)} %get-tuple-element.30), channel_id=1, source_target_pairs={{0,10},{1,31},{2,12},{3,25},{4,14},{5,27},{6,8},{7,29},{8,18},{9,7... | collective-permute-start | bytes 786440 | tf_op jit(solution)/shard_map/ppermute | solution.py:64
  447.9 10.3 %collective-permute-start.26 = (bf16[8,128,128]{2,1,0:T(8,128)(2,1)S(1)}, bf16[8,128,128]{2,1,0:T(8,128)(2,1)}, u32[]{:S(2)}, u32[]{:S(2)}) collective-permute-start(bf16[8,128,128]{2,1,0:T(8,128)(2,1)S(1)} %get-tuple-element.31), channel_id=1, source_target_pairs={{0,14},{1,27},{2,8},{3,29},{4,10},{5,31},{6,12},{7,25},{8,22},{9,3... | collective-permute-start | bytes 786440 | tf_op jit(solution)/shard_map/ppermute | solution.py:64
  450.1 10.2 %collective-permute-start.27 = (bf16[8,128,128]{2,1,0:T(8,128)(2,1)S(1)}, bf16[8,128,128]{2,1,0:T(8,128)(2,1)}, u32[]{:S(2)}, u32[]{:S(2)}) collective-permute-start(bf16[8,128,128]{2,1,0:T(8,128)(2,1)S(1)} %get-tuple-element.32), channel_id=1, source_target_pairs={{0,8},{1,25},{2,10},{3,27},{4,12},{5,29},{6,14},{7,31},{8,16},{9,1... | collective-permute-start | bytes 786440 | tf_op jit(solution)/shard_map/ppermute | solution.py:64
  498.6 12.9 %collective-permute-start.29 = (bf16[32,128,128]{2,1,0:T(8,128)(2,1)}, bf16[32,128,128]{2,1,0:T(8,128)(2,1)S(1)}, u32[]{:S(2)}, u32[]{:S(2)}) collective-permute-start(bf16[32,128,128]{2,1,0:T(8,128)(2,1)} %collect_swapped.5), channel_id=1, source_target_pairs={{0,1},{1,0},{2,3},{3,2},{4,5},{5,4},{6,7},{7,6},{8,9},{9,8},{10,11... | collective-permute-start | bytes 3145736 | tf_op jit(solution)/shard_map/ppermute | solution.py:55
  (47 other events, 887.1 us)

commit v6 on v5

--- a/solution.py
+++ b/solution.py
@@ -99,7 +99,7 @@
 
 
 def collect_kernel(*refs, part, whole):
-    *pieces, out_ref, sems = refs
+    *pieces, out_ref, buffer, sems = refs
     copies = []
     places = [(source, first, 2) for source in pieces[: len(STEPS)] for first in (2 * part, 2 * part + 4)]
     if whole:
@@ -108,13 +108,16 @@
     for number, (source, first, size) in enumerate(places):
         copies.append(
             pltpu.make_async_copy(
-                source.at[pl.ds(first, size)], out_ref.at[pl.ds(at, size)], sems.at[number]
+                source.at[pl.ds(first, size)], buffer.at[pl.ds(at, size)], sems.at[number]
             )
         )
         copies[-1].start()
         at += size
     for copy in copies:
         copy.wait()
+    leaving = pltpu.make_async_copy(buffer, out_ref, sems.at[len(places)])
+    leaving.start()
+    leaving.wait()
 
 
 def collect(pieces, part, extra):
@@ -127,7 +130,10 @@
         out_shape=pltpu.HBM((count,) + pieces[0].shape[1:], pieces[0].dtype),
         in_specs=[hbm] * len(operands),
         out_specs=hbm,
-        scratch_shapes=[pltpu.SemaphoreType.DMA((2 * len(pieces) + 1,))],
+        scratch_shapes=[
+            pltpu.VMEM((count,) + pieces[0].shape[1:], pieces[0].dtype),
+            pltpu.SemaphoreType.DMA((2 * len(pieces) + 2,)),
+        ],
         name="collect_kept" if whole else "collect_swapped",
     )(*operands)
 

time: 589 us -> 316 us (0.54)
  Pallas kernels: 310 us -> 33.1 us
    pallas_call x6, Pallas kernels: 293 us -> 16.6 us  [collect(): pl.pallas_call(functools.partial(collect_kernel, part=part, whole=whole),...]
  transfers between devices with their start and end apart: 33 -> 33, of which waited for: 14 -> 16; matrix products, arithmetic and copies ran while one was open for 6% -> 11% of each run, Pallas kernels for 50% -> 5%
where the time goes in v6:
time: 316 us; the launch traced here: 310 us
  starting transfers between devices  160 us (51%)
  blocking collectives  42.7 us (14%)
  Pallas kernels  33.1 us (10%)
  waiting for transfers between devices  29.2 us (9%)
  local copies, waits for them, and re-layouts  25.9 us (8%)
  other arithmetic  9.03 us (3%)
  matrix products  7.71 us (2%)
    ppermute x24, starting transfers between devices, chip_exchange(): return lax.ppermute(blocks, 'oj', pairs)  86.4 us
    ppermute x6, starting transfers between devices, core_exchange(): lax.ppermute(blocks, 'oj', [(source, source ^ 1) for source in range(32)])  45.7 us
    all_to_all x3, starting transfers between devices, body(): lax.all_to_all(col_send, 'oi', split_axis=0, concat_axis=0, tiled=True)  28 us
    all_to_all x1, blocking collectives, body(): lax.all_to_all(col_table, 'oi', split_axis=0, concat_axis=0, tiled=True)  26.8 us
    ppermute x24, waiting for transfers between devices, chip_exchange(): return lax.ppermute(blocks, 'oj', pairs)  18.9 us
    pallas_call x6, Pallas kernels, collect(): pl.pallas_call(functools.partial(collect_kernel, part=part, whole=whole),...  16.6 us
    pallas_call x3, Pallas kernels, finish(): pl.pallas_call(last_kernel if last else middle_kernel, out_shape=(pltpu.H...  16.5 us
    unnamed x1, blocking collectives  15.9 us
  transfers between devices with their start and end apart: 33, of which 16 were waited for; matrix products, arithmetic and copies ran while one was open for 11% of the time, Pallas kernels for 5%

profile of v6, /device:TPU:1, one launch (start us, length us, event | category | flops | bytes accessed | tf_op | source)
XLA Modules:
  0.0 310.4 jit_solution(8799444893590551511)
XLA Ops:
  3.1 26.8 %all_to_all.24 = s32[16,1,3]{2,1,0:T(1,128)S(1)} all-to-all(s32[16,1,3]{2,1,0:T(1,128)S(1)} %bitcast.119), channel_id=1, replica_groups=mesh['oi'=16,'oj'=32] {'oi'}, dimensions={0} | all-to-all | bytes 384 | tf_op jit(solution)/shard_map/all_to_all | solution.py:300
  33.2 4.5 %all-to-all-start.1 = ((bf16[48,128,128]{2,1,0:T(8,128)(2,1)}), bf16[48,128,128]{2,1,0:T(8,128)(2,1)}, u32[]{:S(2)}, u32[]{:S(2)}) async-start(bf16[48,128,128]{2,1,0:T(8,128)(2,1)} %gather_fusion), calls=%async_computation.1 | async-start | bytes 3145728 | tf_op jit(solution)/shard_map/all_to_all | solution.py:315
  40.1 15.9 %all-reduce = s32[768]{0:T(1024)S(1)} all-reduce(s32[768]{0:T(1024)S(1)} %get-tuple-element.65), channel_id=2, replica_groups=mesh['oi'=16,'oj'=32] {'oj'}, use_global_device_ids=true, to_apply=%add | all-reduce | flops 768 | bytes 6144
  59.4 5.0 %collective-permute-start = (bf16[32,128,128]{2,1,0:T(8,128)(2,1)}, bf16[32,128,128]{2,1,0:T(8,128)(2,1)}, u32[]{:S(2)}, u32[]{:S(2)}) collective-permute-start(bf16[32,128,128]{2,1,0:T(8,128)(2,1)} %gather_fusion.3), channel_id=1, source_target_pairs={{0,1},{1,0},{2,3},{3,2},{4,5},{5,4},{6,7},{7,6},{8,9},{9,8},{10,11... | collective-permute-start | bytes 3145736 | tf_op jit(solution)/shard_map/ppermute | solution.py:55
  71.0 4.8 %collective-permute-start.2 = (bf16[8,128,128]{2,1,0:T(8,128)(2,1)S(1)}, bf16[8,128,128]{2,1,0:T(8,128)(2,1)S(1)}, u32[]{:S(2)}, u32[]{:S(2)}) collective-permute-start(bf16[8,128,128]{2,1,0:T(8,128)(2,1)S(1)} %get-tuple-element.54), channel_id=1, source_target_pairs={{0,12},{1,29},{2,14},{3,31},{4,8},{5,25},{6,10},{7,27},{8,20},{9,5... | collective-permute-start | bytes 786440 | tf_op jit(solution)/shard_map/ppermute | solution.py:64
  79.2 4.8 %collective-permute-start.4 = (bf16[8,128,128]{2,1,0:T(8,128)(2,1)S(1)}, bf16[8,128,128]{2,1,0:T(8,128)(2,1)S(1)}, u32[]{:S(2)}, u32[]{:S(2)}) collective-permute-start(bf16[8,128,128]{2,1,0:T(8,128)(2,1)S(1)} %get-tuple-element.56), channel_id=1, source_target_pairs={{0,4},{1,17},{2,6},{3,19},{4,0},{5,21},{6,2},{7,23},{8,12},{9,25},... | collective-permute-start | bytes 786440 | tf_op jit(solution)/shard_map/ppermute | solution.py:64
  93.5 4.6 %collective-permute-start.8 = (bf16[8,128,128]{2,1,0:T(8,128)(2,1)S(1)}, bf16[8,128,128]{2,1,0:T(8,128)(2,1)}, u32[]{:S(2)}, u32[]{:S(2)}) collective-permute-start(bf16[8,128,128]{2,1,0:T(8,128)(2,1)S(1)} %get-tuple-element.21), channel_id=1, source_target_pairs={{0,2},{1,7},{2,4},{3,1},{4,6},{5,3},{6,0},{7,5},{8,10},{9,15},{10,... | collective-permute-start | bytes 786440 | tf_op jit(solution)/shard_map/ppermute | solution.py:64
  104.6 12.1 %collective-permute-start.9 = (bf16[32,128,128]{2,1,0:T(8,128)(2,1)}, bf16[32,128,128]{2,1,0:T(8,128)(2,1)S(1)}, u32[]{:S(2)}, u32[]{:S(2)}) collective-permute-start(bf16[32,128,128]{2,1,0:T(8,128)(2,1)} %collect_swapped.3), channel_id=1, source_target_pairs={{0,1},{1,0},{2,3},{3,2},{4,5},{5,4},{6,7},{7,6},{8,9},{9,8},{10,11... | collective-permute-start | bytes 3145736 | tf_op jit(solution)/shard_map/ppermute | solution.py:55
  130.1 5.8 %finish.2 = (bf16[24,128,128]{2,1,0:T(8,128)(2,1)}, bf16[48,128,128]{2,1,0:T(8,128)(2,1)}) custom-call(s32[24]{0:T(128)} %copy-done.31, s32[48]{0:T(128)} %reshape.270.refs_1_, f32[24]{0:T(128)} %copy-done.27, f32[24]{0:T(128)} %refs_3_.5, f32[24,128]{1,0:T(8,128)} %refs_4_.5, f32[128,24]{1,0:T(8,128)} %bitcast.114, ...), custom_call_target="tpu_custom_call" | custom-call | tf_op jit(solution)/shard_map/finish/pallas_call | solution.py:266
  135.9 11.8 %all-to-all-start.2 = ((bf16[48,128,128]{2,1,0:T(8,128)(2,1)}), bf16[48,128,128]{2,1,0:T(8,128)(2,1)}, u32[]{:S(2)}, u32[]{:S(2)}) async-start(bf16[48,128,128]{2,1,0:T(8,128)(2,1)} %get-tuple-element.22), calls=%async_computation.2 | async-start | bytes 3145728 | tf_op jit(solution)/shard_map/all_to_all | solution.py:315
  155.7 4.0 %collective-permute-start.11 = (bf16[8,128,128]{2,1,0:T(8,128)(2,1)S(1)}, bf16[8,128,128]{2,1,0:T(8,128)(2,1)S(1)}, u32[]{:S(2)}, u32[]{:S(2)}) collective-permute-start(bf16[8,128,128]{2,1,0:T(8,128)(2,1)S(1)} %get-tuple-element.45), channel_id=1, source_target_pairs={{0,18},{1,23},{2,20},{3,17},{4,22},{5,19},{6,16},{7,21},{8,26},{9,... | collective-permute-start | bytes 786440 | tf_op jit(solution)/shard_map/ppermute | solution.py:64
  163.3 4.0 %collective-permute-start.13 = (bf16[8,128,128]{2,1,0:T(8,128)(2,1)S(1)}, bf16[8,128,128]{2,1,0:T(8,128)(2,1)S(1)}, u32[]{:S(2)}, u32[]{:S(2)}) collective-permute-start(bf16[8,128,128]{2,1,0:T(8,128)(2,1)S(1)} %get-tuple-element.47), channel_id=1, source_target_pairs={{0,0},{1,21},{2,2},{3,23},{4,4},{5,17},{6,6},{7,19},{8,8},{9,29},{... | collective-permute-start | bytes 786440 | tf_op jit(solution)/shard_map/ppermute | solution.py:64
  167.3 4.3 %collective-permute-start.14 = (bf16[8,128,128]{2,1,0:T(8,128)(2,1)S(1)}, bf16[8,128,128]{2,1,0:T(8,128)(2,1)S(1)}, u32[]{:S(2)}, u32[]{:S(2)}) collective-permute-start(bf16[8,128,128]{2,1,0:T(8,128)(2,1)S(1)} %get-tuple-element.48), channel_id=1, source_target_pairs={{0,4},{1,17},{2,6},{3,19},{4,0},{5,21},{6,2},{7,23},{8,12},{9,25},... | collective-permute-start | bytes 786440 | tf_op jit(solution)/shard_map/ppermute | solution.py:64
  178.4 4.4 %collective-permute-start.17 = (bf16[8,128,128]{2,1,0:T(8,128)(2,1)S(1)}, bf16[8,128,128]{2,1,0:T(8,128)(2,1)}, u32[]{:S(2)}, u32[]{:S(2)}) collective-permute-start(bf16[8,128,128]{2,1,0:T(8,128)(2,1)S(1)} %get-tuple-element.26), channel_id=1, source_target_pairs={{0,8},{1,25},{2,10},{3,27},{4,12},{5,29},{6,14},{7,31},{8,16},{9,1... | collective-permute-start | bytes 786440 | tf_op jit(solution)/shard_map/ppermute | solution.py:64
  193.6 12.3 %collective-permute-start.19 = (bf16[32,128,128]{2,1,0:T(8,128)(2,1)}, bf16[32,128,128]{2,1,0:T(8,128)(2,1)S(1)}, u32[]{:S(2)}, u32[]{:S(2)}) collective-permute-start(bf16[32,128,128]{2,1,0:T(8,128)(2,1)} %collect_swapped.4), channel_id=1, source_target_pairs={{0,1},{1,0},{2,3},{3,2},{4,5},{5,4},{6,7},{7,6},{8,9},{9,8},{10,11... | collective-permute-start | bytes 3145736 | tf_op jit(solution)/shard_map/ppermute | solution.py:55
  217.4 5.9 %finish.3 = (bf16[24,128,128]{2,1,0:T(8,128)(2,1)}, bf16[48,128,128]{2,1,0:T(8,128)(2,1)}) custom-call(s32[24]{0:T(128)} %copy-done.31, s32[48]{0:T(128)} %reshape.270.refs_1_, f32[24]{0:T(128)} %copy-done.27, f32[24]{0:T(128)} %refs_3_.5, f32[24,128]{1,0:T(8,128)} %refs_4_.5, f32[128,24]{1,0:T(8,128)} %bitcast.115, ...), custom_call_target="tpu_custom_call" | custom-call | tf_op jit(solution)/shard_map/finish/pallas_call | solution.py:266
  223.3 11.7 %all-to-all-start.3 = ((bf16[48,128,128]{2,1,0:T(8,128)(2,1)}), bf16[48,128,128]{2,1,0:T(8,128)(2,1)}, u32[]{:S(2)}, u32[]{:S(2)}) async-start(bf16[48,128,128]{2,1,0:T(8,128)(2,1)} %get-tuple-element.28), calls=%async_computation.3 | async-start | bytes 3145728 | tf_op jit(solution)/shard_map/all_to_all | solution.py:315
  243.3 4.3 %collective-permute-start.21 = (bf16[8,128,128]{2,1,0:T(8,128)(2,1)S(1)}, bf16[8,128,128]{2,1,0:T(8,128)(2,1)S(1)}, u32[]{:S(2)}, u32[]{:S(2)}) collective-permute-start(bf16[8,128,128]{2,1,0:T(8,128)(2,1)S(1)} %get-tuple-element.37), channel_id=1, source_target_pairs={{0,18},{1,23},{2,20},{3,17},{4,22},{5,19},{6,16},{7,21},{8,26},{9,... | collective-permute-start | bytes 786440 | tf_op jit(solution)/shard_map/ppermute | solution.py:64
  250.4 4.4 %collective-permute-start.23 = (bf16[8,128,128]{2,1,0:T(8,128)(2,1)S(1)}, bf16[8,128,128]{2,1,0:T(8,128)(2,1)S(1)}, u32[]{:S(2)}, u32[]{:S(2)}) collective-permute-start(bf16[8,128,128]{2,1,0:T(8,128)(2,1)S(1)} %get-tuple-element.39), channel_id=1, source_target_pairs={{0,0},{1,21},{2,2},{3,23},{4,4},{5,17},{6,6},{7,19},{8,8},{9,29},{... | collective-permute-start | bytes 786440 | tf_op jit(solution)/shard_map/ppermute | solution.py:64
  258.8 4.6 %collective-permute-start.25 = (bf16[8,128,128]{2,1,0:T(8,128)(2,1)S(1)}, bf16[8,128,128]{2,1,0:T(8,128)(2,1)}, u32[]{:S(2)}, u32[]{:S(2)}) collective-permute-start(bf16[8,128,128]{2,1,0:T(8,128)(2,1)S(1)} %get-tuple-element.30), channel_id=1, source_target_pairs={{0,10},{1,31},{2,12},{3,25},{4,14},{5,27},{6,8},{7,29},{8,18},{9,7... | collective-permute-start | bytes 786440 | tf_op jit(solution)/shard_map/ppermute | solution.py:64
  265.6 5.3 %collective-permute-start.27 = (bf16[8,128,128]{2,1,0:T(8,128)(2,1)S(1)}, bf16[8,128,128]{2,1,0:T(8,128)(2,1)}, u32[]{:S(2)}, u32[]{:S(2)}) collective-permute-start(bf16[8,128,128]{2,1,0:T(8,128)(2,1)S(1)} %get-tuple-element.32), channel_id=1, source_target_pairs={{0,8},{1,25},{2,10},{3,27},{4,12},{5,29},{6,14},{7,31},{8,16},{9,1... | collective-permute-start | bytes 786440 | tf_op jit(solution)/shard_map/ppermute | solution.py:64
  275.8 4.2 %collective-permute-done.28.refs_7_ = bf16[8,128,128]{2,1,0:T(8,128)(2,1)} collective-permute-done((bf16[8,128,128]{2,1,0:T(8,128)(2,1)S(1)}, bf16[8,128,128]{2,1,0:T(8,128)(2,1)}, u32[]{:S(2)}, u32[]{:S(2)}) %collective-permute-start.28) | collective-permute-done | bytes 262176 | tf_op jit(solution)/shard_map/ppermute | solution.py:64
  282.4 11.5 %collective-permute-start.29 = (bf16[32,128,128]{2,1,0:T(8,128)(2,1)}, bf16[32,128,128]{2,1,0:T(8,128)(2,1)S(1)}, u32[]{:S(2)}, u32[]{:S(2)}) collective-permute-start(bf16[32,128,128]{2,1,0:T(8,128)(2,1)} %collect_swapped.5), channel_id=1, source_target_pairs={{0,1},{1,0},{2,3},{3,2},{4,5},{5,4},{6,7},{7,6},{8,9},{9,8},{10,11... | collective-permute-start | bytes 3145736 | tf_op jit(solution)/shard_map/ppermute | solution.py:55
  305.4 4.9 %finish_last.1 = (bf16[24,128,128]{2,1,0:T(8,128)(2,1)}, bf16[24,128,128]{2,1,0:T(8,128)(2,1)}) custom-call(s32[24]{0:T(128)} %copy-done.31, s32[48]{0:T(128)} %reshape.270.refs_1_, f32[24]{0:T(128)} %copy-done.27, f32[24]{0:T(128)} %refs_3_.5, f32[24,128]{1,0:T(8,128)} %refs_4_.5, f32[128,24]{1,0:T(8,128)} %bitcast.116, ...), custom_call_target="tpu_custom_call" | custom-call | tf_op jit(solution)/shard_map/finish_last/pallas_call | solution.py:266
  (194 shorter events, 126.0 us)
Async XLA Ops:
  33.2 96.9 %all-to-all-start.1 = ((bf16[48,128,128]{2,1,0:T(8,128)(2,1)}), bf16[48,128,128]{2,1,0:T(8,128)(2,1)}, u32[]{:S(2)}, u32[]{:S(2)}) async-start(bf16[48,128,128]{2,1,0:T(8,128)(2,1)} %gather_fusion), calls=%async_computation.1 | async-start | bytes 3145728 | tf_op jit(solution)/shard_map/all_to_all | solution.py:315
  68.5 15.5 %collective-permute-start.1 = (bf16[8,128,128]{2,1,0:T(8,128)(2,1)S(1)}, bf16[8,128,128]{2,1,0:T(8,128)(2,1)S(1)}, u32[]{:S(2)}, u32[]{:S(2)}) collective-permute-start(bf16[8,128,128]{2,1,0:T(8,128)(2,1)S(1)} %get-tuple-element.53), channel_id=1, source_target_pairs={{0,18},{1,23},{2,20},{3,17},{4,22},{5,19},{6,16},{7,21},{8,26},{9,... | collective-permute-start | bytes 786440 | tf_op jit(solution)/shard_map/ppermute | solution.py:64
  71.0 16.0 %collective-permute-start.2 = (bf16[8,128,128]{2,1,0:T(8,128)(2,1)S(1)}, bf16[8,128,128]{2,1,0:T(8,128)(2,1)S(1)}, u32[]{:S(2)}, u32[]{:S(2)}) collective-permute-start(bf16[8,128,128]{2,1,0:T(8,128)(2,1)S(1)} %get-tuple-element.54), channel_id=1, source_target_pairs={{0,12},{1,29},{2,14},{3,31},{4,8},{5,25},{6,10},{7,27},{8,20},{9,5... | collective-permute-start | bytes 786440 | tf_op jit(solution)/shard_map/ppermute | solution.py:64
  75.8 14.7 %collective-permute-start.3 = (bf16[8,128,128]{2,1,0:T(8,128)(2,1)S(1)}, bf16[8,128,128]{2,1,0:T(8,128)(2,1)S(1)}, u32[]{:S(2)}, u32[]{:S(2)}) collective-permute-start(bf16[8,128,128]{2,1,0:T(8,128)(2,1)S(1)} %get-tuple-element.55), channel_id=1, source_target_pairs={{0,0},{1,21},{2,2},{3,23},{4,4},{5,17},{6,6},{7,19},{8,8},{9,29},{... | collective-permute-start | bytes 786440 | tf_op jit(solution)/shard_map/ppermute | solution.py:64
  79.2 14.2 %collective-permute-start.4 = (bf16[8,128,128]{2,1,0:T(8,128)(2,1)S(1)}, bf16[8,128,128]{2,1,0:T(8,128)(2,1)S(1)}, u32[]{:S(2)}, u32[]{:S(2)}) collective-permute-start(bf16[8,128,128]{2,1,0:T(8,128)(2,1)S(1)} %get-tuple-element.56), channel_id=1, source_target_pairs={{0,4},{1,17},{2,6},{3,19},{4,0},{5,21},{6,2},{7,23},{8,12},{9,25},... | collective-permute-start | bytes 786440 | tf_op jit(solution)/shard_map/ppermute | solution.py:64
  84.0 14.0 %collective-permute-start.5 = (bf16[8,128,128]{2,1,0:T(8,128)(2,1)S(1)}, bf16[8,128,128]{2,1,0:T(8,128)(2,1)S(1)}, u32[]{:S(2)}, u32[]{:S(2)}) collective-permute-start(bf16[8,128,128]{2,1,0:T(8,128)(2,1)S(1)} %get-tuple-element.18), channel_id=1, source_target_pairs={{0,10},{1,31},{2,12},{3,25},{4,14},{5,27},{6,8},{7,29},{8,18},{9,7... | collective-permute-start | bytes 786440 | tf_op jit(solution)/shard_map/ppermute | solution.py:64
  87.0 11.1 %collective-permute-start.6 = (bf16[8,128,128]{2,1,0:T(8,128)(2,1)S(1)}, bf16[8,128,128]{2,1,0:T(8,128)(2,1)S(1)}, u32[]{:S(2)}, u32[]{:S(2)}) collective-permute-start(bf16[8,128,128]{2,1,0:T(8,128)(2,1)S(1)} %get-tuple-element.19), channel_id=1, source_target_pairs={{0,14},{1,27},{2,8},{3,29},{4,10},{5,31},{6,12},{7,25},{8,22},{9,3... | collective-permute-start | bytes 786440 | tf_op jit(solution)/shard_map/ppermute | solution.py:64
  104.6 16.4 %collective-permute-start.9 = (bf16[32,128,128]{2,1,0:T(8,128)(2,1)}, bf16[32,128,128]{2,1,0:T(8,128)(2,1)S(1)}, u32[]{:S(2)}, u32[]{:S(2)}) collective-permute-start(bf16[32,128,128]{2,1,0:T(8,128)(2,1)} %collect_swapped.3), channel_id=1, source_target_pairs={{0,1},{1,0},{2,3},{3,2},{4,5},{5,4},{6,7},{7,6},{8,9},{9,8},{10,11... | collective-permute-start | bytes 3145736 | tf_op jit(solution)/shard_map/ppermute | solution.py:55
  135.9 81.5 %all-to-all-start.2 = ((bf16[48,128,128]{2,1,0:T(8,128)(2,1)}), bf16[48,128,128]{2,1,0:T(8,128)(2,1)}, u32[]{:S(2)}, u32[]{:S(2)}) async-start(bf16[48,128,128]{2,1,0:T(8,128)(2,1)} %get-tuple-element.22), calls=%async_computation.2 | async-start | bytes 3145728 | tf_op jit(solution)/shard_map/all_to_all | solution.py:315
  155.7 16.0 %collective-permute-start.11 = (bf16[8,128,128]{2,1,0:T(8,128)(2,1)S(1)}, bf16[8,128,128]{2,1,0:T(8,128)(2,1)S(1)}, u32[]{:S(2)}, u32[]{:S(2)}) collective-permute-start(bf16[8,128,128]{2,1,0:T(8,128)(2,1)S(1)} %get-tuple-element.45), channel_id=1, source_target_pairs={{0,18},{1,23},{2,20},{3,17},{4,22},{5,19},{6,16},{7,21},{8,26},{9,... | collective-permute-start | bytes 786440 | tf_op jit(solution)/shard_map/ppermute | solution.py:64
  159.7 15.7 %collective-permute-start.12 = (bf16[8,128,128]{2,1,0:T(8,128)(2,1)S(1)}, bf16[8,128,128]{2,1,0:T(8,128)(2,1)S(1)}, u32[]{:S(2)}, u32[]{:S(2)}) collective-permute-start(bf16[8,128,128]{2,1,0:T(8,128)(2,1)S(1)} %get-tuple-element.46), channel_id=1, source_target_pairs={{0,12},{1,29},{2,14},{3,31},{4,8},{5,25},{6,10},{7,27},{8,20},{9,5... | collective-permute-start | bytes 786440 | tf_op jit(solution)/shard_map/ppermute | solution.py:64
  163.3 15.1 %collective-permute-start.13 = (bf16[8,128,128]{2,1,0:T(8,128)(2,1)S(1)}, bf16[8,128,128]{2,1,0:T(8,128)(2,1)S(1)}, u32[]{:S(2)}, u32[]{:S(2)}) collective-permute-start(bf16[8,128,128]{2,1,0:T(8,128)(2,1)S(1)} %get-tuple-element.47), channel_id=1, source_target_pairs={{0,0},{1,21},{2,2},{3,23},{4,4},{5,17},{6,6},{7,19},{8,8},{9,29},{... | collective-permute-start | bytes 786440 | tf_op jit(solution)/shard_map/ppermute | solution.py:64
  167.3 15.6 %collective-permute-start.14 = (bf16[8,128,128]{2,1,0:T(8,128)(2,1)S(1)}, bf16[8,128,128]{2,1,0:T(8,128)(2,1)S(1)}, u32[]{:S(2)}, u32[]{:S(2)}) collective-permute-start(bf16[8,128,128]{2,1,0:T(8,128)(2,1)S(1)} %get-tuple-element.48), channel_id=1, source_target_pairs={{0,4},{1,17},{2,6},{3,19},{4,0},{5,21},{6,2},{7,23},{8,12},{9,25},... | collective-permute-start | bytes 786440 | tf_op jit(solution)/shard_map/ppermute | solution.py:64
  171.7 13.2 %collective-permute-start.15 = (bf16[8,128,128]{2,1,0:T(8,128)(2,1)S(1)}, bf16[8,128,128]{2,1,0:T(8,128)(2,1)}, u32[]{:S(2)}, u32[]{:S(2)}) collective-permute-start(bf16[8,128,128]{2,1,0:T(8,128)(2,1)S(1)} %get-tuple-element.24), channel_id=1, source_target_pairs={{0,10},{1,31},{2,12},{3,25},{4,14},{5,27},{6,8},{7,29},{8,18},{9,7... | collective-permute-start | bytes 786440 | tf_op jit(solution)/shard_map/ppermute | solution.py:64
  175.4 9.6 %collective-permute-start.16 = (bf16[8,128,128]{2,1,0:T(8,128)(2,1)S(1)}, bf16[8,128,128]{2,1,0:T(8,128)(2,1)}, u32[]{:S(2)}, u32[]{:S(2)}) collective-permute-start(bf16[8,128,128]{2,1,0:T(8,128)(2,1)S(1)} %get-tuple-element.25), channel_id=1, source_target_pairs={{0,14},{1,27},{2,8},{3,29},{4,10},{5,31},{6,12},{7,25},{8,22},{9,3... | collective-permute-start | bytes 786440 | tf_op jit(solution)/shard_map/ppermute | solution.py:64
  193.6 14.6 %collective-permute-start.19 = (bf16[32,128,128]{2,1,0:T(8,128)(2,1)}, bf16[32,128,128]{2,1,0:T(8,128)(2,1)S(1)}, u32[]{:S(2)}, u32[]{:S(2)}) collective-permute-start(bf16[32,128,128]{2,1,0:T(8,128)(2,1)} %collect_swapped.4), channel_id=1, source_target_pairs={{0,1},{1,0},{2,3},{3,2},{4,5},{5,4},{6,7},{7,6},{8,9},{9,8},{10,11... | collective-permute-start | bytes 3145736 | tf_op jit(solution)/shard_map/ppermute | solution.py:55
  223.3 82.1 %all-to-all-start.3 = ((bf16[48,128,128]{2,1,0:T(8,128)(2,1)}), bf16[48,128,128]{2,1,0:T(8,128)(2,1)}, u32[]{:S(2)}, u32[]{:S(2)}) async-start(bf16[48,128,128]{2,1,0:T(8,128)(2,1)} %get-tuple-element.28), calls=%async_computation.3 | async-start | bytes 3145728 | tf_op jit(solution)/shard_map/all_to_all | solution.py:315
  243.3 15.4 %collective-permute-start.21 = (bf16[8,128,128]{2,1,0:T(8,128)(2,1)S(1)}, bf16[8,128,128]{2,1,0:T(8,128)(2,1)S(1)}, u32[]{:S(2)}, u32[]{:S(2)}) collective-permute-start(bf16[8,128,128]{2,1,0:T(8,128)(2,1)S(1)} %get-tuple-element.37), channel_id=1, source_target_pairs={{0,18},{1,23},{2,20},{3,17},{4,22},{5,19},{6,16},{7,21},{8,26},{9,... | collective-permute-start | bytes 786440 | tf_op jit(solution)/shard_map/ppermute | solution.py:64
  247.6 15.7 %collective-permute-start.22 = (bf16[8,128,128]{2,1,0:T(8,128)(2,1)S(1)}, bf16[8,128,128]{2,1,0:T(8,128)(2,1)S(1)}, u32[]{:S(2)}, u32[]{:S(2)}) collective-permute-start(bf16[8,128,128]{2,1,0:T(8,128)(2,1)S(1)} %get-tuple-element.38), channel_id=1, source_target_pairs={{0,12},{1,29},{2,14},{3,31},{4,8},{5,25},{6,10},{7,27},{8,20},{9,5... | collective-permute-start | bytes 786440 | tf_op jit(solution)/shard_map/ppermute | solution.py:64
  250.4 15.2 %collective-permute-start.23 = (bf16[8,128,128]{2,1,0:T(8,128)(2,1)S(1)}, bf16[8,128,128]{2,1,0:T(8,128)(2,1)S(1)}, u32[]{:S(2)}, u32[]{:S(2)}) collective-permute-start(bf16[8,128,128]{2,1,0:T(8,128)(2,1)S(1)} %get-tuple-element.39), channel_id=1, source_target_pairs={{0,0},{1,21},{2,2},{3,23},{4,4},{5,17},{6,6},{7,19},{8,8},{9,29},{... | collective-permute-start | bytes 786440 | tf_op jit(solution)/shard_map/ppermute | solution.py:64
  254.8 16.1 %collective-permute-start.24 = (bf16[8,128,128]{2,1,0:T(8,128)(2,1)S(1)}, bf16[8,128,128]{2,1,0:T(8,128)(2,1)S(1)}, u32[]{:S(2)}, u32[]{:S(2)}) collective-permute-start(bf16[8,128,128]{2,1,0:T(8,128)(2,1)S(1)} %get-tuple-element.40), channel_id=1, source_target_pairs={{0,4},{1,17},{2,6},{3,19},{4,0},{5,21},{6,2},{7,23},{8,12},{9,25},... | collective-permute-start | bytes 786440 | tf_op jit(solution)/shard_map/ppermute | solution.py:64
  258.8 14.1 %collective-permute-start.25 = (bf16[8,128,128]{2,1,0:T(8,128)(2,1)S(1)}, bf16[8,128,128]{2,1,0:T(8,128)(2,1)}, u32[]{:S(2)}, u32[]{:S(2)}) collective-permute-start(bf16[8,128,128]{2,1,0:T(8,128)(2,1)S(1)} %get-tuple-element.30), channel_id=1, source_target_pairs={{0,10},{1,31},{2,12},{3,25},{4,14},{5,27},{6,8},{7,29},{8,18},{9,7... | collective-permute-start | bytes 786440 | tf_op jit(solution)/shard_map/ppermute | solution.py:64
  265.6 10.2 %collective-permute-start.27 = (bf16[8,128,128]{2,1,0:T(8,128)(2,1)S(1)}, bf16[8,128,128]{2,1,0:T(8,128)(2,1)}, u32[]{:S(2)}, u32[]{:S(2)}) collective-permute-start(bf16[8,128,128]{2,1,0:T(8,128)(2,1)S(1)} %get-tuple-element.32), channel_id=1, source_target_pairs={{0,8},{1,25},{2,10},{3,27},{4,12},{5,29},{6,14},{7,31},{8,16},{9,1... | collective-permute-start | bytes 786440 | tf_op jit(solution)/shard_map/ppermute | solution.py:64
  282.4 14.0 %collective-permute-start.29 = (bf16[32,128,128]{2,1,0:T(8,128)(2,1)}, bf16[32,128,128]{2,1,0:T(8,128)(2,1)S(1)}, u32[]{:S(2)}, u32[]{:S(2)}) collective-permute-start(bf16[32,128,128]{2,1,0:T(8,128)(2,1)} %collect_swapped.5), channel_id=1, source_target_pairs={{0,1},{1,0},{2,3},{3,2},{4,5},{5,4},{6,7},{7,6},{8,9},{9,8},{10,11... | collective-permute-start | bytes 3145736 | tf_op jit(solution)/shard_map/ppermute | solution.py:55
  (47 other events, 604.5 us)
